TPU v7x, 256 devices: a whole 4x4x8 slice. The times are simulated.
256 devices in a mesh: lev: 16 (over y, z_lo, core), lat: 16 (over x, z_hi).
Axes of the slice: x: 4, y: 4, z: 8 (z_hi: 4, z_lo: 2; z = z_hi * 2 + z_lo), core: 2. Of those that a mesh axis runs over, the one named last changes fastest.
Arguments:
- fields: bfloat16 [128, 768, 3072], P('lat', None, 'lev'), may hold values from -6 to 6
- level_group: int32 [128], replicated, may hold values from 0 to 2
- lat_start: int32 [128], replicated, may hold values from 0 to 115, as said below
- w_embed: bfloat16 [3072, 768], P('lev'), may hold values from -0.1875 to 0.1875
- group_bias: float32 [3, 768], replicated, may hold values from -4 to 4
- group_gain: float32 [3, 768], replicated, may hold values from 0.5 to 2
- norm_gain: float32 [768], replicated, may hold values from 0.1 to 1.9
- w_qkv: bfloat16 [768, 2304], replicated, may hold values from -3 to 3
- w_out: bfloat16 [768, 768], replicated, may hold values from -0.21875 to 0.21875
Outputs:
- encoded: bfloat16 [128, 768, 768], P('lat', 'lev')
Inputs may be any that keep to these rules, and one draw needn't show every extreme that they name: lat_start[i] lies from i - 8 to i - 4, moved into 0 to 115 at the ends of the grid.
All inputs are finite; a program needn't handle non-finite values.
Results may differ from a plain program's by a relative error of at most 0.0025.
The roundings to bfloat16 on the way count: a program that leaves them out, or rounds other values in their place, can miss the bound.
Values may be sent and summed in bfloat16 or wider, within the bound.
No kernel may reach another device: no remote copies, remote signals or barrier semaphores. Data moves between devices by JAX's collectives and lax.ppermute only.
A program may use at most 256 MiB of HBM per device.

v0:
```python
import functools

import jax
import jax.numpy as jnp
from jax import lax
from jax.experimental import pallas as pl
from jax.experimental.pallas import tpu as pltpu
from jax.sharding import PartitionSpec as P

DH = 64
IN_LEV = 24
WIN = 13
LAT_REACH = 8
STRIP = 8
QCOLS = 16
KCOLS = QCOLS + 2 * STRIP
CHUNK = 4
SOURCES = 4
MASKED = -1e30


def params(mib):
    return pltpu.CompilerParams(vmem_limit_bytes=mib << 20)


def cost(flops, nbytes, trans=0):
    return pl.CostEstimate(flops=int(flops), bytes_accessed=int(nbytes), transcendentals=int(trans))


def smem():
    return pl.BlockSpec(memory_space=pltpu.SMEM)


def vmem():
    return pl.BlockSpec(memory_space=pltpu.VMEM)


def pack_kernel(x_ref, o_ref):
    rows, width, lon_all = x_ref.shape
    lev = o_ref.shape[0]
    cols = lon_all // lev
    tokens = rows * cols

    def put(block, first):
        turned = block.T.reshape(lev, cols, 128)
        o_ref[:, first:first + cols, :] = turned

    for r in range(rows):
        put(x_ref[r, :128, :], r * cols)
    for r in range(rows // 2):
        both = jnp.concatenate([x_ref[r, 128:, :], x_ref[r + rows // 2, 128:, :]], axis=0)
        put(both, tokens + r * cols)


def pack(turned, lev):
    rows, width, lon_all = turned.shape
    tokens = rows * lon_all // lev
    return pl.pallas_call(
        pack_kernel,
        out_shape=jax.ShapeDtypeStruct((lev, tokens + tokens // 2, 128), turned.dtype),
        compiler_params=params(60),
        cost_estimate=cost(0, 2 * turned.size * 2),
        name="pack",
    )(turned)


def embed_kernel(x_ref, w_hbm, pick_ref, bias_ref, gain_ref, norm_ref, emb_ref, normed_ref, xs_ref, sum_ref, w_ref, sem):
    groups, width = bias_ref.shape
    lev = x_ref.shape[0]
    parts, depth, part = w_ref.shape
    per = depth // lev
    tokens = xs_ref.shape[0] // groups
    span = SOURCES * per
    loads = [pltpu.make_async_copy(w_hbm.at[:, j * part:(j + 1) * part], w_ref.at[j], sem.at[j]) for j in range(parts)]
    for load in loads:
        load.start()

    for c in range(lev // SOURCES):
        here = range(c * SOURCES, (c + 1) * SOURCES)
        main = [x_ref[s, :tokens, :] for s in here]
        low = jnp.concatenate([x_ref[s, tokens:, :64] for s in here], axis=1)
        high = jnp.concatenate([x_ref[s, tokens:, 64:] for s in here], axis=1)
        x = jnp.concatenate(main + [jnp.concatenate([low, high], axis=0)], axis=1)
        for g in range(groups):
            xs_ref[g * tokens:(g + 1) * tokens, c * span:(c + 1) * span] = x * pick_ref[g:g + 1, c * span:(c + 1) * span]

    for j in range(parts):
        loads[j].wait()
        cols = slice(j * part, (j + 1) * part)
        acc = None
        for c in range(lev // SOURCES):
            here = range(c * SOURCES, (c + 1) * SOURCES)
            w = jnp.concatenate(
                [w_ref[j, s * per:s * per + 128, :] for s in here] + [w_ref[j, s * per + 128:(s + 1) * per, :] for s in here],
                axis=0,
            )
            term = jnp.dot(xs_ref[:, c * span:(c + 1) * span], w, preferred_element_type=jnp.float32)
            acc = term if acc is None else acc + term
        total = jnp.zeros((tokens, part), jnp.float32)
        for g in range(groups):
            v = acc[g * tokens:(g + 1) * tokens] + bias_ref[g:g + 1, cols]
            total += v / (1.0 + jnp.exp(-v)) * gain_ref[g:g + 1, cols]
        sum_ref[:, cols] = total

    emb = sum_ref[...].astype(jnp.bfloat16)
    wide = emb.astype(jnp.float32)
    inv = lax.rsqrt(jnp.mean(wide * wide, axis=-1, keepdims=True) + 1e-05)
    emb_ref[...] = emb.reshape(emb_ref.shape)
    normed_ref[...] = (wide * inv * norm_ref[...]).astype(jnp.bfloat16).reshape(normed_ref.shape)


def embed(moved, w_all, pick, bias, gain, norm_gain):
    tokens = moved.shape[1] * 2 // 3
    depth, width = w_all.shape
    groups = bias.shape[0]
    cols = tokens // CHUNK
    part = 256
    return pl.pallas_call(
        embed_kernel,
        in_specs=[vmem(), pl.BlockSpec(memory_space=pltpu.HBM)] + [vmem()] * 4,
        out_specs=[vmem()] * 2,
        out_shape=[jax.ShapeDtypeStruct((CHUNK, cols, width), jnp.bfloat16)] * 2,
        scratch_shapes=[
            pltpu.VMEM((groups * tokens, depth), jnp.bfloat16),
            pltpu.VMEM((tokens, width), jnp.float32),
            pltpu.VMEM((width // part, depth, part), jnp.bfloat16),
            pltpu.SemaphoreType.DMA((width // part,)),
        ],
        compiler_params=params(60),
        cost_estimate=cost(2 * tokens * depth * width * groups, depth * width * 2 + tokens * depth * 2),
        name="embed",
    )(moved, w_all, pick, bias, gain, norm_gain[None, :])


def picks(level_group, lev, groups):
    row_groups = jnp.repeat(level_group, IN_LEV).reshape(lev // SOURCES, SOURCES, -1)
    steps = row_groups.shape[0]
    order = jnp.concatenate(
        [row_groups[:, :, :128].reshape(steps, -1), row_groups[:, :, 128:].reshape(steps, -1)], axis=1
    ).reshape(-1)
    return (order[None, :] == jnp.arange(groups, dtype=jnp.int32)[:, None]).astype(jnp.bfloat16)


def keys_values(x, w):
    n = x.shape[0] * x.shape[1]
    out = jnp.dot(x.reshape(n, x.shape[2]), w, preferred_element_type=jnp.float32).astype(jnp.bfloat16)
    return out.reshape(x.shape[0], x.shape[1], w.shape[1])


def queries_of(x, w):
    rows, cols, width = x.shape
    q = jnp.dot(x.reshape(rows * cols, width), w, preferred_element_type=jnp.float32).astype(jnp.bfloat16)
    return (q * jnp.bfloat16(DH ** (-0.5))).reshape(rows, cols, width)


def project_kernel(own0_ref, own1_ref, low_ref, high_ref, w_ref, q_ref, own_kv_ref, low_kv_ref, high_kv_ref):
    rows, cols, width = low_ref.shape
    for c, ref in enumerate((own0_ref, own1_ref)):
        q = queries_of(ref[...], w_ref[:, :width])
        for b in range(cols // QCOLS):
            q_ref[b, c * rows * QCOLS:(c + 1) * rows * QCOLS, :] = q[:, b * QCOLS:(b + 1) * QCOLS, :].reshape(rows * QCOLS, width)
        own_kv_ref[c * rows:(c + 1) * rows] = keys_values(ref[...], w_ref[:, width:])
    low_kv_ref[...] = keys_values(low_ref[...], w_ref[:, width:])
    high_kv_ref[...] = keys_values(high_ref[...], w_ref[:, width:])


def project(own0, own1, low, high, w_qkv):
    rows, cols, width = low.shape
    kv = lambda n: jax.ShapeDtypeStruct((n, cols, 2 * width), jnp.bfloat16)
    return pl.pallas_call(
        project_kernel,
        out_shape=[jax.ShapeDtypeStruct((cols // QCOLS, 2 * rows * QCOLS, width), jnp.bfloat16), kv(2 * rows), kv(rows), kv(rows)],
        compiler_params=params(60),
        cost_estimate=cost(2 * low.size * 10 * width, w_qkv.size * 2 + low.size * 24),
        name="project",
    )(own0, own1, low, high, w_qkv)


def attend_kernel(start_ref, first_ref, q_ref, own_ref, low0_ref, high0_ref, low1_ref, high1_ref, left0_ref, right0_ref,
                  left1_ref, right1_ref, w_ref, wout_ref, emb0_ref, emb1_ref, out_ref, kv_ref, att_ref):
    rows, cols, width = out_ref.shape
    half = rows // 2
    blocks, queries, _ = q_ref.shape
    keys = 3 * rows * KCOLS
    wkv = w_ref[:, width:]
    inner = slice(STRIP, STRIP + cols)
    kv_ref[rows:2 * rows, inner, :] = own_ref[...]
    kv_ref[:half, inner, :] = low0_ref[...]
    kv_ref[2 * rows:2 * rows + half, inner, :] = high0_ref[...]
    kv_ref[half:rows, inner, :] = keys_values(low1_ref[...], wkv)
    kv_ref[2 * rows + half:, inner, :] = keys_values(high1_ref[...], wkv)
    for c, (left, right) in enumerate(((left0_ref, right0_ref), (left1_ref, right1_ref))):
        for side, at in ((left, slice(0, STRIP)), (right, slice(STRIP + cols, None))):
            strip = keys_values(side[...], wkv)
            for t in range(3):
                kv_ref[t * rows + c * half:t * rows + (c + 1) * half, at, :] = strip[t * half:(t + 1) * half]

    key = lax.broadcasted_iota(jnp.int32, (QCOLS, keys), 1)
    key_row = key // KCOLS
    shift = key % KCOLS - lax.broadcasted_iota(jnp.int32, (QCOLS, keys), 0)
    near = STRIP - WIN // 2
    col_ok = (shift >= near) & (shift < near + WIN)
    first_row = first_ref[0]
    bias = []
    for r in range(rows):
        start = start_ref[first_row + r] - first_row + LAT_REACH
        ok = col_ok & (key_row >= start) & (key_row < start + WIN)
        bias.append(jnp.where(ok, 0.0, MASKED))
    bias = jnp.concatenate(bias + bias, axis=0)

    lane = lax.broadcasted_iota(jnp.int32, (queries, 128), 1)
    is_first = lane < DH
    ones = jnp.ones((keys, 128), jnp.bfloat16)
    for p in range(width // 128):
        here = slice(p * 128, (p + 1) * 128)
        here_v = slice(width + p * 128, width + (p + 1) * 128)
        for b in range(blocks):
            band = slice(b * QCOLS, b * QCOLS + KCOLS)
            q = q_ref[b, :, here]
            zero = jnp.zeros_like(q)
            qq = jnp.concatenate([jnp.where(is_first, q, zero), jnp.where(is_first, zero, q)], axis=0)
            k = kv_ref[:, band, here].reshape(keys, 128)
            v = kv_ref[:, band, here_v].reshape(keys, 128)
            s = lax.dot_general(qq, k, (((1,), (1,)), ((), ())), preferred_element_type=jnp.float32) + bias
            e = jnp.exp(s - jnp.max(s, axis=-1, keepdims=True)).astype(jnp.bfloat16)
            o = jnp.dot(e, jnp.concatenate([v, ones], axis=1), preferred_element_type=jnp.float32)
            o = o[:, :128] / o[:, 128:]
            att_ref[b, :, here] = jnp.where(is_first, o[:queries], o[queries:]).astype(jnp.bfloat16)
    for b in range(blocks):
        mixed = jnp.dot(att_ref[b], wout_ref[...], preferred_element_type=jnp.float32)
        mixed = mixed.reshape(rows, QCOLS, width)
        here = slice(b * QCOLS, (b + 1) * QCOLS)
        for c, ref in enumerate((emb0_ref, emb1_ref)):
            wide = ref[:, here, :].astype(jnp.float32)
            out_ref[c * half:(c + 1) * half, here, :] = (wide + mixed[c * half:(c + 1) * half]).astype(jnp.bfloat16)


def attend(lat_start, first_row, q, own, low0, high0, low1, high1, sides, w_qkv, w_out, emb0, emb1):
    rows, cols, _ = own.shape
    width = w_out.shape[0]
    flops = 2 * 18 * rows * cols * width * width
    return pl.pallas_call(
        attend_kernel,
        in_specs=[smem(), smem()] + [vmem()] * 14,
        out_specs=vmem(),
        out_shape=jax.ShapeDtypeStruct((rows, cols, width), jnp.bfloat16),
        scratch_shapes=[
            pltpu.VMEM((3 * rows, cols + 2 * STRIP, 2 * width), jnp.bfloat16),
            pltpu.VMEM(q.shape, jnp.bfloat16),
        ],
        compiler_params=params(60),
        cost_estimate=cost(flops, 12e6, 4e6),
        name="attend",
    )(lat_start, first_row, q, own, low0, high0, low1, high1, *sides, w_qkv, w_out, emb0, emb1)


def per_device(
    fields, level_group, lat_start, w_embed, group_bias, group_gain, norm_gain, w_qkv, w_out
):
    rows = fields.shape[0]
    lev = lax.axis_size("lev")
    lat = lax.axis_size("lat")
    w_all = lax.all_gather(w_embed, "lev", axis=0, tiled=True)
    turned = jnp.transpose(fields, (0, 2, 1))
    pick = picks(level_group, lev, group_bias.shape[0])
    first_row = (lax.axis_index("lat") * rows).astype(jnp.int32).reshape(1)
    up = [(i, i + 1) for i in range(lat - 1)]
    down = [(b, a) for a, b in up]
    right_way = [(i, (i + 1) % lev) for i in range(lev)]
    left_way = [(b, a) for a, b in right_way]

    emb, normed, low, high, sides = [], [], [], [], []
    for c in range(rows // CHUNK):
        packed = pack(turned[c * CHUNK:(c + 1) * CHUNK], lev)
        moved = lax.all_to_all(packed, "lev", split_axis=0, concat_axis=0, tiled=True)
        e, n = embed(moved, w_all, pick, group_bias, group_gain, norm_gain)
        emb.append(e)
        normed.append(n)
        low.append(lax.ppermute(n, "lat", up))
        high.append(lax.ppermute(n, "lat", down))
    q, own_kv, low_kv, high_kv = project(normed[0], normed[1], low[0], high[0], w_qkv)
    low[1], high[1], q = lax.optimization_barrier((low[1], high[1], q))
    for c in range(rows // CHUNK):
        tall = [low[c], normed[c], high[c]]
        sides.append(lax.ppermute(jnp.concatenate([t[:, -STRIP:] for t in tall], axis=0), "lev", right_way))
        sides.append(lax.ppermute(jnp.concatenate([t[:, :STRIP] for t in tall], axis=0), "lev", left_way))
    return attend(lat_start, first_row, q, own_kv, low_kv, high_kv, low[1], high[1], sides, w_qkv, w_out, emb[0], emb[1])


def solution(mesh):
    return jax.shard_map(
        per_device,
        mesh=mesh,
        in_specs=(P("lat", None, "lev"), P(), P(), P("lev", None), P(), P(), P(), P(), P()),
        out_specs=P("lat", "lev", None),
        check_vma=False,
    )
```

profile of v0, /device:TPU:2, one launch (start us, length us, event | category | flops | bytes accessed | tf_op | source)
XLA Modules:
  0.0 155.2 jit_solution(14944673724312907480)
XLA Ops:
  6.5 0.7 all-gather.2.cloned.1.call-update
  7.3 3.2 %fusion.1 = (bf16[4,192,768]{2,1,0:T(8,128)(2,1)}, bf16[4,192,768]{2,1,0:T(8,128)(2,1)}) fusion(bf16[8,192,768]{2,1,0:T(8,128)(2,1)} %bitcast.9), kind=kLoop, calls=%fused_computation.9 | loop fusion | bytes 4718592 | tf_op jit(solution)/shard_map/slice | solution.py:274
  10.5 2.7 %pack.3 = bf16[16,288,128]{2,1,0:T(8,128)(2,1)} custom-call(bf16[4,192,768]{2,1,0:T(8,128)(2,1)} %get-tuple-element.27.x_ref), custom_call_target="tpu_custom_call" | custom-call | bytes 2359296 | tf_op jit(solution)/shard_map/pack/pallas_call | solution.py:58
  13.2 5.9 %all-to-all-start.1 = ((bf16[16,288,128]{2,1,0:T(8,128)(2,1)}), bf16[16,288,128]{2,1,0:T(8,128)(2,1)S(1)}, u32[]{:S(2)}, u32[]{:S(2)}) async-start(bf16[16,288,128]{2,1,0:T(8,128)(2,1)} %pack.3), calls=%async_computation.1 | async-start | bytes 2359296 | tf_op jit(solution)/shard_map/all_to_all | solution.py:275
  19.2 2.7 %pack.2 = bf16[16,288,128]{2,1,0:T(8,128)(2,1)} custom-call(bf16[4,192,768]{2,1,0:T(8,128)(2,1)} %get-tuple-element.28.x_ref), custom_call_target="tpu_custom_call" | custom-call | bytes 2359296 | tf_op jit(solution)/shard_map/pack/pallas_call | solution.py:58
  21.8 24.1 %all-to-all-done.1.x_ref = bf16[16,288,128]{2,1,0:T(8,128)(2,1)S(1)} async-done(((bf16[16,288,128]{2,1,0:T(8,128)(2,1)}), bf16[16,288,128]{2,1,0:T(8,128)(2,1)S(1)}, u32[]{:S(2)}, u32[]{:S(2)}) %all-to-all-start.1) | async-done | bytes 1179680 | tf_op jit(solution)/shard_map/all_to_all | solution.py:275
  46.0 3.7 %all-to-all-start = ((bf16[16,288,128]{2,1,0:T(8,128)(2,1)}), bf16[16,288,128]{2,1,0:T(8,128)(2,1)S(1)}, u32[]{:S(2)}, u32[]{:S(2)}) async-start(bf16[16,288,128]{2,1,0:T(8,128)(2,1)} %pack.2), calls=%async_computation | async-start | bytes 2359296 | tf_op jit(solution)/shard_map/all_to_all | solution.py:275
  50.1 0.6 broadcast_in_dim.15.norm_ref
  50.7 0.6 fusion.pick_ref
  51.3 21.8 %all-gather.2.cloned.1.call-done.w_hbm = bf16[3072,768]{1,0:T(8,128)(2,1)} async-done(((bf16[192,768]{1,0:T(8,128)(2,1)}), bf16[3072,768]{1,0:T(8,128)(2,1)}) %all-gather.2.cloned.1.call-update) | async-done | bytes 4718608 | tf_op jit(solution)/shard_map/all_gather | solution.py:263
  73.2 8.8 %embed.3 = (bf16[4,48,768]{2,1,0:T(8,128)(2,1)}, bf16[4,48,768]{2,1,0:T(8,128)(2,1)}) custom-call(bf16[16,288,128]{2,1,0:T(8,128)(2,1)} %copy-done.1, bf16[3072,768]{1,0:T(8,128)(2,1)} %all-gather.2.cloned.1.call-done.w_hbm, bf16[3,3072]{1,0:T(4,128)(2,1)} %fusion.pick_ref, f32[3,768]{1,0:T(4,128)} %bias_ref.3, f32[3,768]{1,0:T(4,128)} %gain_ref.3, ...), custom_call_target="tpu_custom_call" | custom-call | flops 2717908992 | bytes 5898240 | tf_op jit(solution)/shard_map/embed/pallas_call | solution.py:118
  82.0 4.9 %collective-permute-start.2 = (bf16[4,48,768]{2,1,0:T(8,128)(2,1)}, bf16[4,48,768]{2,1,0:T(8,128)(2,1)S(1)}, u32[]{:S(2)}, u32[]{:S(2)}) collective-permute-start(bf16[4,48,768]{2,1,0:T(8,128)(2,1)} %get-tuple-element.17.own0_ref), channel_id=1, source_target_pairs={{0,1},{1,2},{2,3},{3,4},{4,5},{5,6},{6,7},{7,8},{8,9},{9,10},{10,1... | collective-permute-start | bytes 884744 | tf_op jit(solution)/shard_map/ppermute | solution.py:279
  86.9 4.0 %collective-permute-start.3 = (bf16[4,48,768]{2,1,0:T(8,128)(2,1)}, bf16[4,48,768]{2,1,0:T(8,128)(2,1)S(1)}, u32[]{:S(2)}, u32[]{:S(2)}) collective-permute-start(bf16[4,48,768]{2,1,0:T(8,128)(2,1)} %get-tuple-element.17.own0_ref), channel_id=1, source_target_pairs={{1,0},{2,1},{3,2},{4,3},{5,4},{6,5},{7,6},{8,7},{9,8},{10,9},{11,1... | collective-permute-start | bytes 884744 | tf_op jit(solution)/shard_map/ppermute | solution.py:280
  90.9 1.0 copy-done
  91.9 8.8 %embed.2 = (bf16[4,48,768]{2,1,0:T(8,128)(2,1)}, bf16[4,48,768]{2,1,0:T(8,128)(2,1)}) custom-call(bf16[16,288,128]{2,1,0:T(8,128)(2,1)} %copy-done, bf16[3072,768]{1,0:T(8,128)(2,1)} %all-gather.2.cloned.1.call-done.w_hbm, bf16[3,3072]{1,0:T(4,128)(2,1)} %fusion.pick_ref, f32[3,768]{1,0:T(4,128)} %bias_ref.3, f32[3,768]{1,0:T(4,128)} %gain_ref.3, ...), custom_call_target="tpu_custom_call" | custom-call | flops 2717908992 | bytes 5898240 | tf_op jit(solution)/shard_map/embed/pallas_call | solution.py:118
  100.7 3.6 %collective-permute-start = (bf16[4,48,768]{2,1,0:T(8,128)(2,1)}, bf16[4,48,768]{2,1,0:T(8,128)(2,1)S(1)}, u32[]{:S(2)}, u32[]{:S(2)}) collective-permute-start(bf16[4,48,768]{2,1,0:T(8,128)(2,1)} %get-tuple-element.16.own1_ref), channel_id=1, source_target_pairs={{0,1},{1,2},{2,3},{3,4},{4,5},{5,6},{6,7},{7,8},{8,9},{9,10},{10,1... | collective-permute-start | bytes 884744 | tf_op jit(solution)/shard_map/ppermute | solution.py:279
  104.4 5.2 %collective-permute-start.1 = (bf16[4,48,768]{2,1,0:T(8,128)(2,1)}, bf16[4,48,768]{2,1,0:T(8,128)(2,1)S(1)}, u32[]{:S(2)}, u32[]{:S(2)}) collective-permute-start(bf16[4,48,768]{2,1,0:T(8,128)(2,1)} %get-tuple-element.16.own1_ref), channel_id=1, source_target_pairs={{1,0},{2,1},{3,2},{4,3},{5,4},{6,5},{7,6},{8,7},{9,8},{10,9},{11,1... | collective-permute-start | bytes 884744 | tf_op jit(solution)/shard_map/ppermute | solution.py:280
  109.6 0.9 fusion.3
  110.4 0.8 fusion.6
  111.3 0.7 copy-done.2
  112.0 0.7 copy-done.3
  112.7 5.7 %project.1 = (bf16[3,128,768]{2,1,0:T(8,128)(2,1)}, bf16[8,48,1536]{2,1,0:T(8,128)(2,1)}, bf16[4,48,1536]{2,1,0:T(8,128)(2,1)}, bf16[4,48,1536]{2,1,0:T(8,128)(2,1)}) custom-call(bf16[4,48,768]{2,1,0:T(8,128)(2,1)} %get-tuple-element.17.own0_ref, bf16[4,48,768]{2,1,0:T(8,128)(2,1)} %get-tuple-element.16.own1_ref, bf16[4,48,768]{2,1,0:T(8,128)(2,1)} %copy-done.2, ...), custom_call_target="tpu_custom_call" | custom-call | flops 2264924160 | bytes 7077888 | tf_op jit(solution)/shard_map/project/pallas_call | solution.py:170
  118.3 1.6 %collective-permute-done.low1_ref = bf16[4,48,768]{2,1,0:T(8,128)(2,1)S(1)} collective-permute-done((bf16[4,48,768]{2,1,0:T(8,128)(2,1)}, bf16[4,48,768]{2,1,0:T(8,128)(2,1)S(1)}, u32[]{:S(2)}, u32[]{:S(2)}) %collective-permute-start) | collective-permute-done | bytes 294944 | tf_op jit(solution)/shard_map/ppermute | solution.py:279
  120.0 3.0 %collective-permute-done.1.high1_ref = bf16[4,48,768]{2,1,0:T(8,128)(2,1)S(1)} collective-permute-done((bf16[4,48,768]{2,1,0:T(8,128)(2,1)}, bf16[4,48,768]{2,1,0:T(8,128)(2,1)S(1)}, u32[]{:S(2)}, u32[]{:S(2)}) %collective-permute-start.1) | collective-permute-done | bytes 294944 | tf_op jit(solution)/shard_map/ppermute | solution.py:280
  123.7 0.8 fusion.5
  124.5 0.8 fusion.7
  125.4 3.7 %collective-permute-start.5 = (bf16[12,8,768]{2,1,0:T(8,128)(2,1)S(1)}, bf16[12,8,768]{2,1,0:T(8,128)(2,1)S(1)}, u32[]{:S(2)}, u32[]{:S(2)}) collective-permute-start(bf16[12,8,768]{2,1,0:T(8,128)(2,1)S(1)} %pad_maximum_fusion.1), channel_id=1, source_target_pairs={{16,0},{32,16},{48,32},{64,48},{80,64},{96,80},{112,96},{128,112},... | collective-permute-start | bytes 442376 | tf_op jit(solution)/shard_map/ppermute | solution.py:286
  129.2 0.7 collective-permute-done.6.left1_ref
  129.9 2.4 %collective-permute-done.5.right0_ref = bf16[12,8,768]{2,1,0:T(8,128)(2,1)S(1)} collective-permute-done((bf16[12,8,768]{2,1,0:T(8,128)(2,1)S(1)}, bf16[12,8,768]{2,1,0:T(8,128)(2,1)S(1)}, u32[]{:S(2)}, u32[]{:S(2)}) %collective-permute-start.5) | collective-permute-done | bytes 147488 | tf_op jit(solution)/shard_map/ppermute | solution.py:286
  132.3 3.5 %collective-permute-done.4.left0_ref = bf16[12,8,768]{2,1,0:T(8,128)(2,1)S(1)} collective-permute-done((bf16[12,8,768]{2,1,0:T(8,128)(2,1)S(1)}, bf16[12,8,768]{2,1,0:T(8,128)(2,1)S(1)}, u32[]{:S(2)}, u32[]{:S(2)}) %collective-permute-start.4) | collective-permute-done | bytes 147488 | tf_op jit(solution)/shard_map/ppermute | solution.py:285
  135.9 0.6 copy-done.11
  136.5 11.9 %attend.1 = bf16[8,48,768]{2,1,0:T(8,128)(2,1)} custom-call(s32[128]{0:T(128)} %start_ref.1, s32[1]{0:T(128)} %bitcast.first_ref, bf16[3,128,768]{2,1,0:T(8,128)(2,1)} %get-tuple-element.19.q_ref, bf16[8,48,1536]{2,1,0:T(8,128)(2,1)} %get-tuple-element.20.own_ref, bf16[4,48,1536]{2,1,0:T(8,128)(2,1)} %get-tuple-element.21.low0_ref, ...), custom_call_target="tpu_custom_call" | custom-call | flops 8153726976 | bytes 12000000 | tf_op jit(solution)/shard_map/attend/pallas_call | solution.py:242
  (42 shorter events, 1.3 us)
Async XLA Ops:
  6.5 66.6 %all-gather.2.cloned.1.call-start = ((), (), s32[]{:S(2)}) async-start(), calls=%async_computation.2 | async-start | bytes 5013504 | tf_op jit(solution)/shard_map/all_gather | solution.py:263
  13.2 32.7 %all-to-all-start.1 = ((bf16[16,288,128]{2,1,0:T(8,128)(2,1)}), bf16[16,288,128]{2,1,0:T(8,128)(2,1)S(1)}, u32[]{:S(2)}, u32[]{:S(2)}) async-start(bf16[16,288,128]{2,1,0:T(8,128)(2,1)} %pack.3), calls=%async_computation.1 | async-start | bytes 2359296 | tf_op jit(solution)/shard_map/all_to_all | solution.py:275
  21.8 27.9 %copy-start.7 = (s32[128]{0:T(128)S(1)}, s32[128]{0:T(128)}, u32[]{:S(2)}) copy-start(s32[128]{0:T(128)} %param.10) | copy-start | bytes 1540
  21.8 28.3 %copy-start.6 = (f32[768]{0:T(1024)S(1)}, f32[768]{0:T(1024)}, u32[]{:S(2)}) copy-start(f32[768]{0:T(1024)} %param.15) | copy-start | bytes 9220
  46.0 3.8 %copy-start.1 = (bf16[16,288,128]{2,1,0:T(8,128)(2,1)}, bf16[16,288,128]{2,1,0:T(8,128)(2,1)S(1)}, u32[]{:S(2)}) copy-start(bf16[16,288,128]{2,1,0:T(8,128)(2,1)S(1)} %all-to-all-done.1.x_ref) | copy-start | bytes 3538948
  46.0 44.9 %all-to-all-start = ((bf16[16,288,128]{2,1,0:T(8,128)(2,1)}), bf16[16,288,128]{2,1,0:T(8,128)(2,1)S(1)}, u32[]{:S(2)}, u32[]{:S(2)}) async-start(bf16[16,288,128]{2,1,0:T(8,128)(2,1)} %pack.2), calls=%async_computation | async-start | bytes 2359296 | tf_op jit(solution)/shard_map/all_to_all | solution.py:275
  82.0 29.3 %collective-permute-start.2 = (bf16[4,48,768]{2,1,0:T(8,128)(2,1)}, bf16[4,48,768]{2,1,0:T(8,128)(2,1)S(1)}, u32[]{:S(2)}, u32[]{:S(2)}) collective-permute-start(bf16[4,48,768]{2,1,0:T(8,128)(2,1)} %get-tuple-element.17.own0_ref), channel_id=1, source_target_pairs={{0,1},{1,2},{2,3},{3,4},{4,5},{5,6},{6,7},{7,8},{8,9},{9,10},{10,1... | collective-permute-start | bytes 884744 | tf_op jit(solution)/shard_map/ppermute | solution.py:279
  86.9 24.4 %collective-permute-start.3 = (bf16[4,48,768]{2,1,0:T(8,128)(2,1)}, bf16[4,48,768]{2,1,0:T(8,128)(2,1)S(1)}, u32[]{:S(2)}, u32[]{:S(2)}) collective-permute-start(bf16[4,48,768]{2,1,0:T(8,128)(2,1)} %get-tuple-element.17.own0_ref), channel_id=1, source_target_pairs={{1,0},{2,1},{3,2},{4,3},{5,4},{6,5},{7,6},{8,7},{9,8},{10,9},{11,1... | collective-permute-start | bytes 884744 | tf_op jit(solution)/shard_map/ppermute | solution.py:280
  90.8 1.0 copy-start
  100.7 19.3 %collective-permute-start = (bf16[4,48,768]{2,1,0:T(8,128)(2,1)}, bf16[4,48,768]{2,1,0:T(8,128)(2,1)S(1)}, u32[]{:S(2)}, u32[]{:S(2)}) collective-permute-start(bf16[4,48,768]{2,1,0:T(8,128)(2,1)} %get-tuple-element.16.own1_ref), channel_id=1, source_target_pairs={{0,1},{1,2},{2,3},{3,4},{4,5},{5,6},{6,7},{7,8},{8,9},{9,10},{10,1... | collective-permute-start | bytes 884744 | tf_op jit(solution)/shard_map/ppermute | solution.py:279
  104.4 18.6 %collective-permute-start.1 = (bf16[4,48,768]{2,1,0:T(8,128)(2,1)}, bf16[4,48,768]{2,1,0:T(8,128)(2,1)S(1)}, u32[]{:S(2)}, u32[]{:S(2)}) collective-permute-start(bf16[4,48,768]{2,1,0:T(8,128)(2,1)} %get-tuple-element.16.own1_ref), channel_id=1, source_target_pairs={{1,0},{2,1},{3,2},{4,3},{5,4},{6,5},{7,6},{8,7},{9,8},{10,9},{11,1... | collective-permute-start | bytes 884744 | tf_op jit(solution)/shard_map/ppermute | solution.py:280
  111.3 0.7 copy-start.2
  112.0 0.7 copy-start.3
  120.0 15.9 %copy-start.4 = (bf16[4,48,768]{2,1,0:T(8,128)(2,1)}, bf16[4,48,768]{2,1,0:T(8,128)(2,1)S(1)}, u32[]{:S(2)}) copy-start(bf16[4,48,768]{2,1,0:T(8,128)(2,1)S(1)} %collective-permute-done.low1_ref) | copy-start | bytes 884740
  123.0 12.9 %copy-start.5 = (bf16[4,48,768]{2,1,0:T(8,128)(2,1)}, bf16[4,48,768]{2,1,0:T(8,128)(2,1)S(1)}, u32[]{:S(2)}) copy-start(bf16[4,48,768]{2,1,0:T(8,128)(2,1)S(1)} %collective-permute-done.1.high1_ref) | copy-start | bytes 884740
  123.0 6.2 %collective-permute-start.7 = (bf16[12,8,768]{2,1,0:T(8,128)(2,1)S(1)}, bf16[12,8,768]{2,1,0:T(8,128)(2,1)S(1)}, u32[]{:S(2)}, u32[]{:S(2)}) collective-permute-start(bf16[12,8,768]{2,1,0:T(8,128)(2,1)S(1)} %pad_maximum_fusion.3), channel_id=1, source_target_pairs={{16,0},{32,16},{48,32},{64,48},{80,64},{96,80},{112,96},{128,112},... | collective-permute-start | bytes 442376 | tf_op jit(solution)/shard_map/ppermute | solution.py:286
  123.2 6.8 %collective-permute-start.6 = (bf16[12,8,768]{2,1,0:T(8,128)(2,1)S(1)}, bf16[12,8,768]{2,1,0:T(8,128)(2,1)S(1)}, u32[]{:S(2)}, u32[]{:S(2)}) collective-permute-start(bf16[12,8,768]{2,1,0:T(8,128)(2,1)S(1)} %pad_maximum_fusion.2), channel_id=1, source_target_pairs={{0,16},{16,32},{32,48},{48,64},{64,80},{80,96},{96,112},{112,128},... | collective-permute-start | bytes 442376 | tf_op jit(solution)/shard_map/ppermute | solution.py:285
  125.4 6.9 %collective-permute-start.5 = (bf16[12,8,768]{2,1,0:T(8,128)(2,1)S(1)}, bf16[12,8,768]{2,1,0:T(8,128)(2,1)S(1)}, u32[]{:S(2)}, u32[]{:S(2)}) collective-permute-start(bf16[12,8,768]{2,1,0:T(8,128)(2,1)S(1)} %pad_maximum_fusion.1), channel_id=1, source_target_pairs={{16,0},{32,16},{48,32},{64,48},{80,64},{96,80},{112,96},{128,112},... | collective-permute-start | bytes 442376 | tf_op jit(solution)/shard_map/ppermute | solution.py:286
  129.1 6.8 %collective-permute-start.4 = (bf16[12,8,768]{2,1,0:T(8,128)(2,1)S(1)}, bf16[12,8,768]{2,1,0:T(8,128)(2,1)S(1)}, u32[]{:S(2)}, u32[]{:S(2)}) collective-permute-start(bf16[12,8,768]{2,1,0:T(8,128)(2,1)S(1)} %pad_maximum_fusion), channel_id=1, source_target_pairs={{0,16},{16,32},{32,48},{48,64},{64,80},{80,96},{96,112},{112,128},... | collective-permute-start | bytes 442376 | tf_op jit(solution)/shard_map/ppermute | solution.py:285
  129.2 6.7 %copy-start.8 = (bf16[12,8,768]{2,1,0:T(8,128)(2,1)}, bf16[12,8,768]{2,1,0:T(8,128)(2,1)S(1)}, u32[]{:S(2)}) copy-start(bf16[12,8,768]{2,1,0:T(8,128)(2,1)S(1)} %collective-permute-done.7.right1_ref) | copy-start | bytes 442372
  129.9 5.9 %copy-start.9 = (bf16[12,8,768]{2,1,0:T(8,128)(2,1)}, bf16[12,8,768]{2,1,0:T(8,128)(2,1)S(1)}, u32[]{:S(2)}) copy-start(bf16[12,8,768]{2,1,0:T(8,128)(2,1)S(1)} %collective-permute-done.6.left1_ref) | copy-start | bytes 442372
  132.3 3.6 %copy-start.10 = (bf16[12,8,768]{2,1,0:T(8,128)(2,1)}, bf16[12,8,768]{2,1,0:T(8,128)(2,1)S(1)}, u32[]{:S(2)}) copy-start(bf16[12,8,768]{2,1,0:T(8,128)(2,1)S(1)} %collective-permute-done.5.right0_ref) | copy-start | bytes 442372
  135.8 0.7 copy-start.11
Sparse Core Ops, SparseCore 0:
  9.2 63.9 all-gather.1
where the time goes:
time: 156 us; the launch traced here: 155 us
  waiting for transfers between devices  57.9 us (37%)
  Pallas kernels  40.6 us (26%)
  starting transfers between devices  31.7 us (20%)
  between operations  13.6 us (9%)
  local copies, waits for them, and re-layouts  10.6 us (7%)
    all_to_all x2, waiting for transfers between devices, per_device(): lax.all_to_all(packed, 'lev', split_axis=0, concat_axis=0, tiled=True)  24.1 us
    all_gather x1, waiting for transfers between devices, per_device(): w_all = lax.all_gather(w_embed, 'lev', axis=0, tiled=True)  21.8 us
    pallas_call x2, Pallas kernels, embed(): pl.pallas_call(embed_kernel, in_specs=[vmem(), pl.BlockSpec(memory_space=...  17.6 us
    pallas_call x1, Pallas kernels, attend(): pl.pallas_call(attend_kernel, in_specs=[smem(), smem()] + [vmem()] * 14,...  11.9 us
    all_to_all x2, starting transfers between devices, per_device(): lax.all_to_all(packed, 'lev', split_axis=0, concat_axis=0, tiled=True)  9.63 us
    ppermute x2, starting transfers between devices, per_device(): high.append(lax.ppermute(n, 'lat', down))  9.17 us
    ppermute x2, starting transfers between devices, per_device(): low.append(lax.ppermute(n, 'lat', up))  8.53 us
    pallas_call x1, Pallas kernels, project(): pl.pallas_call(project_kernel, out_shape=[jax.ShapeDtypeStruct((cols // Q...  5.66 us
  transfers between devices with their start and end apart: 11, of which 7 were waited for; matrix products, arithmetic and copies ran while one was open for 5% of the time, Pallas kernels for 18%

commit v1 on v0

--- a/solution.py
+++ b/solution.py
@@ -17,6 +17,7 @@
 CHUNK = 4
 SOURCES = 4
 MASKED = -1e30
+LIMIT = 36
 
 
 def params(mib):
@@ -52,14 +53,17 @@
         put(both, tokens + r * cols)
 
 
-def pack(turned, lev):
-    rows, width, lon_all = turned.shape
-    tokens = rows * lon_all // lev
+def pack(turned, lev, chunk):
+    _, width, lon_all = turned.shape
+    tokens = CHUNK * lon_all // lev
     return pl.pallas_call(
         pack_kernel,
+        grid=(1,),
+        in_specs=[pl.BlockSpec((CHUNK, width, lon_all), lambda i: (chunk, 0, 0))],
+        out_specs=pl.BlockSpec((lev, tokens + tokens // 2, 128), lambda i: (0, 0, 0)),
         out_shape=jax.ShapeDtypeStruct((lev, tokens + tokens // 2, 128), turned.dtype),
         compiler_params=params(60),
-        cost_estimate=cost(0, 2 * turned.size * 2),
+        cost_estimate=cost(0, 2 * turned.size),
         name="pack",
     )(turned)
 
@@ -153,48 +157,35 @@
     return (q * jnp.bfloat16(DH ** (-0.5))).reshape(rows, cols, width)
 
 
-def project_kernel(own0_ref, own1_ref, low_ref, high_ref, w_ref, q_ref, own_kv_ref, low_kv_ref, high_kv_ref):
+def project_kernel(own0_ref, own1_ref, low_ref, high_ref, w_ref, q_ref, kv_ref):
     rows, cols, width = low_ref.shape
+    inner = slice(STRIP, STRIP + cols)
     for c, ref in enumerate((own0_ref, own1_ref)):
         q = queries_of(ref[...], w_ref[:, :width])
         for b in range(cols // QCOLS):
             q_ref[b, c * rows * QCOLS:(c + 1) * rows * QCOLS, :] = q[:, b * QCOLS:(b + 1) * QCOLS, :].reshape(rows * QCOLS, width)
-        own_kv_ref[c * rows:(c + 1) * rows] = keys_values(ref[...], w_ref[:, width:])
-    low_kv_ref[...] = keys_values(low_ref[...], w_ref[:, width:])
-    high_kv_ref[...] = keys_values(high_ref[...], w_ref[:, width:])
+    for ref, at in ((own0_ref, 2), (own1_ref, 3), (low_ref, 0), (high_ref, 4)):
+        kv_ref[at * rows:(at + 1) * rows, inner, :] = keys_values(ref[...], w_ref[:, width:])
 
 
 def project(own0, own1, low, high, w_qkv):
     rows, cols, width = low.shape
-    kv = lambda n: jax.ShapeDtypeStruct((n, cols, 2 * width), jnp.bfloat16)
     return pl.pallas_call(
         project_kernel,
-        out_shape=[jax.ShapeDtypeStruct((cols // QCOLS, 2 * rows * QCOLS, width), jnp.bfloat16), kv(2 * rows), kv(rows), kv(rows)],
-        compiler_params=params(60),
+        in_specs=[vmem()] * 5,
+        out_specs=[vmem()] * 2,
+        out_shape=[
+            pltpu.VMEM((cols // QCOLS, 2 * rows * QCOLS, width), jnp.bfloat16),
+            pltpu.VMEM((6 * rows, cols + 2 * STRIP, 2 * width), jnp.bfloat16),
+        ],
+        compiler_params=params(LIMIT),
         cost_estimate=cost(2 * low.size * 10 * width, w_qkv.size * 2 + low.size * 24),
         name="project",
     )(own0, own1, low, high, w_qkv)
 
 
-def attend_kernel(start_ref, first_ref, q_ref, own_ref, low0_ref, high0_ref, low1_ref, high1_ref, left0_ref, right0_ref,
-                  left1_ref, right1_ref, w_ref, wout_ref, emb0_ref, emb1_ref, out_ref, kv_ref, att_ref):
-    rows, cols, width = out_ref.shape
-    half = rows // 2
-    blocks, queries, _ = q_ref.shape
+def window_bias(start_ref, first_ref, rows):
     keys = 3 * rows * KCOLS
-    wkv = w_ref[:, width:]
-    inner = slice(STRIP, STRIP + cols)
-    kv_ref[rows:2 * rows, inner, :] = own_ref[...]
-    kv_ref[:half, inner, :] = low0_ref[...]
-    kv_ref[2 * rows:2 * rows + half, inner, :] = high0_ref[...]
-    kv_ref[half:rows, inner, :] = keys_values(low1_ref[...], wkv)
-    kv_ref[2 * rows + half:, inner, :] = keys_values(high1_ref[...], wkv)
-    for c, (left, right) in enumerate(((left0_ref, right0_ref), (left1_ref, right1_ref))):
-        for side, at in ((left, slice(0, STRIP)), (right, slice(STRIP + cols, None))):
-            strip = keys_values(side[...], wkv)
-            for t in range(3):
-                kv_ref[t * rows + c * half:t * rows + (c + 1) * half, at, :] = strip[t * half:(t + 1) * half]
-
     key = lax.broadcasted_iota(jnp.int32, (QCOLS, keys), 1)
     key_row = key // KCOLS
     shift = key % KCOLS - lax.broadcasted_iota(jnp.int32, (QCOLS, keys), 0)
@@ -206,52 +197,111 @@
         start = start_ref[first_row + r] - first_row + LAT_REACH
         ok = col_ok & (key_row >= start) & (key_row < start + WIN)
         bias.append(jnp.where(ok, 0.0, MASKED))
-    bias = jnp.concatenate(bias + bias, axis=0)
-
+    return jnp.concatenate(bias + bias, axis=0)
+
+
+def attend_block(b, bias, q_ref, kv_ref, att_ref):
+    _, queries, width = q_ref.shape
+    keys = bias.shape[1]
     lane = lax.broadcasted_iota(jnp.int32, (queries, 128), 1)
     is_first = lane < DH
     ones = jnp.ones((keys, 128), jnp.bfloat16)
+    band = slice(b * QCOLS, b * QCOLS + KCOLS)
     for p in range(width // 128):
         here = slice(p * 128, (p + 1) * 128)
         here_v = slice(width + p * 128, width + (p + 1) * 128)
-        for b in range(blocks):
-            band = slice(b * QCOLS, b * QCOLS + KCOLS)
-            q = q_ref[b, :, here]
-            zero = jnp.zeros_like(q)
-            qq = jnp.concatenate([jnp.where(is_first, q, zero), jnp.where(is_first, zero, q)], axis=0)
-            k = kv_ref[:, band, here].reshape(keys, 128)
-            v = kv_ref[:, band, here_v].reshape(keys, 128)
-            s = lax.dot_general(qq, k, (((1,), (1,)), ((), ())), preferred_element_type=jnp.float32) + bias
-            e = jnp.exp(s - jnp.max(s, axis=-1, keepdims=True)).astype(jnp.bfloat16)
-            o = jnp.dot(e, jnp.concatenate([v, ones], axis=1), preferred_element_type=jnp.float32)
-            o = o[:, :128] / o[:, 128:]
-            att_ref[b, :, here] = jnp.where(is_first, o[:queries], o[queries:]).astype(jnp.bfloat16)
-    for b in range(blocks):
-        mixed = jnp.dot(att_ref[b], wout_ref[...], preferred_element_type=jnp.float32)
-        mixed = mixed.reshape(rows, QCOLS, width)
-        here = slice(b * QCOLS, (b + 1) * QCOLS)
-        for c, ref in enumerate((emb0_ref, emb1_ref)):
-            wide = ref[:, here, :].astype(jnp.float32)
-            out_ref[c * half:(c + 1) * half, here, :] = (wide + mixed[c * half:(c + 1) * half]).astype(jnp.bfloat16)
-
-
-def attend(lat_start, first_row, q, own, low0, high0, low1, high1, sides, w_qkv, w_out, emb0, emb1):
-    rows, cols, _ = own.shape
-    width = w_out.shape[0]
-    flops = 2 * 18 * rows * cols * width * width
-    return pl.pallas_call(
-        attend_kernel,
-        in_specs=[smem(), smem()] + [vmem()] * 14,
-        out_specs=vmem(),
-        out_shape=jax.ShapeDtypeStruct((rows, cols, width), jnp.bfloat16),
-        scratch_shapes=[
-            pltpu.VMEM((3 * rows, cols + 2 * STRIP, 2 * width), jnp.bfloat16),
-            pltpu.VMEM(q.shape, jnp.bfloat16),
-        ],
-        compiler_params=params(60),
-        cost_estimate=cost(flops, 12e6, 4e6),
-        name="attend",
-    )(lat_start, first_row, q, own, low0, high0, low1, high1, *sides, w_qkv, w_out, emb0, emb1)
+        q = q_ref[b, :, here]
+        zero = jnp.zeros_like(q)
+        qq = jnp.concatenate([jnp.where(is_first, q, zero), jnp.where(is_first, zero, q)], axis=0)
+        k = kv_ref[:, band, here].reshape(keys, 128)
+        v = kv_ref[:, band, here_v].reshape(keys, 128)
+        s = lax.dot_general(qq, k, (((1,), (1,)), ((), ())), preferred_element_type=jnp.float32) + bias
+        e = jnp.exp(s - jnp.max(s, axis=-1, keepdims=True)).astype(jnp.bfloat16)
+        o = jnp.dot(e, jnp.concatenate([v, ones], axis=1), preferred_element_type=jnp.float32)
+        o = o[:, :128] / o[:, 128:]
+        att_ref[b, :, here] = jnp.where(is_first, o[:queries], o[queries:]).astype(jnp.bfloat16)
+
+
+def finish_block(b, rows, att_ref, wout_ref, emb_refs, write):
+    mixed = jnp.dot(att_ref[b], wout_ref[...], preferred_element_type=jnp.float32)
+    mixed = mixed.reshape(rows, QCOLS, mixed.shape[1])
+    half = rows // 2
+    for c, ref in enumerate(emb_refs):
+        wide = ref[:, b * QCOLS:(b + 1) * QCOLS, :].astype(jnp.float32)
+        write(slice(c * half, (c + 1) * half), (wide + mixed[c * half:(c + 1) * half]).astype(jnp.bfloat16))
+
+
+def middle_kernel(start_ref, first_ref, q_ref, _, low_ref, high_ref, left_ref, right_ref, w_ref, wout_ref, emb0_ref, emb1_ref,
+                  kv_ref, out_ref, att_ref):
+    half, cols, width = low_ref.shape
+    rows = 2 * half
+    wkv = w_ref[:, width:]
+    inner = slice(STRIP, STRIP + cols)
+    kv_ref[half:rows, inner, :] = keys_values(low_ref[...], wkv)
+    kv_ref[2 * rows + half:, inner, :] = keys_values(high_ref[...], wkv)
+    bias = window_bias(start_ref, first_ref, rows)
+    attend_block(1, bias, q_ref, kv_ref, att_ref)
+
+    def write(at, value):
+        out_ref[at] = value
+
+    finish_block(1, rows, att_ref, wout_ref, (emb0_ref, emb1_ref), write)
+    for side, at in ((left_ref, slice(0, STRIP)), (right_ref, slice(STRIP + cols, None))):
+        strip = keys_values(side[...], wkv)
+        kv_ref[:half, at, :] = strip[:half]
+        kv_ref[rows:2 * rows, at, :] = strip[half:3 * half]
+        kv_ref[2 * rows:2 * rows + half, at, :] = strip[3 * half:]
+
+
+def middle(lat_start, first_row, q, kv, low, high, left, right, w_qkv, w_out, emb0, emb1):
+    half, cols, width = low.shape
+    return pl.pallas_call(
+        middle_kernel,
+        in_specs=[smem(), smem()] + [vmem()] * 10,
+        out_specs=[vmem()] * 2,
+        out_shape=[pltpu.VMEM(kv.shape, kv.dtype), pltpu.VMEM((2 * half, QCOLS, width), jnp.bfloat16)],
+        input_output_aliases={3: 0},
+        scratch_shapes=[pltpu.VMEM(q.shape, jnp.bfloat16)],
+        compiler_params=params(LIMIT),
+        cost_estimate=cost(8e9, 10e6, 1e6),
+        name="middle",
+    )(lat_start, first_row, q, kv, low, high, left, right, w_qkv, w_out, emb0, emb1)
+
+
+def sides_kernel(start_ref, first_ref, q_ref, _, left_ref, right_ref, w_ref, wout_ref, emb0_ref, emb1_ref, middle_ref,
+                 out_ref, kv_ref, att_ref):
+    rows, cols, width = out_ref.shape
+    half = rows // 2
+    blocks = q_ref.shape[0]
+    wkv = w_ref[:, width:]
+    for side, at in ((left_ref, slice(0, STRIP)), (right_ref, slice(STRIP + cols, None))):
+        strip = keys_values(side[...], wkv)
+        kv_ref[half:rows, at, :] = strip[:half]
+        kv_ref[2 * rows + half:, at, :] = strip[half:]
+    bias = window_bias(start_ref, first_ref, rows)
+    out_ref[:, QCOLS:2 * QCOLS, :] = middle_ref[...]
+    for b in (0, blocks - 1):
+        attend_block(b, bias, q_ref, kv_ref, att_ref)
+
+        def write(at, value):
+            out_ref[at, b * QCOLS:(b + 1) * QCOLS, :] = value
+
+        finish_block(b, rows, att_ref, wout_ref, (emb0_ref, emb1_ref), write)
+
+
+def sides(lat_start, first_row, q, kv, left, right, w_qkv, w_out, emb0, emb1, centre):
+    half, cols, width = emb0.shape
+    return pl.pallas_call(
+        sides_kernel,
+        in_specs=[smem(), smem()] + [vmem()] * 9,
+        out_specs=[vmem()] * 2,
+        out_shape=[jax.ShapeDtypeStruct((2 * half, cols, width), jnp.bfloat16), pltpu.VMEM(kv.shape, kv.dtype)],
+        input_output_aliases={3: 1},
+        scratch_shapes=[pltpu.VMEM(q.shape, jnp.bfloat16)],
+        compiler_params=params(LIMIT),
+        cost_estimate=cost(9e9, 10e6, 2e6),
+        name="sides",
+    )(lat_start, first_row, q, kv, left, right, w_qkv, w_out, emb0, emb1, centre)[0]
 
 
 def per_device(
@@ -269,22 +319,32 @@
     right_way = [(i, (i + 1) % lev) for i in range(lev)]
     left_way = [(b, a) for a, b in right_way]
 
-    emb, normed, low, high, sides = [], [], [], [], []
+    emb, normed, low, high = [], [], [], []
     for c in range(rows // CHUNK):
-        packed = pack(turned[c * CHUNK:(c + 1) * CHUNK], lev)
+        packed = pack(turned, lev, c)
+        if c > 0:
+            packed, w_all = lax.optimization_barrier((packed, w_all))
         moved = lax.all_to_all(packed, "lev", split_axis=0, concat_axis=0, tiled=True)
         e, n = embed(moved, w_all, pick, group_bias, group_gain, norm_gain)
         emb.append(e)
         normed.append(n)
         low.append(lax.ppermute(n, "lat", up))
         high.append(lax.ppermute(n, "lat", down))
-    q, own_kv, low_kv, high_kv = project(normed[0], normed[1], low[0], high[0], w_qkv)
+
+    def strips(tall):
+        left = lax.ppermute(jnp.concatenate([t[:, -STRIP:] for t in tall], axis=0), "lev", right_way)
+        right = lax.ppermute(jnp.concatenate([t[:, :STRIP] for t in tall], axis=0), "lev", left_way)
+        return left, right
+
+    low[0], high[0], normed[1] = lax.optimization_barrier((low[0], high[0], normed[1]))
+    left, right = strips([low[0], normed[0], normed[1], high[0]])
+    q, kv = project(normed[0], normed[1], low[0], high[0], w_qkv)
     low[1], high[1], q = lax.optimization_barrier((low[1], high[1], q))
-    for c in range(rows // CHUNK):
-        tall = [low[c], normed[c], high[c]]
-        sides.append(lax.ppermute(jnp.concatenate([t[:, -STRIP:] for t in tall], axis=0), "lev", right_way))
-        sides.append(lax.ppermute(jnp.concatenate([t[:, :STRIP] for t in tall], axis=0), "lev", left_way))
-    return attend(lat_start, first_row, q, own_kv, low_kv, high_kv, low[1], high[1], sides, w_qkv, w_out, emb[0], emb[1])
+    last_left, last_right = strips([low[1], high[1]])
+    kv, centre = middle(
+        lat_start, first_row, q, kv, low[1], high[1], left, right, w_qkv, w_out, emb[0], emb[1]
+    )
+    return sides(lat_start, first_row, q, kv, last_left, last_right, w_qkv, w_out, emb[0], emb[1], centre)
 
 
 def solution(mesh):

time: 156 us -> 144 us (0.923)
  waiting for transfers between devices: 57.9 us -> 49.6 us
  Pallas kernels: 40.6 us -> 35.9 us
  starting transfers between devices: 31.7 us -> 36.3 us
  local copies, waits for them, and re-layouts: 10.6 us -> 6.73 us
    all_to_all x2, waiting for transfers between devices: 24.1 us -> 0.01 us  [per_device(): lax.all_to_all(packed, 'lev', split_axis=0, concat_axis=0, tiled=True)]
    all_gather x1, waiting for transfers between devices: 21.8 us -> 39.9 us  [per_device(): w_all = lax.all_gather(w_embed, 'lev', axis=0, tiled=True)]
    ppermute x2, waiting for transfers between devices: 1.63 us -> 8.36 us  [per_device(): low.append(lax.ppermute(n, 'lat', up))]
    ppermute x4, waiting for transfers between devices: 6.64 us -> 0.01 us  [the longest x2 0.01 us: strips(): lax.ppermute(jnp.concatenate([t[:, :STRIP] for t in tall], axis=0), 'lev'...]
    ppermute x2, starting transfers between devices: 9.17 us -> 14.6 us  [per_device(): high.append(lax.ppermute(n, 'lat', down))]
    slice x6 -> x4, local copies, waits for them, and re-layouts: 6.59 us -> 1.72 us  [strips(): t[:, :STRIP]]
    pallas_call x4 -> x5, Pallas kernels: 22.9 us -> 18.2 us  [the longest x1 6.2 us: sides(): pl.pallas_call(sides_kernel, in_specs=[smem(), smem()] + [vmem()] * 9, ou...]
    ppermute x2, starting transfers between devices: 8.53 us -> 3.84 us  [per_device(): low.append(lax.ppermute(n, 'lat', up))]
  transfers between devices with their start and end apart: 11 -> 11, of which waited for: 7 -> 3; matrix products, arithmetic and copies ran while one was open for 5% -> 2% of each run, Pallas kernels for 18% -> 21%
where the time goes in v1:
time: 144 us; the launch traced here: 143 us
  waiting for transfers between devices  49.6 us (34%)
  starting transfers between devices  36.3 us (25%)
  Pallas kernels  35.9 us (25%)
  between operations  13.7 us (10%)
  local copies, waits for them, and re-layouts  6.73 us (5%)
    all_gather x1, waiting for transfers between devices, per_device(): w_all = lax.all_gather(w_embed, 'lev', axis=0, tiled=True)  39.9 us
    pallas_call x2, Pallas kernels, embed(): pl.pallas_call(embed_kernel, in_specs=[vmem(), pl.BlockSpec(memory_space=...  17.6 us
    ppermute x2, starting transfers between devices, per_device(): high.append(lax.ppermute(n, 'lat', down))  14.6 us
    all_to_all x2, starting transfers between devices, per_device(): lax.all_to_all(packed, 'lev', split_axis=0, concat_axis=0, tiled=True)  9.72 us
    ppermute x2, waiting for transfers between devices, per_device(): low.append(lax.ppermute(n, 'lat', up))  8.36 us
    ppermute x2, starting transfers between devices, strips(): lax.ppermute(jnp.concatenate([t[:, :STRIP] for t in tall], axis=0), 'lev'...  7.82 us
    pallas_call x1, Pallas kernels, sides(): pl.pallas_call(sides_kernel, in_specs=[smem(), smem()] + [vmem()] * 9, ou...  6.2 us
    pallas_call x2, Pallas kernels, pack(): pl.pallas_call(pack_kernel, grid=(1,), in_specs=[pl.BlockSpec((CHUNK, wid...  5.34 us
  transfers between devices with their start and end apart: 11, of which 3 were waited for; matrix products, arithmetic and copies ran while one was open for 2% of the time, Pallas kernels for 21%

profile of v1, /device:TPU:2, one launch (start us, length us, event | category | flops | bytes accessed | tf_op | source)
XLA Modules:
  0.0 142.9 jit_solution(10170249100685707177)
XLA Ops:
  6.5 0.7 all-gather.2.cloned.1.call-update
  7.3 2.7 %pack.3 = bf16[16,288,128]{2,1,0:T(8,128)(2,1)} custom-call(bf16[8,192,768]{2,1,0:T(8,128)(2,1)} %bitcast.9), custom_call_target="tpu_custom_call" | custom-call | bytes 2359296 | tf_op jit(solution)/shard_map/pack/pallas_call | solution.py:59
  9.9 5.9 %all-to-all-start.1 = ((bf16[16,288,128]{2,1,0:T(8,128)(2,1)}), bf16[16,288,128]{2,1,0:T(8,128)(2,1)S(1)}, u32[]{:S(2)}, u32[]{:S(2)}) async-start(bf16[16,288,128]{2,1,0:T(8,128)(2,1)} %pack.3), calls=%async_computation.1 | async-start | bytes 2359296 | tf_op jit(solution)/shard_map/all_to_all | solution.py:327
  15.9 2.7 %pack.2 = bf16[16,288,128]{2,1,0:T(8,128)(2,1)} custom-call(bf16[8,192,768]{2,1,0:T(8,128)(2,1)} %bitcast.10), custom_call_target="tpu_custom_call" | custom-call | bytes 2359296 | tf_op jit(solution)/shard_map/pack/pallas_call | solution.py:59
  18.6 39.9 %all-gather.2.cloned.1.call-done.w_hbm = bf16[3072,768]{1,0:T(8,128)(2,1)} async-done(((bf16[192,768]{1,0:T(8,128)(2,1)}), bf16[3072,768]{1,0:T(8,128)(2,1)}) %all-gather.2.cloned.1.call-update) | async-done | bytes 4718608 | tf_op jit(solution)/shard_map/all_gather | solution.py:313
  58.5 3.8 %all-to-all-start = ((bf16[16,288,128]{2,1,0:T(8,128)(2,1)}), bf16[16,288,128]{2,1,0:T(8,128)(2,1)S(1)}, u32[]{:S(2)}, u32[]{:S(2)}) async-start(bf16[16,288,128]{2,1,0:T(8,128)(2,1)} %pack.2), calls=%async_computation | async-start | bytes 2359296 | tf_op jit(solution)/shard_map/all_to_all | solution.py:327
  62.3 0.6 broadcast_in_dim.15.norm_ref
  62.9 0.1 broadcast_in_dim.12
  63.0 0.1 broadcast_in_dim.13
  63.0 0.1 broadcast_in_dim.14
  63.2 0.1 reshape.14
  63.3 0.6 fusion.pick_ref
  63.9 8.8 %embed.3 = (bf16[4,48,768]{2,1,0:T(8,128)(2,1)}, bf16[4,48,768]{2,1,0:T(8,128)(2,1)}) custom-call(bf16[16,288,128]{2,1,0:T(8,128)(2,1)} %copy-done.9, bf16[3072,768]{1,0:T(8,128)(2,1)} %all-gather.2.cloned.1.call-done.w_hbm, bf16[3,3072]{1,0:T(4,128)(2,1)} %fusion.pick_ref, f32[3,768]{1,0:T(4,128)} %bias_ref.3, f32[3,768]{1,0:T(4,128)} %gain_ref.3, ...), custom_call_target="tpu_custom_call" | custom-call | flops 2717908992 | bytes 5898240 | tf_op jit(solution)/shard_map/embed/pallas_call | solution.py:122
  72.7 7.7 %collective-permute-start.3 = (bf16[4,48,768]{2,1,0:T(8,128)(2,1)}, bf16[4,48,768]{2,1,0:T(8,128)(2,1)S(1)}, u32[]{:S(2)}, u32[]{:S(2)}) collective-permute-start(bf16[4,48,768]{2,1,0:T(8,128)(2,1)} %get-tuple-element.25.own0_ref), channel_id=1, source_target_pairs={{1,0},{2,1},{3,2},{4,3},{5,4},{6,5},{7,6},{8,7},{9,8},{10,9},{11,1... | collective-permute-start | bytes 884744 | tf_op jit(solution)/shard_map/ppermute | solution.py:332
  80.4 1.9 %collective-permute-start.2 = (bf16[4,48,768]{2,1,0:T(8,128)(2,1)}, bf16[4,48,768]{2,1,0:T(8,128)(2,1)S(1)}, u32[]{:S(2)}, u32[]{:S(2)}) collective-permute-start(bf16[4,48,768]{2,1,0:T(8,128)(2,1)} %get-tuple-element.25.own0_ref), channel_id=1, source_target_pairs={{0,1},{1,2},{2,3},{3,4},{4,5},{5,6},{6,7},{7,8},{8,9},{9,10},{10,1... | collective-permute-start | bytes 884744 | tf_op jit(solution)/shard_map/ppermute | solution.py:331
  82.3 0.9 fusion.4
  83.2 1.0 copy-done.8
  84.2 8.8 %embed.2 = (bf16[4,48,768]{2,1,0:T(8,128)(2,1)}, bf16[4,48,768]{2,1,0:T(8,128)(2,1)}) custom-call(bf16[16,288,128]{2,1,0:T(8,128)(2,1)} %copy-done.8, bf16[3072,768]{1,0:T(8,128)(2,1)} %all-gather.2.cloned.1.call-done.w_hbm, bf16[3,3072]{1,0:T(4,128)(2,1)} %fusion.pick_ref, f32[3,768]{1,0:T(4,128)} %bias_ref.3, f32[3,768]{1,0:T(4,128)} %gain_ref.3, ...), custom_call_target="tpu_custom_call" | custom-call | flops 2717908992 | bytes 5898240 | tf_op jit(solution)/shard_map/embed/pallas_call | solution.py:122
  93.0 6.9 %collective-permute-start.1 = (bf16[4,48,768]{2,1,0:T(8,128)(2,1)}, bf16[4,48,768]{2,1,0:T(8,128)(2,1)S(1)}, u32[]{:S(2)}, u32[]{:S(2)}) collective-permute-start(bf16[4,48,768]{2,1,0:T(8,128)(2,1)} %get-tuple-element.26.own1_ref), channel_id=1, source_target_pairs={{1,0},{2,1},{3,2},{4,3},{5,4},{6,5},{7,6},{8,7},{9,8},{10,9},{11,1... | collective-permute-start | bytes 884744 | tf_op jit(solution)/shard_map/ppermute | solution.py:332
  100.0 1.9 %collective-permute-start = (bf16[4,48,768]{2,1,0:T(8,128)(2,1)}, bf16[4,48,768]{2,1,0:T(8,128)(2,1)S(1)}, u32[]{:S(2)}, u32[]{:S(2)}) collective-permute-start(bf16[4,48,768]{2,1,0:T(8,128)(2,1)} %get-tuple-element.26.own1_ref), channel_id=1, source_target_pairs={{0,1},{1,2},{2,3},{3,4},{4,5},{5,6},{6,7},{7,8},{8,9},{9,10},{10,1... | collective-permute-start | bytes 884744 | tf_op jit(solution)/shard_map/ppermute | solution.py:331
  101.9 0.8 fusion.3
  102.8 0.1 collective-permute-start.4
  103.0 3.9 %collective-permute-start.5 = (bf16[16,8,768]{2,1,0:T(8,128)(2,1)S(1)}, bf16[16,8,768]{2,1,0:T(8,128)(2,1)S(1)}, u32[]{:S(2)}, u32[]{:S(2)}) collective-permute-start(bf16[16,8,768]{2,1,0:T(8,128)(2,1)S(1)} %pad_maximum_fusion.1), channel_id=1, source_target_pairs={{16,0},{32,16},{48,32},{64,48},{80,64},{96,80},{112,96},{128,112},... | collective-permute-start | bytes 589832 | tf_op jit(solution)/shard_map/ppermute | solution.py:336
  106.9 1.0 copy-done.1
  107.8 2.0 %copy-done.2 = bf16[768,2304]{1,0:T(8,128)(2,1)S(1)} copy-done((bf16[768,2304]{1,0:T(8,128)(2,1)S(1)}, bf16[768,2304]{1,0:T(8,128)(2,1)}, u32[]{:S(2)}) %copy-start.2) | copy-done | bytes 3538968
  109.9 2.5 %project.1 = (bf16[3,128,768]{2,1,0:T(8,128)(2,1)S(1)}, bf16[24,64,1536]{2,1,0:T(8,128)(2,1)S(1)}) custom-call(bf16[4,48,768]{2,1,0:T(8,128)(2,1)S(1)} %copy-done, bf16[4,48,768]{2,1,0:T(8,128)(2,1)S(1)} %copy-done.1, bf16[4,48,768]{2,1,0:T(8,128)(2,1)S(1)} %collective-permute-done.2.low_ref, bf16[4,48,768]{2,1,0:T(8,128)(2,1)S(1)} %collective-permute-done.3.high_ref, ...), custom_call_target="tpu_custom_call" | custom-call | flops 2264924160 | bytes 7077888 | tf_op jit(solution)/shard_map/project/pallas_call | solution.py:173
  112.4 0.6 collective-permute-done.1.high_ref
  112.9 8.4 %collective-permute-done.low_ref = bf16[4,48,768]{2,1,0:T(8,128)(2,1)S(1)} collective-permute-done((bf16[4,48,768]{2,1,0:T(8,128)(2,1)}, bf16[4,48,768]{2,1,0:T(8,128)(2,1)S(1)}, u32[]{:S(2)}, u32[]{:S(2)}) %collective-permute-start) | collective-permute-done | bytes 294944 | tf_op jit(solution)/shard_map/ppermute | solution.py:331
  121.3 0.3 collective-permute-start.6
  121.6 3.9 %collective-permute-start.7 = (bf16[8,8,768]{2,1,0:T(8,128)(2,1)S(1)}, bf16[8,8,768]{2,1,0:T(8,128)(2,1)S(1)}, u32[]{:S(2)}, u32[]{:S(2)}) collective-permute-start(bf16[8,8,768]{2,1,0:T(8,128)(2,1)S(1)} %pad_maximum_fusion.3), channel_id=1, source_target_pairs={{16,0},{32,16},{48,32},{64,48},{80,64},{96,80},{112,96},{128,112},... | collective-permute-start | bytes 294920 | tf_op jit(solution)/shard_map/ppermute | solution.py:336
  125.6 4.2 %middle.1 = (bf16[24,64,1536]{2,1,0:T(8,128)(2,1)S(1)}, bf16[8,16,768]{2,1,0:T(8,128)(2,1)S(1)}) custom-call(s32[128]{0:T(128)S(1)} %copy-done.5, s32[1]{0:T(128)} %bitcast.first_ref, bf16[3,128,768]{2,1,0:T(8,128)(2,1)S(1)} %get-tuple-element.30.q_ref, bf16[24,64,1536]{2,1,0:T(8,128)(2,1)S(1)} %get-tuple-element.31._, ...), custom_call_target="tpu_custom_call", output_to_operand_aliasing={{0}: (3, {})} | custom-call | flops 8000000000 | bytes 10000000 | tf_op jit(solution)/shard_map/middle/pallas_call | solution.py:258
  129.8 6.2 %sides.1 = (bf16[8,48,768]{2,1,0:T(8,128)(2,1)}, bf16[24,64,1536]{2,1,0:T(8,128)(2,1)S(1)}) custom-call(s32[128]{0:T(128)S(1)} %copy-done.5, s32[1]{0:T(128)} %bitcast.first_ref, bf16[3,128,768]{2,1,0:T(8,128)(2,1)S(1)} %get-tuple-element.30.q_ref, bf16[24,64,1536]{2,1,0:T(8,128)(2,1)S(1)} %get-tuple-element.36._, ...), custom_call_target="tpu_custom_call", output_to_operand_aliasing={{1}: (3, {})} | custom-call | flops 8999999488 | bytes 10000000 | tf_op jit(solution)/shard_map/sides/pallas_call | solution.py:294
  (41 shorter events, 0.2 us)
Async XLA Ops:
  6.5 51.9 %all-gather.2.cloned.1.call-start = ((), (), s32[]{:S(2)}) async-start(), calls=%async_computation.2 | async-start | bytes 5013504 | tf_op jit(solution)/shard_map/all_gather | solution.py:313
  9.9 48.5 %all-to-all-start.1 = ((bf16[16,288,128]{2,1,0:T(8,128)(2,1)}), bf16[16,288,128]{2,1,0:T(8,128)(2,1)S(1)}, u32[]{:S(2)}, u32[]{:S(2)}) async-start(bf16[16,288,128]{2,1,0:T(8,128)(2,1)} %pack.3), calls=%async_computation.1 | async-start | bytes 2359296 | tf_op jit(solution)/shard_map/all_to_all | solution.py:327
  15.9 46.4 %copy-start.10 = (f32[768]{0:T(1024)S(1)}, f32[768]{0:T(1024)}, u32[]{:S(2)}) copy-start(f32[768]{0:T(1024)} %param.15) | copy-start | bytes 9220
  15.9 47.0 %copy-start.11 = (s32[128]{0:T(128)S(1)}, s32[128]{0:T(128)}, u32[]{:S(2)}) copy-start(s32[128]{0:T(128)} %param.10) | copy-start | bytes 1540
  58.5 5.4 %copy-start.9 = (bf16[16,288,128]{2,1,0:T(8,128)(2,1)}, bf16[16,288,128]{2,1,0:T(8,128)(2,1)S(1)}, u32[]{:S(2)}) copy-start(bf16[16,288,128]{2,1,0:T(8,128)(2,1)S(1)} %all-to-all-done.1.x_ref) | copy-start | bytes 3538948
  58.5 24.7 %all-to-all-start = ((bf16[16,288,128]{2,1,0:T(8,128)(2,1)}), bf16[16,288,128]{2,1,0:T(8,128)(2,1)S(1)}, u32[]{:S(2)}, u32[]{:S(2)}) async-start(bf16[16,288,128]{2,1,0:T(8,128)(2,1)} %pack.2), calls=%async_computation | async-start | bytes 2359296 | tf_op jit(solution)/shard_map/all_to_all | solution.py:327
  72.7 29.2 %collective-permute-start.3 = (bf16[4,48,768]{2,1,0:T(8,128)(2,1)}, bf16[4,48,768]{2,1,0:T(8,128)(2,1)S(1)}, u32[]{:S(2)}, u32[]{:S(2)}) collective-permute-start(bf16[4,48,768]{2,1,0:T(8,128)(2,1)} %get-tuple-element.25.own0_ref), channel_id=1, source_target_pairs={{1,0},{2,1},{3,2},{4,3},{5,4},{6,5},{7,6},{8,7},{9,8},{10,9},{11,1... | collective-permute-start | bytes 884744 | tf_op jit(solution)/shard_map/ppermute | solution.py:332
  80.4 21.5 %collective-permute-start.2 = (bf16[4,48,768]{2,1,0:T(8,128)(2,1)}, bf16[4,48,768]{2,1,0:T(8,128)(2,1)S(1)}, u32[]{:S(2)}, u32[]{:S(2)}) collective-permute-start(bf16[4,48,768]{2,1,0:T(8,128)(2,1)} %get-tuple-element.25.own0_ref), channel_id=1, source_target_pairs={{0,1},{1,2},{2,3},{3,4},{4,5},{5,6},{6,7},{7,8},{8,9},{9,10},{10,1... | collective-permute-start | bytes 884744 | tf_op jit(solution)/shard_map/ppermute | solution.py:331
  83.2 23.7 %copy-start = (bf16[4,48,768]{2,1,0:T(8,128)(2,1)S(1)}, bf16[4,48,768]{2,1,0:T(8,128)(2,1)}, u32[]{:S(2)}) copy-start(bf16[4,48,768]{2,1,0:T(8,128)(2,1)} %get-tuple-element.25.own0_ref) | copy-start | bytes 884740
  83.2 1.0 copy-start.8
  93.0 19.9 %collective-permute-start.1 = (bf16[4,48,768]{2,1,0:T(8,128)(2,1)}, bf16[4,48,768]{2,1,0:T(8,128)(2,1)S(1)}, u32[]{:S(2)}, u32[]{:S(2)}) collective-permute-start(bf16[4,48,768]{2,1,0:T(8,128)(2,1)} %get-tuple-element.26.own1_ref), channel_id=1, source_target_pairs={{1,0},{2,1},{3,2},{4,3},{5,4},{6,5},{7,6},{8,7},{9,8},{10,9},{11,1... | collective-permute-start | bytes 884744 | tf_op jit(solution)/shard_map/ppermute | solution.py:332
  100.0 21.3 %collective-permute-start = (bf16[4,48,768]{2,1,0:T(8,128)(2,1)}, bf16[4,48,768]{2,1,0:T(8,128)(2,1)S(1)}, u32[]{:S(2)}, u32[]{:S(2)}) collective-permute-start(bf16[4,48,768]{2,1,0:T(8,128)(2,1)} %get-tuple-element.26.own1_ref), channel_id=1, source_target_pairs={{0,1},{1,2},{2,3},{3,4},{4,5},{5,6},{6,7},{7,8},{8,9},{9,10},{10,1... | collective-permute-start | bytes 884744 | tf_op jit(solution)/shard_map/ppermute | solution.py:331
  102.8 22.7 %collective-permute-start.4 = (bf16[16,8,768]{2,1,0:T(8,128)(2,1)S(1)}, bf16[16,8,768]{2,1,0:T(8,128)(2,1)S(1)}, u32[]{:S(2)}, u32[]{:S(2)}) collective-permute-start(bf16[16,8,768]{2,1,0:T(8,128)(2,1)S(1)} %pad_maximum_fusion), channel_id=1, source_target_pairs={{0,16},{16,32},{32,48},{48,64},{64,80},{80,96},{96,112},{112,128},... | collective-permute-start | bytes 589832 | tf_op jit(solution)/shard_map/ppermute | solution.py:335
  103.0 22.6 %collective-permute-start.5 = (bf16[16,8,768]{2,1,0:T(8,128)(2,1)S(1)}, bf16[16,8,768]{2,1,0:T(8,128)(2,1)S(1)}, u32[]{:S(2)}, u32[]{:S(2)}) collective-permute-start(bf16[16,8,768]{2,1,0:T(8,128)(2,1)S(1)} %pad_maximum_fusion.1), channel_id=1, source_target_pairs={{16,0},{32,16},{48,32},{64,48},{80,64},{96,80},{112,96},{128,112},... | collective-permute-start | bytes 589832 | tf_op jit(solution)/shard_map/ppermute | solution.py:336
  106.9 1.0 copy-start.1
  107.8 2.0 %copy-start.2 = (bf16[768,2304]{1,0:T(8,128)(2,1)S(1)}, bf16[768,2304]{1,0:T(8,128)(2,1)}, u32[]{:S(2)}) copy-start(bf16[768,2304]{1,0:T(8,128)(2,1)} %w_ref.5) | copy-start | bytes 10616836
  109.8 15.7 %copy-start.3 = (bf16[768,2304]{1,0:T(8,128)(2,1)S(1)}, bf16[768,2304]{1,0:T(8,128)(2,1)}, u32[]{:S(2)}) copy-start(bf16[768,2304]{1,0:T(8,128)(2,1)} %w_ref.5) | copy-start | bytes 10616836
  109.8 15.7 %copy-start.4 = (bf16[768,768]{1,0:T(8,128)(2,1)S(1)}, bf16[768,768]{1,0:T(8,128)(2,1)}, u32[]{:S(2)}) copy-start(bf16[768,768]{1,0:T(8,128)(2,1)} %wout_ref.3) | copy-start | bytes 3538948
  109.8 15.7 %copy-start.5 = (s32[128]{0:T(128)S(1)}, s32[128]{0:T(128)}, u32[]{:S(2)}) copy-start(s32[128]{0:T(128)} %start_ref.3) | copy-start | bytes 1540
  109.8 15.7 %copy-start.6 = (bf16[4,48,768]{2,1,0:T(8,128)(2,1)S(1)}, bf16[4,48,768]{2,1,0:T(8,128)(2,1)}, u32[]{:S(2)}) copy-start(bf16[4,48,768]{2,1,0:T(8,128)(2,1)} %get-tuple-element.34.emb0_ref) | copy-start | bytes 884740
  109.8 15.7 %copy-start.7 = (bf16[4,48,768]{2,1,0:T(8,128)(2,1)S(1)}, bf16[4,48,768]{2,1,0:T(8,128)(2,1)}, u32[]{:S(2)}) copy-start(bf16[4,48,768]{2,1,0:T(8,128)(2,1)} %get-tuple-element.35.emb1_ref) | copy-start | bytes 884740
  121.3 8.5 %collective-permute-start.6 = (bf16[8,8,768]{2,1,0:T(8,128)(2,1)S(1)}, bf16[8,8,768]{2,1,0:T(8,128)(2,1)S(1)}, u32[]{:S(2)}, u32[]{:S(2)}) collective-permute-start(bf16[8,8,768]{2,1,0:T(8,128)(2,1)S(1)} %pad_maximum_fusion.2), channel_id=1, source_target_pairs={{0,16},{16,32},{32,48},{48,64},{64,80},{80,96},{96,112},{112,128},... | collective-permute-start | bytes 294920 | tf_op jit(solution)/shard_map/ppermute | solution.py:335
  121.6 8.2 %collective-permute-start.7 = (bf16[8,8,768]{2,1,0:T(8,128)(2,1)S(1)}, bf16[8,8,768]{2,1,0:T(8,128)(2,1)S(1)}, u32[]{:S(2)}, u32[]{:S(2)}) collective-permute-start(bf16[8,8,768]{2,1,0:T(8,128)(2,1)S(1)} %pad_maximum_fusion.3), channel_id=1, source_target_pairs={{16,0},{32,16},{48,32},{64,48},{80,64},{96,80},{112,96},{128,112},... | collective-permute-start | bytes 294920 | tf_op jit(solution)/shard_map/ppermute | solution.py:336
Sparse Core Ops, SparseCore 0:
  9.2 49.2 all-gather.1

commit v2 on v1

--- a/solution.py
+++ b/solution.py
@@ -14,9 +14,12 @@
 STRIP = 8
 QCOLS = 16
 KCOLS = QCOLS + 2 * STRIP
+PLANES = 4
 CHUNK = 4
 SOURCES = 4
 MASKED = -1e30
+PART = 256
+EMBED_LIMIT = 50
 LIMIT = 36
 
 
@@ -68,16 +71,23 @@
     )(turned)
 
 
-def embed_kernel(x_ref, w_hbm, pick_ref, bias_ref, gain_ref, norm_ref, emb_ref, normed_ref, xs_ref, sum_ref, w_ref, sem):
+def weight_rows(w_ref, s, first, last):
+    size = w_ref.shape[2]
+    out = []
+    for quarter in range(w_ref.shape[1]):
+        low, high = max(first - quarter * size, 0), min(last - quarter * size, size)
+        if low < high:
+            out.append((s, quarter, low, high))
+    return out
+
+
+def embed_body(x_ref, w_ref, pick_ref, bias_ref, gain_ref, norm_ref, emb_ref, normed_ref, xs_ref, sum_ref, before):
     groups, width = bias_ref.shape
-    lev = x_ref.shape[0]
-    parts, depth, part = w_ref.shape
-    per = depth // lev
+    lev, quarters, size, _ = w_ref.shape
+    per = quarters * size
+    part = PART
     tokens = xs_ref.shape[0] // groups
     span = SOURCES * per
-    loads = [pltpu.make_async_copy(w_hbm.at[:, j * part:(j + 1) * part], w_ref.at[j], sem.at[j]) for j in range(parts)]
-    for load in loads:
-        load.start()
 
     for c in range(lev // SOURCES):
         here = range(c * SOURCES, (c + 1) * SOURCES)
@@ -88,16 +98,15 @@
         for g in range(groups):
             xs_ref[g * tokens:(g + 1) * tokens, c * span:(c + 1) * span] = x * pick_ref[g:g + 1, c * span:(c + 1) * span]
 
-    for j in range(parts):
-        loads[j].wait()
+    for j in range(width // part):
+        before(j)
         cols = slice(j * part, (j + 1) * part)
         acc = None
         for c in range(lev // SOURCES):
             here = range(c * SOURCES, (c + 1) * SOURCES)
-            w = jnp.concatenate(
-                [w_ref[j, s * per:s * per + 128, :] for s in here] + [w_ref[j, s * per + 128:(s + 1) * per, :] for s in here],
-                axis=0,
-            )
+            rows = [r for s in here for r in weight_rows(w_ref, s, 0, 128)]
+            rows += [r for s in here for r in weight_rows(w_ref, s, 128, per)]
+            w = jnp.concatenate([w_ref[s, quarter, low:high, cols] for s, quarter, low, high in rows], axis=0)
             term = jnp.dot(xs_ref[:, c * span:(c + 1) * span], w, preferred_element_type=jnp.float32)
             acc = term if acc is None else acc + term
         total = jnp.zeros((tokens, part), jnp.float32)
@@ -113,27 +122,91 @@
     normed_ref[...] = (wide * inv * norm_ref[...]).astype(jnp.bfloat16).reshape(normed_ref.shape)
 
 
-def embed(moved, w_all, pick, bias, gain, norm_gain):
+def embed_first_kernel(place_ref, x_ref, pick_ref, bias_ref, gain_ref, norm_ref, *refs):
+    pieces, (emb_ref, normed_ref, kept_ref, xs_ref, sum_ref, w_ref, sem) = refs[:10], refs[10:]
+    lev, quarters, _, width = w_ref.shape
+    half = width // 2
+    plane, core = place_ref[0], place_ref[1]
+    loads = []
+    for sibling in (0, 1):
+        column = pl.multiple_of(lax.rem(core + sibling, 2) * half, 128)
+        spots = ((0, 0, lev), (quarters - 1, 0, lev), (1, 0, lev), (2, 0, lev // 2), (2, lev // 2, lev))
+        for n, (ahead, first, last) in enumerate(spots):
+            quarter = lax.rem(plane + ahead, quarters)
+            loads.append(
+                pltpu.make_async_copy(
+                    pieces[sibling * 5 + n],
+                    w_ref.at[first:last, quarter, :, pl.ds(column, half)],
+                    sem.at[sibling * 5 + n],
+                )
+            )
+    for load in loads:
+        load.start()
+    keep = pltpu.make_async_copy(w_ref, kept_ref, sem.at[10])
+
+    def before(j):
+        if j == 0:
+            for load in loads:
+                load.wait()
+            keep.start()
+
+    embed_body(x_ref, w_ref, pick_ref, bias_ref, gain_ref, norm_ref, emb_ref, normed_ref, xs_ref, sum_ref, before)
+    keep.wait()
+
+
+def embed_next_kernel(x_ref, pick_ref, bias_ref, gain_ref, norm_ref, kept_ref, emb_ref, normed_ref, xs_ref, sum_ref, w_ref, sem):
+    loads = []
+    for j in range(w_ref.shape[3] // PART):
+        cols = slice(j * PART, (j + 1) * PART)
+        loads.append(pltpu.make_async_copy(kept_ref.at[:, :, :, cols], w_ref.at[:, :, :, cols], sem.at[j]))
+        loads[j].start()
+    embed_body(
+        x_ref, w_ref, pick_ref, bias_ref, gain_ref, norm_ref, emb_ref, normed_ref, xs_ref, sum_ref, lambda j: loads[j].wait()
+    )
+
+
+def embed(moved, place, w_all, pick, bias, gain, norm_gain):
+    lev = moved.shape[0]
     tokens = moved.shape[1] * 2 // 3
-    depth, width = w_all.shape
-    groups = bias.shape[0]
+    groups, width = bias.shape
+    depth = pick.shape[1]
     cols = tokens // CHUNK
-    part = 256
-    return pl.pallas_call(
-        embed_kernel,
-        in_specs=[vmem(), pl.BlockSpec(memory_space=pltpu.HBM)] + [vmem()] * 4,
-        out_specs=[vmem()] * 2,
-        out_shape=[jax.ShapeDtypeStruct((CHUNK, cols, width), jnp.bfloat16)] * 2,
-        scratch_shapes=[
-            pltpu.VMEM((groups * tokens, depth), jnp.bfloat16),
-            pltpu.VMEM((tokens, width), jnp.float32),
-            pltpu.VMEM((width // part, depth, part), jnp.bfloat16),
-            pltpu.SemaphoreType.DMA((width // part,)),
-        ],
-        compiler_params=params(60),
+    out_shape = [jax.ShapeDtypeStruct((CHUNK, cols, width), jnp.bfloat16)] * 2
+    size = w_all[0].shape[-2]
+    kept = jax.ShapeDtypeStruct((lev, depth // lev // size, size, width), jnp.bfloat16)
+    scratch = [
+        pltpu.VMEM((groups * tokens, depth), jnp.bfloat16),
+        pltpu.VMEM((tokens, width), jnp.float32),
+        pltpu.VMEM(kept.shape, kept.dtype),
+    ]
+    far = pl.BlockSpec(memory_space=pl.ANY)
+    common = dict(
+        compiler_params=params(EMBED_LIMIT),
         cost_estimate=cost(2 * tokens * depth * width * groups, depth * width * 2 + tokens * depth * 2),
-        name="embed",
-    )(moved, w_all, pick, bias, gain, norm_gain[None, :])
+    )
+    shared = (moved, pick, bias, gain, norm_gain[None, :])
+    if len(w_all) > 1:
+        return pl.pallas_call(
+            embed_first_kernel,
+            in_specs=[smem()] + [vmem()] * 5 + [far] * 10,
+            out_specs=[vmem()] * 2 + [far],
+            out_shape=out_shape + [kept],
+            scratch_shapes=scratch + [pltpu.SemaphoreType.DMA((11,))],
+            name="embed_first",
+            **common,
+        )(place, *shared, *w_all)
+    return (
+        *pl.pallas_call(
+            embed_next_kernel,
+            in_specs=[vmem()] * 5 + [far],
+            out_specs=[vmem()] * 2,
+            out_shape=out_shape,
+            scratch_shapes=scratch + [pltpu.SemaphoreType.DMA((width // PART,))],
+            name="embed_next",
+            **common,
+        )(*shared, *w_all),
+        w_all[0],
+    )
 
 
 def picks(level_group, lev, groups):
@@ -304,13 +377,42 @@
     )(lat_start, first_row, q, kv, left, right, w_qkv, w_out, emb0, emb1, centre)[0]
 
 
+def ring(count, stride, step):
+    return [
+        (base + i * stride, base + (i + step) % count * stride)
+        for base in range(stride)
+        for i in range(count)
+    ]
+
+
+def quarter_of_weights(w_embed, plane, lev):
+    size, half = w_embed.shape[0] // PLANES, w_embed.shape[1] // 2
+    mine = lax.dynamic_slice_in_dim(w_embed, plane * size, size, 0)
+    both = jnp.stack([mine[:, :half], mine[:, half:]], axis=0)
+    sent = jnp.broadcast_to(both[None], (lev // 2, 2, size, half)).reshape(lev, size, half)
+    return lax.all_to_all(sent, "lev", split_axis=0, concat_axis=0, tiled=True)
+
+
+def weight_pieces(own, lat):
+    stride = lat // PLANES
+    up, down = ring(PLANES, stride, 1), ring(PLANES, stride, -1)
+    near = [lax.ppermute(own, "lat", up), lax.ppermute(own, "lat", down)]
+    half = own.shape[0] // 2
+    far = [lax.ppermute(near[0][:half], "lat", up), lax.ppermute(near[1][half:], "lat", down)]
+    pieces = [own] + near + far
+    swap = [(i, i ^ 1) for i in range(own.shape[0])]
+    return pieces + [lax.ppermute(piece, "lev", swap) for piece in pieces]
+
+
 def per_device(
     fields, level_group, lat_start, w_embed, group_bias, group_gain, norm_gain, w_qkv, w_out
 ):
     rows = fields.shape[0]
     lev = lax.axis_size("lev")
     lat = lax.axis_size("lat")
-    w_all = lax.all_gather(w_embed, "lev", axis=0, tiled=True)
+    plane = lax.axis_index("lat") // (lat // PLANES)
+    place = jnp.stack([plane, lax.axis_index("lev") % 2]).astype(jnp.int32)
+    own = quarter_of_weights(w_embed, plane, lev)
     turned = jnp.transpose(fields, (0, 2, 1))
     pick = picks(level_group, lev, group_bias.shape[0])
     first_row = (lax.axis_index("lat") * rows).astype(jnp.int32).reshape(1)
@@ -319,13 +421,18 @@
     right_way = [(i, (i + 1) % lev) for i in range(lev)]
     left_way = [(b, a) for a, b in right_way]
 
+    later, own, pick, place = lax.optimization_barrier((turned, own, pick, place))
+    packed = [pack(later if c == 0 else turned, lev, c) for c in range(rows // CHUNK)]
+    w_all = weight_pieces(own, lat)
     emb, normed, low, high = [], [], [], []
     for c in range(rows // CHUNK):
-        packed = pack(turned, lev, c)
         if c > 0:
-            packed, w_all = lax.optimization_barrier((packed, w_all))
-        moved = lax.all_to_all(packed, "lev", split_axis=0, concat_axis=0, tiled=True)
-        e, n = embed(moved, w_all, pick, group_bias, group_gain, norm_gain)
+            packed[c] = held
+        moved = lax.all_to_all(packed[c], "lev", split_axis=0, concat_axis=0, tiled=True)
+        if c == 0:
+            held, *w_all[1:8] = lax.optimization_barrier((packed[1], *w_all[1:8]))
+        e, n, kept = embed(moved, place, w_all, pick, group_bias, group_gain, norm_gain)
+        w_all = [kept]
         emb.append(e)
         normed.append(n)
         low.append(lax.ppermute(n, "lat", up))

time: 144 us -> 135 us (0.938)
  between operations: 13.7 us -> 0.32 us
  starting transfers between devices: 36.3 us -> 48.2 us
  waiting for transfers between devices: 49.6 us -> 44.3 us
  Pallas kernels: 35.9 us -> 31.8 us
  local copies, waits for them, and re-layouts: 6.73 us -> 8.65 us
    all_gather x1 -> x0, waiting for transfers between devices: 39.9 us -> none  [per_device(): w_all = lax.all_gather(w_embed, 'lev', axis=0, tiled=True)]
    ppermute x0 -> x9, waiting for transfers between devices: none -> 23.1 us  [the longest x2 14.7 us: weight_pieces(): near = [lax.ppermute(own, 'lat', up), lax.ppermute(own, 'lat', down)]]
    all_to_all x2 -> x3, waiting for transfers between devices: 0.01 us -> 10.4 us  [the longest x1 10.4 us: quarter_of_weights(): return lax.all_to_all(sent, 'lev', split_axis=0, concat_axis=0, tiled=True)]
    ppermute x0 -> x9, starting transfers between devices: none -> 5.66 us  [the longest x1 2.95 us: weight_pieces(): lax.ppermute(near[1][half:], 'lat', down)]
    all_to_all x2 -> x3, starting transfers between devices: 9.72 us -> 15.1 us  [the longest x2 9.21 us: per_device(): lax.all_to_all(packed[c], 'lev', split_axis=0, concat_axis=0, tiled=True)]
    pallas_call x2, Pallas kernels: 17.6 us -> 13.5 us  [the longest x1 7 us: embed(): pl.pallas_call(embed_next_kernel, in_specs=[vmem()] * 5 + [far], out_spec...]
    slice x4, local copies, waits for them, and re-layouts: 1.72 us -> 0.05 us  [strips(): t[:, :STRIP]]
    slice x0 -> x2, local copies, waits for them, and re-layouts: none -> 1.5 us  [the longest x1 0.76 us: weight_pieces(): near[1][half:]]
  transfers between devices with their start and end apart: 11 -> 20, of which waited for: 3 -> 10; matrix products, arithmetic and copies ran while one was open for 2% -> 2% of each run, Pallas kernels for 21% -> 17%
where the time goes in v2:
time: 135 us; the launch traced here: 133 us
  starting transfers between devices  48.2 us (36%)
  waiting for transfers between devices  44.3 us (33%)
  Pallas kernels  31.8 us (24%)
  local copies, waits for them, and re-layouts  8.65 us (6%)
    ppermute x2, starting transfers between devices, per_device(): high.append(lax.ppermute(n, 'lat', down))  15.2 us
    ppermute x2, waiting for transfers between devices, weight_pieces(): near = [lax.ppermute(own, 'lat', up), lax.ppermute(own, 'lat', down)]  14.7 us
    all_to_all x1, waiting for transfers between devices, quarter_of_weights(): return lax.all_to_all(sent, 'lev', split_axis=0, concat_axis=0, tiled=True)  10.4 us
    all_to_all x2, starting transfers between devices, per_device(): lax.all_to_all(packed[c], 'lev', split_axis=0, concat_axis=0, tiled=True)  9.21 us
    ppermute x2, waiting for transfers between devices, per_device(): low.append(lax.ppermute(n, 'lat', up))  8.99 us
    ppermute x2, starting transfers between devices, strips(): lax.ppermute(jnp.concatenate([t[:, :STRIP] for t in tall], axis=0), 'lev'...  8.05 us
    pallas_call x1, Pallas kernels, embed(): pl.pallas_call(embed_next_kernel, in_specs=[vmem()] * 5 + [far], out_spec...  7 us
    pallas_call x1, Pallas kernels, embed(): pl.pallas_call(embed_first_kernel, in_specs=[smem()] + [vmem()] * 5 + [fa...  6.49 us
  transfers between devices with their start and end apart: 20, of which 10 were waited for; matrix products, arithmetic and copies ran while one was open for 2% of the time, Pallas kernels for 17%

profile of v2, /device:TPU:2, one launch (start us, length us, event | category | flops | bytes accessed | tf_op | source)
XLA Modules:
  0.0 133.5 jit_solution(17159386901983901079)
XLA Ops:
  0.0 0.8 dynamic-slice_bitcast_fusion.1
  0.8 0.9 broadcast_in_dim.18
  1.7 5.9 %all-to-all-start = ((bf16[16,48,384]{2,1,0:T(8,128)(2,1)}), bf16[16,48,384]{2,1,0:T(8,128)(2,1)S(1)}, u32[]{:S(2)}, u32[]{:S(2)}) async-start(bf16[16,48,384]{2,1,0:T(8,128)(2,1)} %bitcast.4), calls=%async_computation | async-start | bytes 1179648 | tf_op jit(solution)/shard_map/all_to_all | solution.py:393
  8.8 10.4 %all-to-all-done.refs_0_ = bf16[16,48,384]{2,1,0:T(8,128)(2,1)S(1)} async-done(((bf16[16,48,384]{2,1,0:T(8,128)(2,1)}), bf16[16,48,384]{2,1,0:T(8,128)(2,1)S(1)}, u32[]{:S(2)}, u32[]{:S(2)}) %all-to-all-start) | async-done | bytes 589856 | tf_op jit(solution)/shard_map/all_to_all | solution.py:393
  19.2 2.7 %pack.3 = bf16[16,288,128]{2,1,0:T(8,128)(2,1)} custom-call(bf16[8,192,768]{2,1,0:T(8,128)(2,1)} %bitcast.16), custom_call_target="tpu_custom_call" | custom-call | bytes 2359296 | tf_op jit(solution)/shard_map/pack/pallas_call | solution.py:62
  21.9 3.7 %all-to-all-start.2 = ((bf16[16,288,128]{2,1,0:T(8,128)(2,1)}), bf16[16,288,128]{2,1,0:T(8,128)(2,1)S(1)}, u32[]{:S(2)}, u32[]{:S(2)}) async-start(bf16[16,288,128]{2,1,0:T(8,128)(2,1)} %pack.3), calls=%async_computation.2 | async-start | bytes 2359296 | tf_op jit(solution)/shard_map/all_to_all | solution.py:431
  26.2 1.5 %collective-permute-start = (bf16[16,48,384]{2,1,0:T(8,128)(2,1)S(1)}, bf16[16,48,384]{2,1,0:T(8,128)(2,1)S(1)}, u32[]{:S(2)}, u32[]{:S(2)}) collective-permute-start(bf16[16,48,384]{2,1,0:T(8,128)(2,1)S(1)} %all-to-all-done.refs_0_), channel_id=1, source_target_pairs={{0,4},{4,8},{8,12},{12,0},{1,5},{5,9},{9,13},{13,1},{2,6},{6,10},{... | collective-permute-start | bytes 1769480 | tf_op jit(solution)/shard_map/ppermute | solution.py:399
  27.7 13.4 %collective-permute-done.1.refs_2_ = bf16[16,48,384]{2,1,0:T(8,128)(2,1)S(1)} collective-permute-done((bf16[16,48,384]{2,1,0:T(8,128)(2,1)S(1)}, bf16[16,48,384]{2,1,0:T(8,128)(2,1)S(1)}, u32[]{:S(2)}, u32[]{:S(2)}) %collective-permute-start.1) | collective-permute-done | bytes 589856 | tf_op jit(solution)/shard_map/ppermute | solution.py:399
  41.1 1.3 collective-permute-done.refs_1_
  43.1 3.0 %collective-permute-start.3 = (bf16[8,48,384]{2,1,0:T(8,128)(2,1)}, bf16[8,48,384]{2,1,0:T(8,128)(2,1)S(1)}, u32[]{:S(2)}, u32[]{:S(2)}) collective-permute-start(bf16[8,48,384]{2,1,0:T(8,128)(2,1)} %slice.75), channel_id=1, source_target_pairs={{0,12},{4,0},{8,4},{12,8},{1,13},{5,1},{9,5},{13,9},{2,14},{6,2},{... | collective-permute-start | bytes 884744 | tf_op jit(solution)/shard_map/ppermute | solution.py:401
  46.9 2.7 %pack.2 = bf16[16,288,128]{2,1,0:T(8,128)(2,1)} custom-call(bf16[8,192,768]{2,1,0:T(8,128)(2,1)} %bitcast.17), custom_call_target="tpu_custom_call" | custom-call | bytes 2359296 | tf_op jit(solution)/shard_map/pack/pallas_call | solution.py:62
  49.6 3.8 %collective-permute-done.3.refs_4_ = bf16[8,48,384]{2,1,0:T(8,128)(2,1)S(1)} collective-permute-done((bf16[8,48,384]{2,1,0:T(8,128)(2,1)}, bf16[8,48,384]{2,1,0:T(8,128)(2,1)S(1)}, u32[]{:S(2)}, u32[]{:S(2)}) %collective-permute-start.3) | collective-permute-done | bytes 294944 | tf_op jit(solution)/shard_map/ppermute | solution.py:401
  53.4 2.8 %collective-permute-done.2.refs_3_ = bf16[8,48,384]{2,1,0:T(8,128)(2,1)S(1)} collective-permute-done((bf16[8,48,384]{2,1,0:T(8,128)(2,1)}, bf16[8,48,384]{2,1,0:T(8,128)(2,1)S(1)}, u32[]{:S(2)}, u32[]{:S(2)}) %collective-permute-start.2) | collective-permute-done | bytes 294944 | tf_op jit(solution)/shard_map/ppermute | solution.py:401
  56.9 1.0 copy-done.11
  57.9 5.5 %all-to-all-start.1 = ((bf16[16,288,128]{2,1,0:T(8,128)(2,1)}), bf16[16,288,128]{2,1,0:T(8,128)(2,1)S(1)}, u32[]{:S(2)}, u32[]{:S(2)}) async-start(bf16[16,288,128]{2,1,0:T(8,128)(2,1)} %pack.2), calls=%async_computation.1 | async-start | bytes 2359296 | tf_op jit(solution)/shard_map/all_to_all | solution.py:431
  64.1 1.2 collective-permute-done.8.refs_9_
  65.9 1.0 copy-done.3
  66.9 1.0 copy-done.5
  67.8 6.5 %embed_first.1 = (bf16[4,48,768]{2,1,0:T(8,128)(2,1)S(1)}, bf16[4,48,768]{2,1,0:T(8,128)(2,1)S(1)}, bf16[16,4,48,768]{3,2,1,0:T(8,128)(2,1)}) custom-call(s32[2]{0:T(128)S(1)} %pad_add_fusion.1.place_ref, bf16[16,288,128]{2,1,0:T(8,128)(2,1)} %copy-done.11, bf16[3,3072]{1,0:T(4,128)(2,1)S(1)} %fusion.pick_ref, f32[3,768]{1,0:T(4,128)S(1)} %copy-done.6, ...), custom_call_target="tpu_custom_call" | custom-call | flops 2717908992 | bytes 5898240 | tf_op jit(solution)/shard_map/embed_first/pallas_call | solution.py:189
  75.0 8.2 %collective-permute-start.12 = (bf16[4,48,768]{2,1,0:T(8,128)(2,1)S(1)}, bf16[4,48,768]{2,1,0:T(8,128)(2,1)S(1)}, u32[]{:S(2)}, u32[]{:S(2)}) collective-permute-start(bf16[4,48,768]{2,1,0:T(8,128)(2,1)S(1)} %get-tuple-element.47.own0_ref), channel_id=1, source_target_pairs={{1,0},{2,1},{3,2},{4,3},{5,4},{6,5},{7,6},{8,7},{9,8},{10,9},{11,1... | collective-permute-start | bytes 884744 | tf_op jit(solution)/shard_map/ppermute | solution.py:439
  83.3 2.1 %collective-permute-start.11 = (bf16[4,48,768]{2,1,0:T(8,128)(2,1)S(1)}, bf16[4,48,768]{2,1,0:T(8,128)(2,1)S(1)}, u32[]{:S(2)}, u32[]{:S(2)}) collective-permute-start(bf16[4,48,768]{2,1,0:T(8,128)(2,1)S(1)} %get-tuple-element.47.own0_ref), channel_id=1, source_target_pairs={{0,1},{1,2},{2,3},{3,4},{4,5},{5,6},{6,7},{7,8},{8,9},{9,10},{10,1... | collective-permute-start | bytes 884744 | tf_op jit(solution)/shard_map/ppermute | solution.py:438
  85.4 7.0 %embed_next.1 = (bf16[4,48,768]{2,1,0:T(8,128)(2,1)S(1)}, bf16[4,48,768]{2,1,0:T(8,128)(2,1)S(1)}) custom-call(bf16[16,288,128]{2,1,0:T(8,128)(2,1)S(1)} %all-to-all-done.1.x_ref, bf16[3,3072]{1,0:T(4,128)(2,1)S(1)} %fusion.pick_ref, f32[3,768]{1,0:T(4,128)S(1)} %copy-done.6, f32[3,768]{1,0:T(4,128)S(1)} %copy-done.7, ...), custom_call_target="tpu_custom_call" | custom-call | flops 2717908992 | bytes 5898240 | tf_op jit(solution)/shard_map/embed_next/pallas_call | solution.py:199
  92.4 6.9 %collective-permute-start.10 = (bf16[4,48,768]{2,1,0:T(8,128)(2,1)S(1)}, bf16[4,48,768]{2,1,0:T(8,128)(2,1)S(1)}, u32[]{:S(2)}, u32[]{:S(2)}) collective-permute-start(bf16[4,48,768]{2,1,0:T(8,128)(2,1)S(1)} %get-tuple-element.48.own1_ref), channel_id=1, source_target_pairs={{1,0},{2,1},{3,2},{4,3},{5,4},{6,5},{7,6},{8,7},{9,8},{10,9},{11,1... | collective-permute-start | bytes 884744 | tf_op jit(solution)/shard_map/ppermute | solution.py:439
  99.4 1.9 %collective-permute-start.9 = (bf16[4,48,768]{2,1,0:T(8,128)(2,1)S(1)}, bf16[4,48,768]{2,1,0:T(8,128)(2,1)S(1)}, u32[]{:S(2)}, u32[]{:S(2)}) collective-permute-start(bf16[4,48,768]{2,1,0:T(8,128)(2,1)S(1)} %get-tuple-element.48.own1_ref), channel_id=1, source_target_pairs={{0,1},{1,2},{2,3},{3,4},{4,5},{5,6},{6,7},{7,8},{8,9},{9,10},{10,1... | collective-permute-start | bytes 884744 | tf_op jit(solution)/shard_map/ppermute | solution.py:438
  101.3 2.2 %collective-permute-done.11.low_ref = bf16[4,48,768]{2,1,0:T(8,128)(2,1)S(1)} collective-permute-done((bf16[4,48,768]{2,1,0:T(8,128)(2,1)S(1)}, bf16[4,48,768]{2,1,0:T(8,128)(2,1)S(1)}, u32[]{:S(2)}, u32[]{:S(2)}) %collective-permute-start.11) | collective-permute-done | bytes 294944 | tf_op jit(solution)/shard_map/ppermute | solution.py:438
  103.7 3.9 %collective-permute-start.14 = (bf16[16,8,768]{2,1,0:T(8,128)(2,1)S(1)}, bf16[16,8,768]{2,1,0:T(8,128)(2,1)S(1)}, u32[]{:S(2)}, u32[]{:S(2)}) collective-permute-start(bf16[16,8,768]{2,1,0:T(8,128)(2,1)S(1)} %pad_maximum_fusion.1), channel_id=1, source_target_pairs={{16,0},{32,16},{48,32},{64,48},{80,64},{96,80},{112,96},{128,112},... | collective-permute-start | bytes 589832 | tf_op jit(solution)/shard_map/ppermute | solution.py:443
  107.6 2.5 %project.1 = (bf16[3,128,768]{2,1,0:T(8,128)(2,1)S(1)}, bf16[24,64,1536]{2,1,0:T(8,128)(2,1)S(1)}) custom-call(bf16[4,48,768]{2,1,0:T(8,128)(2,1)S(1)} %get-tuple-element.47.own0_ref, bf16[4,48,768]{2,1,0:T(8,128)(2,1)S(1)} %get-tuple-element.48.own1_ref, bf16[4,48,768]{2,1,0:T(8,128)(2,1)S(1)} %collective-permute-done.11.low_ref, ...), custom_call_target="tpu_custom_call" | custom-call | flops 2264924160 | bytes 7077888 | tf_op jit(solution)/shard_map/project/pallas_call | solution.py:246
  110.2 1.8 %collective-permute-done.10.high_ref = bf16[4,48,768]{2,1,0:T(8,128)(2,1)S(1)} collective-permute-done((bf16[4,48,768]{2,1,0:T(8,128)(2,1)S(1)}, bf16[4,48,768]{2,1,0:T(8,128)(2,1)S(1)}, u32[]{:S(2)}, u32[]{:S(2)}) %collective-permute-start.10) | collective-permute-done | bytes 294944 | tf_op jit(solution)/shard_map/ppermute | solution.py:439
  111.9 6.8 %collective-permute-done.9.low_ref = bf16[4,48,768]{2,1,0:T(8,128)(2,1)S(1)} collective-permute-done((bf16[4,48,768]{2,1,0:T(8,128)(2,1)S(1)}, bf16[4,48,768]{2,1,0:T(8,128)(2,1)S(1)}, u32[]{:S(2)}, u32[]{:S(2)}) %collective-permute-start.9) | collective-permute-done | bytes 294944 | tf_op jit(solution)/shard_map/ppermute | solution.py:438
  118.9 4.1 %collective-permute-start.16 = (bf16[8,8,768]{2,1,0:T(8,128)(2,1)S(1)}, bf16[8,8,768]{2,1,0:T(8,128)(2,1)S(1)}, u32[]{:S(2)}, u32[]{:S(2)}) collective-permute-start(bf16[8,8,768]{2,1,0:T(8,128)(2,1)S(1)} %pad_maximum_fusion.3), channel_id=1, source_target_pairs={{16,0},{32,16},{48,32},{64,48},{80,64},{96,80},{112,96},{128,112},... | collective-permute-start | bytes 294920 | tf_op jit(solution)/shard_map/ppermute | solution.py:443
  123.0 4.2 %middle.1 = (bf16[24,64,1536]{2,1,0:T(8,128)(2,1)S(1)}, bf16[8,16,768]{2,1,0:T(8,128)(2,1)S(1)}) custom-call(s32[128]{0:T(128)S(1)} %copy-done.8, s32[1]{0:T(128)} %bitcast.first_ref, bf16[3,128,768]{2,1,0:T(8,128)(2,1)S(1)} %get-tuple-element.52.q_ref, bf16[24,64,1536]{2,1,0:T(8,128)(2,1)S(1)} %get-tuple-element.53._, ...), custom_call_target="tpu_custom_call", output_to_operand_aliasing={{0}: (3, {})} | custom-call | flops 8000000000 | bytes 10000000 | tf_op jit(solution)/shard_map/middle/pallas_call | solution.py:331
  127.3 6.2 %sides.1 = (bf16[8,48,768]{2,1,0:T(8,128)(2,1)}, bf16[24,64,1536]{2,1,0:T(8,128)(2,1)S(1)}) custom-call(s32[128]{0:T(128)S(1)} %copy-done.8, s32[1]{0:T(128)} %bitcast.first_ref, bf16[3,128,768]{2,1,0:T(8,128)(2,1)S(1)} %get-tuple-element.52.q_ref, bf16[24,64,1536]{2,1,0:T(8,128)(2,1)S(1)} %get-tuple-element.58._, ...), custom_call_target="tpu_custom_call", output_to_operand_aliasing={{1}: (3, {})} | custom-call | flops 8999999488 | bytes 10000000 | tf_op jit(solution)/shard_map/sides/pallas_call | solution.py:367
  (66 shorter events, 6.3 us)
Async XLA Ops:
  1.7 17.5 %all-to-all-start = ((bf16[16,48,384]{2,1,0:T(8,128)(2,1)}), bf16[16,48,384]{2,1,0:T(8,128)(2,1)S(1)}, u32[]{:S(2)}, u32[]{:S(2)}) async-start(bf16[16,48,384]{2,1,0:T(8,128)(2,1)} %bitcast.4), calls=%async_computation | async-start | bytes 1179648 | tf_op jit(solution)/shard_map/all_to_all | solution.py:393
  21.9 35.0 %all-to-all-start.2 = ((bf16[16,288,128]{2,1,0:T(8,128)(2,1)}), bf16[16,288,128]{2,1,0:T(8,128)(2,1)S(1)}, u32[]{:S(2)}, u32[]{:S(2)}) async-start(bf16[16,288,128]{2,1,0:T(8,128)(2,1)} %pack.3), calls=%async_computation.2 | async-start | bytes 2359296 | tf_op jit(solution)/shard_map/all_to_all | solution.py:431
  25.6 15.5 %collective-permute-start.1 = (bf16[16,48,384]{2,1,0:T(8,128)(2,1)S(1)}, bf16[16,48,384]{2,1,0:T(8,128)(2,1)S(1)}, u32[]{:S(2)}, u32[]{:S(2)}) collective-permute-start(bf16[16,48,384]{2,1,0:T(8,128)(2,1)S(1)} %all-to-all-done.refs_0_), channel_id=1, source_target_pairs={{0,12},{4,0},{8,4},{12,8},{1,13},{5,1},{9,5},{13,9},{2,14},{6,2},{... | collective-permute-start | bytes 1769480 | tf_op jit(solution)/shard_map/ppermute | solution.py:399
  26.2 16.2 %collective-permute-start = (bf16[16,48,384]{2,1,0:T(8,128)(2,1)S(1)}, bf16[16,48,384]{2,1,0:T(8,128)(2,1)S(1)}, u32[]{:S(2)}, u32[]{:S(2)}) collective-permute-start(bf16[16,48,384]{2,1,0:T(8,128)(2,1)S(1)} %all-to-all-done.refs_0_), channel_id=1, source_target_pairs={{0,4},{4,8},{8,12},{12,0},{1,5},{5,9},{9,13},{13,1},{2,6},{6,10},{... | collective-permute-start | bytes 1769480 | tf_op jit(solution)/shard_map/ppermute | solution.py:399
  27.7 21.9 %collective-permute-start.4 = (bf16[16,48,384]{2,1,0:T(8,128)(2,1)S(1)}, bf16[16,48,384]{2,1,0:T(8,128)(2,1)}, u32[]{:S(2)}, u32[]{:S(2)}) collective-permute-start(bf16[16,48,384]{2,1,0:T(8,128)(2,1)S(1)} %all-to-all-done.refs_0_), channel_id=1, source_target_pairs={{0,16},{16,0},{32,48},{48,32},{64,80},{80,64},{96,112},{112,96},{1... | collective-permute-start | bytes 1769480 | tf_op jit(solution)/shard_map/ppermute | solution.py:404
  41.1 15.1 %collective-permute-start.6 = (bf16[16,48,384]{2,1,0:T(8,128)(2,1)S(1)}, bf16[16,48,384]{2,1,0:T(8,128)(2,1)}, u32[]{:S(2)}, u32[]{:S(2)}) collective-permute-start(bf16[16,48,384]{2,1,0:T(8,128)(2,1)S(1)} %collective-permute-done.1.refs_2_), channel_id=1, source_target_pairs={{0,16},{16,0},{32,48},{48,32},{64,80},{80,64},{96,112},{112,96},{1... | collective-permute-start | bytes 1769480 | tf_op jit(solution)/shard_map/ppermute | solution.py:404
  42.4 14.5 %collective-permute-start.5 = (bf16[16,48,384]{2,1,0:T(8,128)(2,1)S(1)}, bf16[16,48,384]{2,1,0:T(8,128)(2,1)}, u32[]{:S(2)}, u32[]{:S(2)}) collective-permute-start(bf16[16,48,384]{2,1,0:T(8,128)(2,1)S(1)} %collective-permute-done.refs_1_), channel_id=1, source_target_pairs={{0,16},{16,0},{32,48},{48,32},{64,80},{80,64},{96,112},{112,96},{1... | collective-permute-start | bytes 1769480 | tf_op jit(solution)/shard_map/ppermute | solution.py:404
  43.1 10.2 %collective-permute-start.3 = (bf16[8,48,384]{2,1,0:T(8,128)(2,1)}, bf16[8,48,384]{2,1,0:T(8,128)(2,1)S(1)}, u32[]{:S(2)}, u32[]{:S(2)}) collective-permute-start(bf16[8,48,384]{2,1,0:T(8,128)(2,1)} %slice.75), channel_id=1, source_target_pairs={{0,12},{4,0},{8,4},{12,8},{1,13},{5,1},{9,5},{13,9},{2,14},{6,2},{... | collective-permute-start | bytes 884744 | tf_op jit(solution)/shard_map/ppermute | solution.py:401
  46.8 17.2 %copy-start.12 = (f32[768]{0:T(1024)S(1)}, f32[768]{0:T(1024)}, u32[]{:S(2)}) copy-start(f32[768]{0:T(1024)} %param.15) | copy-start | bytes 9220
  46.8 19.0 %copy-start.6 = (f32[3,768]{1,0:T(4,128)S(1)}, f32[3,768]{1,0:T(4,128)}, u32[]{:S(2)}) copy-start(f32[3,768]{1,0:T(4,128)} %bias_ref.3) | copy-start | bytes 27652
  46.8 19.0 %copy-start.7 = (f32[3,768]{1,0:T(4,128)S(1)}, f32[3,768]{1,0:T(4,128)}, u32[]{:S(2)}) copy-start(f32[3,768]{1,0:T(4,128)} %gain_ref.3) | copy-start | bytes 27652
  46.8 9.3 %collective-permute-start.2 = (bf16[8,48,384]{2,1,0:T(8,128)(2,1)}, bf16[8,48,384]{2,1,0:T(8,128)(2,1)S(1)}, u32[]{:S(2)}, u32[]{:S(2)}) collective-permute-start(bf16[8,48,384]{2,1,0:T(8,128)(2,1)} %slice.74), channel_id=1, source_target_pairs={{0,4},{4,8},{8,12},{12,0},{1,5},{5,9},{9,13},{13,1},{2,6},{6,10},{... | collective-permute-start | bytes 884744 | tf_op jit(solution)/shard_map/ppermute | solution.py:401
  53.4 11.9 %copy-start.2 = (bf16[8,48,384]{2,1,0:T(8,128)(2,1)}, bf16[8,48,384]{2,1,0:T(8,128)(2,1)S(1)}, u32[]{:S(2)}) copy-start(bf16[8,48,384]{2,1,0:T(8,128)(2,1)S(1)} %collective-permute-done.3.refs_4_) | copy-start | bytes 884740
  56.9 1.0 copy-start.11
  57.9 27.5 %all-to-all-start.1 = ((bf16[16,288,128]{2,1,0:T(8,128)(2,1)}), bf16[16,288,128]{2,1,0:T(8,128)(2,1)S(1)}, u32[]{:S(2)}, u32[]{:S(2)}) async-start(bf16[16,288,128]{2,1,0:T(8,128)(2,1)} %pack.2), calls=%async_computation.1 | async-start | bytes 2359296 | tf_op jit(solution)/shard_map/all_to_all | solution.py:431
  63.5 1.8 %collective-permute-start.8 = (bf16[8,48,384]{2,1,0:T(8,128)(2,1)S(1)}, bf16[8,48,384]{2,1,0:T(8,128)(2,1)}, u32[]{:S(2)}, u32[]{:S(2)}) collective-permute-start(bf16[8,48,384]{2,1,0:T(8,128)(2,1)S(1)} %collective-permute-done.3.refs_4_), channel_id=1, source_target_pairs={{0,16},{16,0},{32,48},{48,32},{64,80},{80,64},{96,112},{112,96},{1... | collective-permute-start | bytes 884744 | tf_op jit(solution)/shard_map/ppermute | solution.py:404
  63.9 2.0 %collective-permute-start.7 = (bf16[8,48,384]{2,1,0:T(8,128)(2,1)}, bf16[8,48,384]{2,1,0:T(8,128)(2,1)}, u32[]{:S(2)}, u32[]{:S(2)}) collective-permute-start(bf16[8,48,384]{2,1,0:T(8,128)(2,1)} %copy-done.4), channel_id=1, source_target_pairs={{0,16},{16,0},{32,48},{48,32},{64,80},{80,64},{96,112},{112,96},{1... | collective-permute-start | bytes 884744 | tf_op jit(solution)/shard_map/ppermute | solution.py:404
  65.9 1.0 copy-start.3
  66.9 1.0 copy-start.5
  74.3 0.7 copy-start.9
  75.0 26.3 %collective-permute-start.12 = (bf16[4,48,768]{2,1,0:T(8,128)(2,1)S(1)}, bf16[4,48,768]{2,1,0:T(8,128)(2,1)S(1)}, u32[]{:S(2)}, u32[]{:S(2)}) collective-permute-start(bf16[4,48,768]{2,1,0:T(8,128)(2,1)S(1)} %get-tuple-element.47.own0_ref), channel_id=1, source_target_pairs={{1,0},{2,1},{3,2},{4,3},{5,4},{6,5},{7,6},{8,7},{9,8},{10,9},{11,1... | collective-permute-start | bytes 884744 | tf_op jit(solution)/shard_map/ppermute | solution.py:439
  83.3 20.2 %collective-permute-start.11 = (bf16[4,48,768]{2,1,0:T(8,128)(2,1)S(1)}, bf16[4,48,768]{2,1,0:T(8,128)(2,1)S(1)}, u32[]{:S(2)}, u32[]{:S(2)}) collective-permute-start(bf16[4,48,768]{2,1,0:T(8,128)(2,1)S(1)} %get-tuple-element.47.own0_ref), channel_id=1, source_target_pairs={{0,1},{1,2},{2,3},{3,4},{4,5},{5,6},{6,7},{7,8},{8,9},{9,10},{10,1... | collective-permute-start | bytes 884744 | tf_op jit(solution)/shard_map/ppermute | solution.py:438
  85.4 22.2 %copy-start = (bf16[768,2304]{1,0:T(8,128)(2,1)S(1)}, bf16[768,2304]{1,0:T(8,128)(2,1)}, u32[]{:S(2)}) copy-start(bf16[768,2304]{1,0:T(8,128)(2,1)} %w_ref.5) | copy-start | bytes 10616836
  92.4 19.5 %collective-permute-start.10 = (bf16[4,48,768]{2,1,0:T(8,128)(2,1)S(1)}, bf16[4,48,768]{2,1,0:T(8,128)(2,1)S(1)}, u32[]{:S(2)}, u32[]{:S(2)}) collective-permute-start(bf16[4,48,768]{2,1,0:T(8,128)(2,1)S(1)} %get-tuple-element.48.own1_ref), channel_id=1, source_target_pairs={{1,0},{2,1},{3,2},{4,3},{5,4},{6,5},{7,6},{8,7},{9,8},{10,9},{11,1... | collective-permute-start | bytes 884744 | tf_op jit(solution)/shard_map/ppermute | solution.py:439
  99.4 19.4 %collective-permute-start.9 = (bf16[4,48,768]{2,1,0:T(8,128)(2,1)S(1)}, bf16[4,48,768]{2,1,0:T(8,128)(2,1)S(1)}, u32[]{:S(2)}, u32[]{:S(2)}) collective-permute-start(bf16[4,48,768]{2,1,0:T(8,128)(2,1)S(1)} %get-tuple-element.48.own1_ref), channel_id=1, source_target_pairs={{0,1},{1,2},{2,3},{3,4},{4,5},{5,6},{6,7},{7,8},{8,9},{9,10},{10,1... | collective-permute-start | bytes 884744 | tf_op jit(solution)/shard_map/ppermute | solution.py:438
  103.6 19.5 %collective-permute-start.13 = (bf16[16,8,768]{2,1,0:T(8,128)(2,1)S(1)}, bf16[16,8,768]{2,1,0:T(8,128)(2,1)S(1)}, u32[]{:S(2)}, u32[]{:S(2)}) collective-permute-start(bf16[16,8,768]{2,1,0:T(8,128)(2,1)S(1)} %pad_maximum_fusion), channel_id=1, source_target_pairs={{0,16},{16,32},{32,48},{48,64},{64,80},{80,96},{96,112},{112,128},... | collective-permute-start | bytes 589832 | tf_op jit(solution)/shard_map/ppermute | solution.py:442
  103.7 19.3 %copy-start.1 = (bf16[768,768]{1,0:T(8,128)(2,1)S(1)}, bf16[768,768]{1,0:T(8,128)(2,1)}, u32[]{:S(2)}) copy-start(bf16[768,768]{1,0:T(8,128)(2,1)} %wout_ref.3) | copy-start | bytes 3538948
  103.7 19.3 %copy-start.8 = (s32[128]{0:T(128)S(1)}, s32[128]{0:T(128)}, u32[]{:S(2)}) copy-start(s32[128]{0:T(128)} %start_ref.3) | copy-start | bytes 1540
  103.7 19.3 %copy-start.10 = (bf16[4,48,768]{2,1,0:T(8,128)(2,1)S(1)}, bf16[4,48,768]{2,1,0:T(8,128)(2,1)}, u32[]{:S(2)}) copy-start(bf16[4,48,768]{2,1,0:T(8,128)(2,1)} %copy-done.9) | copy-start | bytes 884740
  103.7 19.3 %collective-permute-start.14 = (bf16[16,8,768]{2,1,0:T(8,128)(2,1)S(1)}, bf16[16,8,768]{2,1,0:T(8,128)(2,1)S(1)}, u32[]{:S(2)}, u32[]{:S(2)}) collective-permute-start(bf16[16,8,768]{2,1,0:T(8,128)(2,1)S(1)} %pad_maximum_fusion.1), channel_id=1, source_target_pairs={{16,0},{32,16},{48,32},{64,48},{80,64},{96,80},{112,96},{128,112},... | collective-permute-start | bytes 589832 | tf_op jit(solution)/shard_map/ppermute | solution.py:443
  118.8 8.5 %collective-permute-start.15 = (bf16[8,8,768]{2,1,0:T(8,128)(2,1)S(1)}, bf16[8,8,768]{2,1,0:T(8,128)(2,1)S(1)}, u32[]{:S(2)}, u32[]{:S(2)}) collective-permute-start(bf16[8,8,768]{2,1,0:T(8,128)(2,1)S(1)} %pad_maximum_fusion.2), channel_id=1, source_target_pairs={{0,16},{16,32},{32,48},{48,64},{64,80},{80,96},{96,112},{112,128},... | collective-permute-start | bytes 294920 | tf_op jit(solution)/shard_map/ppermute | solution.py:442
  118.9 8.4 %collective-permute-start.16 = (bf16[8,8,768]{2,1,0:T(8,128)(2,1)S(1)}, bf16[8,8,768]{2,1,0:T(8,128)(2,1)S(1)}, u32[]{:S(2)}, u32[]{:S(2)}) collective-permute-start(bf16[8,8,768]{2,1,0:T(8,128)(2,1)S(1)} %pad_maximum_fusion.3), channel_id=1, source_target_pairs={{16,0},{32,16},{48,32},{64,48},{80,64},{96,80},{112,96},{128,112},... | collective-permute-start | bytes 294920 | tf_op jit(solution)/shard_map/ppermute | solution.py:443
  (1 other events, 0.7 us)

commit v3 on v2

--- a/solution.py
+++ b/solution.py
@@ -19,7 +19,8 @@
 SOURCES = 4
 MASKED = -1e30
 PART = 256
-EMBED_LIMIT = 50
+PACK_FLOPS = (0, 18e9)
+EMBED_LIMIT = 56
 LIMIT = 36
 
 
@@ -66,7 +67,7 @@
         out_specs=pl.BlockSpec((lev, tokens + tokens // 2, 128), lambda i: (0, 0, 0)),
         out_shape=jax.ShapeDtypeStruct((lev, tokens + tokens // 2, 128), turned.dtype),
         compiler_params=params(60),
-        cost_estimate=cost(0, 2 * turned.size),
+        cost_estimate=cost(PACK_FLOPS[chunk], 2 * turned.size),
         name="pack",
     )(turned)
 
@@ -430,7 +431,7 @@
             packed[c] = held
         moved = lax.all_to_all(packed[c], "lev", split_axis=0, concat_axis=0, tiled=True)
         if c == 0:
-            held, *w_all[1:8] = lax.optimization_barrier((packed[1], *w_all[1:8]))
+            held, *w_all = lax.optimization_barrier((packed[1], *w_all))
         e, n, kept = embed(moved, place, w_all, pick, group_bias, group_gain, norm_gain)
         w_all = [kept]
         emb.append(e)

time: 135 us -> 125 us (0.926)
  waiting for transfers between devices: 44.3 us -> 33 us
  Pallas kernels: 31.8 us -> 35 us
  starting transfers between devices: 48.2 us -> 46.6 us
    ppermute x2, waiting for transfers between devices: 14.7 us -> 6.52 us  [weight_pieces(): near = [lax.ppermute(own, 'lat', up), lax.ppermute(own, 'lat', down)]]
    all_to_all x2, waiting for transfers between devices: 0.01 us -> 3.68 us  [per_device(): lax.all_to_all(packed[c], 'lev', split_axis=0, concat_axis=0, tiled=True)]
    ppermute x2, waiting for transfers between devices: 8.99 us -> 6.12 us  [per_device(): low.append(lax.ppermute(n, 'lat', up))]
    ppermute x1, starting transfers between devices: 2.95 us -> 0.89 us  [weight_pieces(): lax.ppermute(near[1][half:], 'lat', down)]
    pallas_call x1, Pallas kernels: 7 us -> 9.05 us  [embed(): pl.pallas_call(embed_next_kernel, in_specs=[vmem()] * 5 + [far], out_spec...]
    ppermute x2, starting transfers between devices: 15.2 us -> 13.2 us  [per_device(): high.append(lax.ppermute(n, 'lat', down))]
    ppermute x5, waiting for transfers between devices: 1.83 us -> 0.01 us  [weight_pieces(): return pieces + [lax.ppermute(piece, 'lev', swap) for piece in pieces]]
    ppermute x2, waiting for transfers between devices: 1.76 us -> 0.01 us  [per_device(): high.append(lax.ppermute(n, 'lat', down))]
  transfers between devices with their start and end apart: 20 -> 20, of which waited for: 10 -> 7; matrix products, arithmetic and copies ran while one was open for 2% -> 4% of each run, Pallas kernels for 17% -> 23%
where the time goes in v3:
time: 125 us; the launch traced here: 124 us
  starting transfers between devices  46.6 us (37%)
  Pallas kernels  35 us (28%)
  waiting for transfers between devices  33 us (26%)
  local copies, waits for them, and re-layouts  7.85 us (6%)
  other arithmetic  1.33 us (1%)
    ppermute x2, starting transfers between devices, per_device(): high.append(lax.ppermute(n, 'lat', down))  13.2 us
    ppermute x2, starting transfers between devices, strips(): lax.ppermute(jnp.concatenate([t[:, :STRIP] for t in tall], axis=0), 'lev'...  9.35 us
    all_to_all x1, waiting for transfers between devices, quarter_of_weights(): return lax.all_to_all(sent, 'lev', split_axis=0, concat_axis=0, tiled=True)  9.31 us
    pallas_call x1, Pallas kernels, embed(): pl.pallas_call(embed_next_kernel, in_specs=[vmem()] * 5 + [far], out_spec...  9.05 us
    all_to_all x2, starting transfers between devices, per_device(): lax.all_to_all(packed[c], 'lev', split_axis=0, concat_axis=0, tiled=True)  8.21 us
    pallas_call x1, Pallas kernels, embed(): pl.pallas_call(embed_first_kernel, in_specs=[smem()] + [vmem()] * 5 + [fa...  7.8 us
    ppermute x2, waiting for transfers between devices, weight_pieces(): near = [lax.ppermute(own, 'lat', up), lax.ppermute(own, 'lat', down)]  6.52 us
    pallas_call x1, Pallas kernels, sides(): pl.pallas_call(sides_kernel, in_specs=[smem(), smem()] + [vmem()] * 9, ou...  6.2 us
  transfers between devices with their start and end apart: 20, of which 7 were waited for; matrix products, arithmetic and copies ran while one was open for 4% of the time, Pallas kernels for 23%

profile of v3, /device:TPU:2, one launch (start us, length us, event | category | flops | bytes accessed | tf_op | source)
XLA Modules:
  0.0 124.2 jit_solution(6462686667255506348)
XLA Ops:
  0.0 0.8 dynamic-slice_bitcast_fusion.1
  0.8 0.9 broadcast_in_dim.18
  1.7 5.9 %all-to-all-start = ((bf16[16,48,384]{2,1,0:T(8,128)(2,1)}), bf16[16,48,384]{2,1,0:T(8,128)(2,1)S(1)}, u32[]{:S(2)}, u32[]{:S(2)}) async-start(bf16[16,48,384]{2,1,0:T(8,128)(2,1)} %bitcast.4), calls=%async_computation | async-start | bytes 1179648 | tf_op jit(solution)/shard_map/all_to_all | solution.py:394
  7.6 0.7 broadcast_in_dim.19
  9.9 9.3 %all-to-all-done.refs_0_ = bf16[16,48,384]{2,1,0:T(8,128)(2,1)S(1)} async-done(((bf16[16,48,384]{2,1,0:T(8,128)(2,1)}), bf16[16,48,384]{2,1,0:T(8,128)(2,1)S(1)}, u32[]{:S(2)}, u32[]{:S(2)}) %all-to-all-start) | async-done | bytes 589856 | tf_op jit(solution)/shard_map/all_to_all | solution.py:394
  19.8 1.5 %collective-permute-start = (bf16[16,48,384]{2,1,0:T(8,128)(2,1)S(1)}, bf16[16,48,384]{2,1,0:T(8,128)(2,1)S(1)}, u32[]{:S(2)}, u32[]{:S(2)}) collective-permute-start(bf16[16,48,384]{2,1,0:T(8,128)(2,1)S(1)} %all-to-all-done.refs_0_), channel_id=1, source_target_pairs={{0,4},{4,8},{8,12},{12,0},{1,5},{5,9},{9,13},{13,1},{2,6},{6,10},{... | collective-permute-start | bytes 1769480 | tf_op jit(solution)/shard_map/ppermute | solution.py:400
  21.2 2.7 %pack.3 = bf16[16,288,128]{2,1,0:T(8,128)(2,1)} custom-call(bf16[8,192,768]{2,1,0:T(8,128)(2,1)} %bitcast.16), custom_call_target="tpu_custom_call" | custom-call | bytes 2359296 | tf_op jit(solution)/shard_map/pack/pallas_call | solution.py:63
  23.9 3.7 %all-to-all-start.2 = ((bf16[16,288,128]{2,1,0:T(8,128)(2,1)}), bf16[16,288,128]{2,1,0:T(8,128)(2,1)S(1)}, u32[]{:S(2)}, u32[]{:S(2)}) async-start(bf16[16,288,128]{2,1,0:T(8,128)(2,1)} %pack.3), calls=%async_computation.2 | async-start | bytes 2359296 | tf_op jit(solution)/shard_map/all_to_all | solution.py:432
  27.6 6.2 %collective-permute-done.1.refs_2_ = bf16[16,48,384]{2,1,0:T(8,128)(2,1)S(1)} collective-permute-done((bf16[16,48,384]{2,1,0:T(8,128)(2,1)S(1)}, bf16[16,48,384]{2,1,0:T(8,128)(2,1)S(1)}, u32[]{:S(2)}, u32[]{:S(2)}) %collective-permute-start.1) | collective-permute-done | bytes 589856 | tf_op jit(solution)/shard_map/ppermute | solution.py:400
  33.8 0.9 collective-permute-start.3
  35.1 1.0 collective-permute-start.2
  36.6 4.7 %collective-permute-done.3.refs_4_ = bf16[8,48,384]{2,1,0:T(8,128)(2,1)S(1)} collective-permute-done((bf16[8,48,384]{2,1,0:T(8,128)(2,1)S(1)}, bf16[8,48,384]{2,1,0:T(8,128)(2,1)S(1)}, u32[]{:S(2)}, u32[]{:S(2)}) %collective-permute-start.3) | collective-permute-done | bytes 294944 | tf_op jit(solution)/shard_map/ppermute | solution.py:402
  41.3 2.7 %collective-permute-done.2.refs_3_ = bf16[8,48,384]{2,1,0:T(8,128)(2,1)} collective-permute-done((bf16[8,48,384]{2,1,0:T(8,128)(2,1)S(1)}, bf16[8,48,384]{2,1,0:T(8,128)(2,1)}, u32[]{:S(2)}, u32[]{:S(2)}) %collective-permute-start.2) | collective-permute-done | bytes 294944 | tf_op jit(solution)/shard_map/ppermute | solution.py:402
  44.0 2.7 %pack.2 = bf16[16,288,128]{2,1,0:T(8,128)(2,1)} custom-call(bf16[8,192,768]{2,1,0:T(8,128)(2,1)} %bitcast.17), custom_call_target="tpu_custom_call" | custom-call | flops 17999998976 | bytes 2359296 | tf_op jit(solution)/shard_map/pack/pallas_call | solution.py:63
  47.5 4.5 %all-to-all-start.1 = ((bf16[16,288,128]{2,1,0:T(8,128)(2,1)}), bf16[16,288,128]{2,1,0:T(8,128)(2,1)S(1)}, u32[]{:S(2)}, u32[]{:S(2)}) async-start(bf16[16,288,128]{2,1,0:T(8,128)(2,1)} %pack.2), calls=%async_computation.1 | async-start | bytes 2359296 | tf_op jit(solution)/shard_map/all_to_all | solution.py:432
  52.6 7.8 %embed_first.1 = (bf16[4,48,768]{2,1,0:T(8,128)(2,1)}, bf16[4,48,768]{2,1,0:T(8,128)(2,1)}, bf16[16,4,48,768]{3,2,1,0:T(8,128)(2,1)}) custom-call(s32[2]{0:T(128)} %pad_add_fusion.1.place_ref, bf16[16,288,128]{2,1,0:T(8,128)(2,1)} %copy-done.7, bf16[3,3072]{1,0:T(4,128)(2,1)} %fusion.pick_ref, f32[3,768]{1,0:T(4,128)} %bias_ref.3, f32[3,768]{1,0:T(4,128)} %gain_ref.3, ...), custom_call_target="tpu_custom_call" | custom-call | flops 2717908992 | bytes 5898240 | tf_op jit(solution)/shard_map/embed_first/pallas_call | solution.py:190
  60.4 9.7 %collective-permute-start.12 = (bf16[4,48,768]{2,1,0:T(8,128)(2,1)}, bf16[4,48,768]{2,1,0:T(8,128)(2,1)S(1)}, u32[]{:S(2)}, u32[]{:S(2)}) collective-permute-start(bf16[4,48,768]{2,1,0:T(8,128)(2,1)} %get-tuple-element.53.own0_ref), channel_id=1, source_target_pairs={{1,0},{2,1},{3,2},{4,3},{5,4},{6,5},{7,6},{8,7},{9,8},{10,9},{11,1... | collective-permute-start | bytes 884744 | tf_op jit(solution)/shard_map/ppermute | solution.py:440
  70.1 2.1 %collective-permute-start.11 = (bf16[4,48,768]{2,1,0:T(8,128)(2,1)}, bf16[4,48,768]{2,1,0:T(8,128)(2,1)S(1)}, u32[]{:S(2)}, u32[]{:S(2)}) collective-permute-start(bf16[4,48,768]{2,1,0:T(8,128)(2,1)} %get-tuple-element.53.own0_ref), channel_id=1, source_target_pairs={{0,1},{1,2},{2,3},{3,4},{4,5},{5,6},{6,7},{7,8},{8,9},{9,10},{10,1... | collective-permute-start | bytes 884744 | tf_op jit(solution)/shard_map/ppermute | solution.py:439
  72.2 0.8 fusion.4
  73.1 3.7 %all-to-all-done.1.x_ref = bf16[16,288,128]{2,1,0:T(8,128)(2,1)S(1)} async-done(((bf16[16,288,128]{2,1,0:T(8,128)(2,1)}), bf16[16,288,128]{2,1,0:T(8,128)(2,1)S(1)}, u32[]{:S(2)}, u32[]{:S(2)}) %all-to-all-start.1) | async-done | bytes 1179680 | tf_op jit(solution)/shard_map/all_to_all | solution.py:432
  76.8 1.0 copy-done.8
  77.8 9.0 %embed_next.1 = (bf16[4,48,768]{2,1,0:T(8,128)(2,1)}, bf16[4,48,768]{2,1,0:T(8,128)(2,1)}) custom-call(bf16[16,288,128]{2,1,0:T(8,128)(2,1)} %copy-done.8, bf16[3,3072]{1,0:T(4,128)(2,1)} %fusion.pick_ref, f32[3,768]{1,0:T(4,128)} %bias_ref.3, f32[3,768]{1,0:T(4,128)} %gain_ref.3, f32[1,768]{1,0:T(1,128)} %broadcast_in_dim.22.norm_ref, ...), custom_call_target="tpu_custom_call" | custom-call | flops 2717908992 | bytes 5898240 | tf_op jit(solution)/shard_map/embed_next/pallas_call | solution.py:200
  86.8 3.5 %collective-permute-start.10 = (bf16[4,48,768]{2,1,0:T(8,128)(2,1)}, bf16[4,48,768]{2,1,0:T(8,128)(2,1)S(1)}, u32[]{:S(2)}, u32[]{:S(2)}) collective-permute-start(bf16[4,48,768]{2,1,0:T(8,128)(2,1)} %get-tuple-element.54.own1_ref), channel_id=1, source_target_pairs={{1,0},{2,1},{3,2},{4,3},{5,4},{6,5},{7,6},{8,7},{9,8},{10,9},{11,1... | collective-permute-start | bytes 884744 | tf_op jit(solution)/shard_map/ppermute | solution.py:440
  90.3 3.2 %collective-permute-start.9 = (bf16[4,48,768]{2,1,0:T(8,128)(2,1)}, bf16[4,48,768]{2,1,0:T(8,128)(2,1)S(1)}, u32[]{:S(2)}, u32[]{:S(2)}) collective-permute-start(bf16[4,48,768]{2,1,0:T(8,128)(2,1)} %get-tuple-element.54.own1_ref), channel_id=1, source_target_pairs={{0,1},{1,2},{2,3},{3,4},{4,5},{5,6},{6,7},{7,8},{8,9},{9,10},{10,1... | collective-permute-start | bytes 884744 | tf_op jit(solution)/shard_map/ppermute | solution.py:439
  93.6 0.8 fusion.3
  94.7 3.9 %collective-permute-start.14 = (bf16[16,8,768]{2,1,0:T(8,128)(2,1)S(1)}, bf16[16,8,768]{2,1,0:T(8,128)(2,1)S(1)}, u32[]{:S(2)}, u32[]{:S(2)}) collective-permute-start(bf16[16,8,768]{2,1,0:T(8,128)(2,1)S(1)} %pad_maximum_fusion.1), channel_id=1, source_target_pairs={{16,0},{32,16},{48,32},{64,48},{80,64},{96,80},{112,96},{128,112},... | collective-permute-start | bytes 589832 | tf_op jit(solution)/shard_map/ppermute | solution.py:444
  98.6 1.0 copy-done.1
  99.5 2.5 %project.1 = (bf16[3,128,768]{2,1,0:T(8,128)(2,1)S(1)}, bf16[24,64,1536]{2,1,0:T(8,128)(2,1)S(1)}) custom-call(bf16[4,48,768]{2,1,0:T(8,128)(2,1)S(1)} %copy-done, bf16[4,48,768]{2,1,0:T(8,128)(2,1)S(1)} %copy-done.1, bf16[4,48,768]{2,1,0:T(8,128)(2,1)S(1)} %collective-permute-done.11.low_ref, bf16[4,48,768]{2,1,0:T(8,128)(2,1)S(1)} %collective-permute-done.12.high_ref, ...), custom_call_target="tpu_custom_call" | custom-call | flops 2264924160 | bytes 7077888 | tf_op jit(solution)/shard_map/project/pallas_call | solution.py:247
  102.0 6.1 %collective-permute-done.9.low_ref = bf16[4,48,768]{2,1,0:T(8,128)(2,1)S(1)} collective-permute-done((bf16[4,48,768]{2,1,0:T(8,128)(2,1)}, bf16[4,48,768]{2,1,0:T(8,128)(2,1)S(1)}, u32[]{:S(2)}, u32[]{:S(2)}) %collective-permute-start.9) | collective-permute-done | bytes 294944 | tf_op jit(solution)/shard_map/ppermute | solution.py:439
  108.3 5.4 %collective-permute-start.16 = (bf16[8,8,768]{2,1,0:T(8,128)(2,1)S(1)}, bf16[8,8,768]{2,1,0:T(8,128)(2,1)S(1)}, u32[]{:S(2)}, u32[]{:S(2)}) collective-permute-start(bf16[8,8,768]{2,1,0:T(8,128)(2,1)S(1)} %pad_maximum_fusion.3), channel_id=1, source_target_pairs={{16,0},{32,16},{48,32},{64,48},{80,64},{96,80},{112,96},{128,112},... | collective-permute-start | bytes 294920 | tf_op jit(solution)/shard_map/ppermute | solution.py:444
  113.8 4.2 %middle.1 = (bf16[24,64,1536]{2,1,0:T(8,128)(2,1)S(1)}, bf16[8,16,768]{2,1,0:T(8,128)(2,1)S(1)}) custom-call(s32[128]{0:T(128)S(1)} %copy-done.4, s32[1]{0:T(128)} %bitcast.first_ref, bf16[3,128,768]{2,1,0:T(8,128)(2,1)S(1)} %get-tuple-element.58.q_ref, bf16[24,64,1536]{2,1,0:T(8,128)(2,1)S(1)} %get-tuple-element.59._, ...), custom_call_target="tpu_custom_call", output_to_operand_aliasing={{0}: (3, {})} | custom-call | flops 8000000000 | bytes 10000000 | tf_op jit(solution)/shard_map/middle/pallas_call | solution.py:332
  118.0 6.2 %sides.1 = (bf16[8,48,768]{2,1,0:T(8,128)(2,1)}, bf16[24,64,1536]{2,1,0:T(8,128)(2,1)S(1)}) custom-call(s32[128]{0:T(128)S(1)} %copy-done.4, s32[1]{0:T(128)} %bitcast.first_ref, bf16[3,128,768]{2,1,0:T(8,128)(2,1)S(1)} %get-tuple-element.58.q_ref, bf16[24,64,1536]{2,1,0:T(8,128)(2,1)S(1)} %get-tuple-element.64._, ...), custom_call_target="tpu_custom_call", output_to_operand_aliasing={{1}: (3, {})} | custom-call | flops 8999999488 | bytes 10000000 | tf_op jit(solution)/shard_map/sides/pallas_call | solution.py:368
  (72 shorter events, 4.7 us)
Async XLA Ops:
  1.7 17.5 %all-to-all-start = ((bf16[16,48,384]{2,1,0:T(8,128)(2,1)}), bf16[16,48,384]{2,1,0:T(8,128)(2,1)S(1)}, u32[]{:S(2)}, u32[]{:S(2)}) async-start(bf16[16,48,384]{2,1,0:T(8,128)(2,1)} %bitcast.4), calls=%async_computation | async-start | bytes 1179648 | tf_op jit(solution)/shard_map/all_to_all | solution.py:394
  19.2 16.8 %copy-start.9 = (bf16[16,48,384]{2,1,0:T(8,128)(2,1)}, bf16[16,48,384]{2,1,0:T(8,128)(2,1)S(1)}, u32[]{:S(2)}) copy-start(bf16[16,48,384]{2,1,0:T(8,128)(2,1)S(1)} %all-to-all-done.refs_0_) | copy-start | bytes 1769476
  19.2 14.6 %collective-permute-start.1 = (bf16[16,48,384]{2,1,0:T(8,128)(2,1)S(1)}, bf16[16,48,384]{2,1,0:T(8,128)(2,1)S(1)}, u32[]{:S(2)}, u32[]{:S(2)}) collective-permute-start(bf16[16,48,384]{2,1,0:T(8,128)(2,1)S(1)} %all-to-all-done.refs_0_), channel_id=1, source_target_pairs={{0,12},{4,0},{8,4},{12,8},{1,13},{5,1},{9,5},{13,9},{2,14},{6,2},{... | collective-permute-start | bytes 1769480 | tf_op jit(solution)/shard_map/ppermute | solution.py:400
  19.8 15.3 %collective-permute-start = (bf16[16,48,384]{2,1,0:T(8,128)(2,1)S(1)}, bf16[16,48,384]{2,1,0:T(8,128)(2,1)S(1)}, u32[]{:S(2)}, u32[]{:S(2)}) collective-permute-start(bf16[16,48,384]{2,1,0:T(8,128)(2,1)S(1)} %all-to-all-done.refs_0_), channel_id=1, source_target_pairs={{0,4},{4,8},{8,12},{12,0},{1,5},{5,9},{9,13},{13,1},{2,6},{6,10},{... | collective-permute-start | bytes 1769480 | tf_op jit(solution)/shard_map/ppermute | solution.py:400
  23.9 22.8 %all-to-all-start.2 = ((bf16[16,288,128]{2,1,0:T(8,128)(2,1)}), bf16[16,288,128]{2,1,0:T(8,128)(2,1)S(1)}, u32[]{:S(2)}, u32[]{:S(2)}) async-start(bf16[16,288,128]{2,1,0:T(8,128)(2,1)} %pack.3), calls=%async_computation.2 | async-start | bytes 2359296 | tf_op jit(solution)/shard_map/all_to_all | solution.py:432
  33.8 12.8 %copy-start.10 = (bf16[16,48,384]{2,1,0:T(8,128)(2,1)}, bf16[16,48,384]{2,1,0:T(8,128)(2,1)S(1)}, u32[]{:S(2)}) copy-start(bf16[16,48,384]{2,1,0:T(8,128)(2,1)S(1)} %collective-permute-done.1.refs_2_) | copy-start | bytes 1769476
  33.8 7.4 %collective-permute-start.3 = (bf16[8,48,384]{2,1,0:T(8,128)(2,1)S(1)}, bf16[8,48,384]{2,1,0:T(8,128)(2,1)S(1)}, u32[]{:S(2)}, u32[]{:S(2)}) collective-permute-start(bf16[8,48,384]{2,1,0:T(8,128)(2,1)S(1)} %slice.75), channel_id=1, source_target_pairs={{0,12},{4,0},{8,4},{12,8},{1,13},{5,1},{9,5},{13,9},{2,14},{6,2},{... | collective-permute-start | bytes 884744 | tf_op jit(solution)/shard_map/ppermute | solution.py:402
  35.1 11.6 %copy-start.11 = (bf16[16,48,384]{2,1,0:T(8,128)(2,1)}, bf16[16,48,384]{2,1,0:T(8,128)(2,1)S(1)}, u32[]{:S(2)}) copy-start(bf16[16,48,384]{2,1,0:T(8,128)(2,1)S(1)} %collective-permute-done.refs_1_) | copy-start | bytes 1769476
  35.1 8.8 %collective-permute-start.2 = (bf16[8,48,384]{2,1,0:T(8,128)(2,1)S(1)}, bf16[8,48,384]{2,1,0:T(8,128)(2,1)}, u32[]{:S(2)}, u32[]{:S(2)}) collective-permute-start(bf16[8,48,384]{2,1,0:T(8,128)(2,1)S(1)} %slice.74), channel_id=1, source_target_pairs={{0,4},{4,8},{8,12},{12,0},{1,5},{5,9},{9,13},{13,1},{2,6},{6,10},{... | collective-permute-start | bytes 884744 | tf_op jit(solution)/shard_map/ppermute | solution.py:402
  36.1 10.6 %collective-permute-start.4 = (bf16[16,48,384]{2,1,0:T(8,128)(2,1)S(1)}, bf16[16,48,384]{2,1,0:T(8,128)(2,1)}, u32[]{:S(2)}, u32[]{:S(2)}) collective-permute-start(bf16[16,48,384]{2,1,0:T(8,128)(2,1)S(1)} %all-to-all-done.refs_0_), channel_id=1, source_target_pairs={{0,16},{16,0},{32,48},{48,32},{64,80},{80,64},{96,112},{112,96},{1... | collective-permute-start | bytes 1769480 | tf_op jit(solution)/shard_map/ppermute | solution.py:405
  36.1 10.6 %collective-permute-start.6 = (bf16[16,48,384]{2,1,0:T(8,128)(2,1)S(1)}, bf16[16,48,384]{2,1,0:T(8,128)(2,1)}, u32[]{:S(2)}, u32[]{:S(2)}) collective-permute-start(bf16[16,48,384]{2,1,0:T(8,128)(2,1)S(1)} %collective-permute-done.1.refs_2_), channel_id=1, source_target_pairs={{0,16},{16,0},{32,48},{48,32},{64,80},{80,64},{96,112},{112,96},{1... | collective-permute-start | bytes 1769480 | tf_op jit(solution)/shard_map/ppermute | solution.py:405
  36.6 10.1 %collective-permute-start.5 = (bf16[16,48,384]{2,1,0:T(8,128)(2,1)S(1)}, bf16[16,48,384]{2,1,0:T(8,128)(2,1)}, u32[]{:S(2)}, u32[]{:S(2)}) collective-permute-start(bf16[16,48,384]{2,1,0:T(8,128)(2,1)S(1)} %collective-permute-done.refs_1_), channel_id=1, source_target_pairs={{0,16},{16,0},{32,48},{48,32},{64,80},{80,64},{96,112},{112,96},{1... | collective-permute-start | bytes 1769480 | tf_op jit(solution)/shard_map/ppermute | solution.py:405
  41.2 5.4 %copy-start.13 = (bf16[8,48,384]{2,1,0:T(8,128)(2,1)}, bf16[8,48,384]{2,1,0:T(8,128)(2,1)S(1)}, u32[]{:S(2)}) copy-start(bf16[8,48,384]{2,1,0:T(8,128)(2,1)S(1)} %collective-permute-done.3.refs_4_) | copy-start | bytes 884740
  41.2 5.4 %collective-permute-start.8 = (bf16[8,48,384]{2,1,0:T(8,128)(2,1)S(1)}, bf16[8,48,384]{2,1,0:T(8,128)(2,1)S(1)}, u32[]{:S(2)}, u32[]{:S(2)}) collective-permute-start(bf16[8,48,384]{2,1,0:T(8,128)(2,1)S(1)} %collective-permute-done.3.refs_4_), channel_id=1, source_target_pairs={{0,16},{16,0},{32,48},{48,32},{64,80},{80,64},{96,112},{112,96},{1... | collective-permute-start | bytes 884744 | tf_op jit(solution)/shard_map/ppermute | solution.py:405
  44.0 2.7 %collective-permute-start.7 = (bf16[8,48,384]{2,1,0:T(8,128)(2,1)}, bf16[8,48,384]{2,1,0:T(8,128)(2,1)S(1)}, u32[]{:S(2)}, u32[]{:S(2)}) collective-permute-start(bf16[8,48,384]{2,1,0:T(8,128)(2,1)} %collective-permute-done.2.refs_3_), channel_id=1, source_target_pairs={{0,16},{16,0},{32,48},{48,32},{64,80},{80,64},{96,112},{112,96},{1... | collective-permute-start | bytes 884744 | tf_op jit(solution)/shard_map/ppermute | solution.py:405
  46.6 5.4 %copy-start.12 = (f32[768]{0:T(1024)S(1)}, f32[768]{0:T(1024)}, u32[]{:S(2)}) copy-start(f32[768]{0:T(1024)} %param.15) | copy-start | bytes 9220
  46.7 5.9 %copy-start.7 = (bf16[16,288,128]{2,1,0:T(8,128)(2,1)}, bf16[16,288,128]{2,1,0:T(8,128)(2,1)S(1)}, u32[]{:S(2)}) copy-start(bf16[16,288,128]{2,1,0:T(8,128)(2,1)S(1)} %all-to-all-done.2.x_ref) | copy-start | bytes 3538948
  47.5 29.2 %all-to-all-start.1 = ((bf16[16,288,128]{2,1,0:T(8,128)(2,1)}), bf16[16,288,128]{2,1,0:T(8,128)(2,1)S(1)}, u32[]{:S(2)}, u32[]{:S(2)}) async-start(bf16[16,288,128]{2,1,0:T(8,128)(2,1)} %pack.2), calls=%async_computation.1 | async-start | bytes 2359296 | tf_op jit(solution)/shard_map/all_to_all | solution.py:432
  60.4 33.2 %collective-permute-start.12 = (bf16[4,48,768]{2,1,0:T(8,128)(2,1)}, bf16[4,48,768]{2,1,0:T(8,128)(2,1)S(1)}, u32[]{:S(2)}, u32[]{:S(2)}) collective-permute-start(bf16[4,48,768]{2,1,0:T(8,128)(2,1)} %get-tuple-element.53.own0_ref), channel_id=1, source_target_pairs={{1,0},{2,1},{3,2},{4,3},{5,4},{6,5},{7,6},{8,7},{9,8},{10,9},{11,1... | collective-permute-start | bytes 884744 | tf_op jit(solution)/shard_map/ppermute | solution.py:440
  70.1 23.5 %collective-permute-start.11 = (bf16[4,48,768]{2,1,0:T(8,128)(2,1)}, bf16[4,48,768]{2,1,0:T(8,128)(2,1)S(1)}, u32[]{:S(2)}, u32[]{:S(2)}) collective-permute-start(bf16[4,48,768]{2,1,0:T(8,128)(2,1)} %get-tuple-element.53.own0_ref), channel_id=1, source_target_pairs={{0,1},{1,2},{2,3},{3,4},{4,5},{5,6},{6,7},{7,8},{8,9},{9,10},{10,1... | collective-permute-start | bytes 884744 | tf_op jit(solution)/shard_map/ppermute | solution.py:439
  77.8 20.8 %copy-start = (bf16[4,48,768]{2,1,0:T(8,128)(2,1)S(1)}, bf16[4,48,768]{2,1,0:T(8,128)(2,1)}, u32[]{:S(2)}) copy-start(bf16[4,48,768]{2,1,0:T(8,128)(2,1)} %get-tuple-element.53.own0_ref) | copy-start | bytes 884740
  77.8 20.8 %copy-start.2 = (bf16[768,2304]{1,0:T(8,128)(2,1)S(1)}, bf16[768,2304]{1,0:T(8,128)(2,1)}, u32[]{:S(2)}) copy-start(bf16[768,2304]{1,0:T(8,128)(2,1)} %w_ref.5) | copy-start | bytes 10616836
  86.8 15.2 %collective-permute-start.10 = (bf16[4,48,768]{2,1,0:T(8,128)(2,1)}, bf16[4,48,768]{2,1,0:T(8,128)(2,1)S(1)}, u32[]{:S(2)}, u32[]{:S(2)}) collective-permute-start(bf16[4,48,768]{2,1,0:T(8,128)(2,1)} %get-tuple-element.54.own1_ref), channel_id=1, source_target_pairs={{1,0},{2,1},{3,2},{4,3},{5,4},{6,5},{7,6},{8,7},{9,8},{10,9},{11,1... | collective-permute-start | bytes 884744 | tf_op jit(solution)/shard_map/ppermute | solution.py:440
  90.3 17.8 %collective-permute-start.9 = (bf16[4,48,768]{2,1,0:T(8,128)(2,1)}, bf16[4,48,768]{2,1,0:T(8,128)(2,1)S(1)}, u32[]{:S(2)}, u32[]{:S(2)}) collective-permute-start(bf16[4,48,768]{2,1,0:T(8,128)(2,1)} %get-tuple-element.54.own1_ref), channel_id=1, source_target_pairs={{0,1},{1,2},{2,3},{3,4},{4,5},{5,6},{6,7},{7,8},{8,9},{9,10},{10,1... | collective-permute-start | bytes 884744 | tf_op jit(solution)/shard_map/ppermute | solution.py:439
  94.5 19.2 %collective-permute-start.13 = (bf16[16,8,768]{2,1,0:T(8,128)(2,1)S(1)}, bf16[16,8,768]{2,1,0:T(8,128)(2,1)S(1)}, u32[]{:S(2)}, u32[]{:S(2)}) collective-permute-start(bf16[16,8,768]{2,1,0:T(8,128)(2,1)S(1)} %pad_maximum_fusion), channel_id=1, source_target_pairs={{0,16},{16,32},{32,48},{48,64},{64,80},{80,96},{96,112},{112,128},... | collective-permute-start | bytes 589832 | tf_op jit(solution)/shard_map/ppermute | solution.py:443
  94.7 19.1 %collective-permute-start.14 = (bf16[16,8,768]{2,1,0:T(8,128)(2,1)S(1)}, bf16[16,8,768]{2,1,0:T(8,128)(2,1)S(1)}, u32[]{:S(2)}, u32[]{:S(2)}) collective-permute-start(bf16[16,8,768]{2,1,0:T(8,128)(2,1)S(1)} %pad_maximum_fusion.1), channel_id=1, source_target_pairs={{16,0},{32,16},{48,32},{64,48},{80,64},{96,80},{112,96},{128,112},... | collective-permute-start | bytes 589832 | tf_op jit(solution)/shard_map/ppermute | solution.py:444
  99.5 14.2 %copy-start.3 = (bf16[768,768]{1,0:T(8,128)(2,1)S(1)}, bf16[768,768]{1,0:T(8,128)(2,1)}, u32[]{:S(2)}) copy-start(bf16[768,768]{1,0:T(8,128)(2,1)} %wout_ref.3) | copy-start | bytes 3538948
  99.5 14.2 %copy-start.4 = (s32[128]{0:T(128)S(1)}, s32[128]{0:T(128)}, u32[]{:S(2)}) copy-start(s32[128]{0:T(128)} %start_ref.3) | copy-start | bytes 1540
  99.5 14.2 %copy-start.5 = (bf16[4,48,768]{2,1,0:T(8,128)(2,1)S(1)}, bf16[4,48,768]{2,1,0:T(8,128)(2,1)}, u32[]{:S(2)}) copy-start(bf16[4,48,768]{2,1,0:T(8,128)(2,1)} %get-tuple-element.62.emb0_ref) | copy-start | bytes 884740
  99.5 14.2 %copy-start.6 = (bf16[4,48,768]{2,1,0:T(8,128)(2,1)S(1)}, bf16[4,48,768]{2,1,0:T(8,128)(2,1)}, u32[]{:S(2)}) copy-start(bf16[4,48,768]{2,1,0:T(8,128)(2,1)} %get-tuple-element.63.emb1_ref) | copy-start | bytes 884740
  108.2 9.8 %collective-permute-start.15 = (bf16[8,8,768]{2,1,0:T(8,128)(2,1)S(1)}, bf16[8,8,768]{2,1,0:T(8,128)(2,1)S(1)}, u32[]{:S(2)}, u32[]{:S(2)}) collective-permute-start(bf16[8,8,768]{2,1,0:T(8,128)(2,1)S(1)} %pad_maximum_fusion.2), channel_id=1, source_target_pairs={{0,16},{16,32},{32,48},{48,64},{64,80},{80,96},{96,112},{112,128},... | collective-permute-start | bytes 294920 | tf_op jit(solution)/shard_map/ppermute | solution.py:443
  108.3 9.7 %collective-permute-start.16 = (bf16[8,8,768]{2,1,0:T(8,128)(2,1)S(1)}, bf16[8,8,768]{2,1,0:T(8,128)(2,1)S(1)}, u32[]{:S(2)}, u32[]{:S(2)}) collective-permute-start(bf16[8,8,768]{2,1,0:T(8,128)(2,1)S(1)} %pad_maximum_fusion.3), channel_id=1, source_target_pairs={{16,0},{32,16},{48,32},{64,48},{80,64},{96,80},{112,96},{128,112},... | collective-permute-start | bytes 294920 | tf_op jit(solution)/shard_map/ppermute | solution.py:444
  (4 other events, 3.5 us)

commit v4 on v2

--- a/solution.py
+++ b/solution.py
@@ -19,7 +19,9 @@
 SOURCES = 4
 MASKED = -1e30
 PART = 256
-EMBED_LIMIT = 50
+SPLIT_FLOPS = 18e9
+FIRST_LIMIT = 56
+NEXT_LIMIT = 50
 LIMIT = 36
 
 
@@ -181,10 +183,10 @@
     ]
     far = pl.BlockSpec(memory_space=pl.ANY)
     common = dict(
-        compiler_params=params(EMBED_LIMIT),
+        compiler_params=params(FIRST_LIMIT if len(w_all) > 1 else NEXT_LIMIT),
         cost_estimate=cost(2 * tokens * depth * width * groups, depth * width * 2 + tokens * depth * 2),
     )
-    shared = (moved, pick, bias, gain, norm_gain[None, :])
+    shared = (moved, pick, bias, gain, norm_gain)
     if len(w_all) > 1:
         return pl.pallas_call(
             embed_first_kernel,
@@ -393,12 +395,32 @@
     return lax.all_to_all(sent, "lev", split_axis=0, concat_axis=0, tiled=True)
 
 
+def split_kernel(up_ref, down_ref, first_ref, second_ref):
+    first_ref[...] = up_ref[...]
+    second_ref[...] = down_ref[...]
+
+
+def split(from_up, from_down):
+    lev, size, half = from_up.shape
+    block = (lev // 2, size, half)
+    return pl.pallas_call(
+        split_kernel,
+        grid=(1,),
+        in_specs=[pl.BlockSpec(block, lambda i: (0, 0, 0)), pl.BlockSpec(block, lambda i: (1, 0, 0))],
+        out_specs=[pl.BlockSpec(block, lambda i: (0, 0, 0))] * 2,
+        out_shape=[jax.ShapeDtypeStruct(block, from_up.dtype)] * 2,
+        compiler_params=params(LIMIT),
+        cost_estimate=cost(SPLIT_FLOPS, 4 * from_up.size),
+        name="split",
+    )(from_up, from_down)
+
+
 def weight_pieces(own, lat):
     stride = lat // PLANES
     up, down = ring(PLANES, stride, 1), ring(PLANES, stride, -1)
     near = [lax.ppermute(own, "lat", up), lax.ppermute(own, "lat", down)]
-    half = own.shape[0] // 2
-    far = [lax.ppermute(near[0][:half], "lat", up), lax.ppermute(near[1][half:], "lat", down)]
+    first, second = split(*near)
+    far = [lax.ppermute(first, "lat", up), lax.ppermute(second, "lat", down)]
     pieces = [own] + near + far
     swap = [(i, i ^ 1) for i in range(own.shape[0])]
     return pieces + [lax.ppermute(piece, "lev", swap) for piece in pieces]
@@ -421,8 +443,9 @@
     right_way = [(i, (i + 1) % lev) for i in range(lev)]
     left_way = [(b, a) for a, b in right_way]
 
-    later, own, pick, place = lax.optimization_barrier((turned, own, pick, place))
-    packed = [pack(later if c == 0 else turned, lev, c) for c in range(rows // CHUNK)]
+    packed = [pack(turned, lev, c) for c in range(rows // CHUNK)]
+    norm_gain = norm_gain[None, :]
+    *packed, own, pick, place, norm_gain = lax.optimization_barrier((*packed, own, pick, place, norm_gain))
     w_all = weight_pieces(own, lat)
     emb, normed, low, high = [], [], [], []
     for c in range(rows // CHUNK):

time: 135 us -> 124 us (0.919)
  waiting for transfers between devices: 44.3 us -> 33.9 us
  local copies, waits for them, and re-layouts: 8.65 us -> 6.09 us
  Pallas kernels: 31.8 us -> 33.6 us
    all_to_all x1, waiting for transfers between devices: 10.4 us -> 4 us  [quarter_of_weights(): return lax.all_to_all(sent, 'lev', split_axis=0, concat_axis=0, tiled=True)]
    ppermute x2, waiting for transfers between devices: 14.7 us -> 9.82 us  [weight_pieces(): near = [lax.ppermute(own, 'lat', up), lax.ppermute(own, 'lat', down)]]
    unnamed x28 -> x44, local copies, waits for them, and re-layouts: 4.41 us -> 2.6 us
    all_to_all x2, starting transfers between devices: 9.21 us -> 7.54 us  [per_device(): lax.all_to_all(packed[c], 'lev', split_axis=0, concat_axis=0, tiled=True)]
    slice x2 -> x0, local copies, waits for them, and re-layouts: 1.5 us -> none  [the longest x1 0.76 us: weight_pieces(): near[1][half:]]
    ppermute x2, starting transfers between devices: 15.2 us -> 16.6 us  [per_device(): high.append(lax.ppermute(n, 'lat', down))]
  transfers between devices with their start and end apart: 20 -> 20, of which waited for: 10 -> 10; matrix products, arithmetic and copies ran while one was open for 2% -> 3% of each run, Pallas kernels for 17% -> 22%
where the time goes in v4:
time: 124 us; the launch traced here: 123 us
  starting transfers between devices  48.1 us (39%)
  waiting for transfers between devices  33.9 us (27%)
  Pallas kernels  33.6 us (27%)
  local copies, waits for them, and re-layouts  6.09 us (5%)
  other arithmetic  1.29 us (1%)
    ppermute x2, starting transfers between devices, per_device(): high.append(lax.ppermute(n, 'lat', down))  16.6 us
    ppermute x2, waiting for transfers between devices, weight_pieces(): near = [lax.ppermute(own, 'lat', up), lax.ppermute(own, 'lat', down)]  9.82 us
    ppermute x2, waiting for transfers between devices, per_device(): low.append(lax.ppermute(n, 'lat', up))  8.98 us
    ppermute x2, starting transfers between devices, strips(): lax.ppermute(jnp.concatenate([t[:, :STRIP] for t in tall], axis=0), 'lev'...  8.05 us
    pallas_call x1, Pallas kernels, embed(): pl.pallas_call(embed_first_kernel, in_specs=[smem()] + [vmem()] * 5 + [fa...  7.82 us
    all_to_all x2, starting transfers between devices, per_device(): lax.all_to_all(packed[c], 'lev', split_axis=0, concat_axis=0, tiled=True)  7.54 us
    ppermute x2, waiting for transfers between devices, weight_pieces(): far = [lax.ppermute(first, 'lat', up), lax.ppermute(second, 'lat', down)]  7.07 us
    pallas_call x1, Pallas kernels, embed(): pl.pallas_call(embed_next_kernel, in_specs=[vmem()] * 5 + [far], out_spec...  7 us
  transfers between devices with their start and end apart: 20, of which 10 were waited for; matrix products, arithmetic and copies ran while one was open for 3% of the time, Pallas kernels for 22%

profile of v4, /device:TPU:2, one launch (start us, length us, event | category | flops | bytes accessed | tf_op | source)
XLA Modules:
  0.0 123.4 jit_solution(15301116298728574744)
XLA Ops:
  0.0 0.8 dynamic-slice_bitcast_fusion.1
  0.8 0.9 broadcast_in_dim.17
  1.7 5.9 %all-to-all-start = ((bf16[16,48,384]{2,1,0:T(8,128)(2,1)}), bf16[16,48,384]{2,1,0:T(8,128)(2,1)S(1)}, u32[]{:S(2)}, u32[]{:S(2)}) async-start(bf16[16,48,384]{2,1,0:T(8,128)(2,1)} %bitcast.4), calls=%async_computation | async-start | bytes 1179648 | tf_op jit(solution)/shard_map/all_to_all | solution.py:395
  7.6 2.7 %pack.3 = bf16[16,288,128]{2,1,0:T(8,128)(2,1)} custom-call(bf16[8,192,768]{2,1,0:T(8,128)(2,1)} %bitcast.16), custom_call_target="tpu_custom_call" | custom-call | bytes 2359296 | tf_op jit(solution)/shard_map/pack/pallas_call | solution.py:64
  10.3 2.7 %pack.2 = bf16[16,288,128]{2,1,0:T(8,128)(2,1)} custom-call(bf16[8,192,768]{2,1,0:T(8,128)(2,1)} %bitcast.17), custom_call_target="tpu_custom_call" | custom-call | bytes 2359296 | tf_op jit(solution)/shard_map/pack/pallas_call | solution.py:64
  15.2 4.0 %all-to-all-done.refs_0_ = bf16[16,48,384]{2,1,0:T(8,128)(2,1)S(1)} async-done(((bf16[16,48,384]{2,1,0:T(8,128)(2,1)}), bf16[16,48,384]{2,1,0:T(8,128)(2,1)S(1)}, u32[]{:S(2)}, u32[]{:S(2)}) %all-to-all-start) | async-done | bytes 589856 | tf_op jit(solution)/shard_map/all_to_all | solution.py:395
  19.8 1.5 %collective-permute-start = (bf16[16,48,384]{2,1,0:T(8,128)(2,1)S(1)}, bf16[16,48,384]{2,1,0:T(8,128)(2,1)S(1)}, u32[]{:S(2)}, u32[]{:S(2)}) collective-permute-start(bf16[16,48,384]{2,1,0:T(8,128)(2,1)S(1)} %all-to-all-done.refs_0_), channel_id=1, source_target_pairs={{0,4},{4,8},{8,12},{12,0},{1,5},{5,9},{9,13},{13,1},{2,6},{6,10},{... | collective-permute-start | bytes 1769480 | tf_op jit(solution)/shard_map/ppermute | solution.py:421
  21.2 3.7 %all-to-all-start.2 = ((bf16[16,288,128]{2,1,0:T(8,128)(2,1)}), bf16[16,288,128]{2,1,0:T(8,128)(2,1)S(1)}, u32[]{:S(2)}, u32[]{:S(2)}) async-start(bf16[16,288,128]{2,1,0:T(8,128)(2,1)} %pack.2), calls=%async_computation.2 | async-start | bytes 2359296 | tf_op jit(solution)/shard_map/all_to_all | solution.py:454
  25.2 8.6 %collective-permute-done.1.down_ref.refs_2_ = bf16[16,48,384]{2,1,0:T(8,128)(2,1)S(1)} collective-permute-done((bf16[16,48,384]{2,1,0:T(8,128)(2,1)S(1)}, bf16[16,48,384]{2,1,0:T(8,128)(2,1)S(1)}, u32[]{:S(2)}, u32[]{:S(2)}) %collective-permute-start.1) | collective-permute-done | bytes 589856 | tf_op jit(solution)/shard_map/ppermute | solution.py:421
  33.8 1.3 %collective-permute-done.up_ref.refs_1_ = bf16[16,48,384]{2,1,0:T(8,128)(2,1)S(1)} collective-permute-done((bf16[16,48,384]{2,1,0:T(8,128)(2,1)S(1)}, bf16[16,48,384]{2,1,0:T(8,128)(2,1)S(1)}, u32[]{:S(2)}, u32[]{:S(2)}) %collective-permute-start) | collective-permute-done | bytes 589856 | tf_op jit(solution)/shard_map/ppermute | solution.py:421
  35.1 0.8 copy-done.6
  36.4 2.5 %collective-permute-start.3 = (bf16[8,48,384]{2,1,0:T(8,128)(2,1)S(1)}, bf16[8,48,384]{2,1,0:T(8,128)(2,1)S(1)}, u32[]{:S(2)}, u32[]{:S(2)}) collective-permute-start(bf16[8,48,384]{2,1,0:T(8,128)(2,1)S(1)} %get-tuple-element.40), channel_id=1, source_target_pairs={{0,12},{4,0},{8,4},{12,8},{1,13},{5,1},{9,5},{13,9},{2,14},{6,2},{... | collective-permute-start | bytes 884744 | tf_op jit(solution)/shard_map/ppermute | solution.py:423
  38.9 7.0 %collective-permute-done.2.refs_3_ = bf16[8,48,384]{2,1,0:T(8,128)(2,1)S(1)} collective-permute-done((bf16[8,48,384]{2,1,0:T(8,128)(2,1)S(1)}, bf16[8,48,384]{2,1,0:T(8,128)(2,1)S(1)}, u32[]{:S(2)}, u32[]{:S(2)}) %collective-permute-start.2) | collective-permute-done | bytes 294944 | tf_op jit(solution)/shard_map/ppermute | solution.py:423
  46.0 0.7 copy-done.18
  46.7 0.8 copy-done.16
  47.6 3.8 %all-to-all-start.1 = ((bf16[16,288,128]{2,1,0:T(8,128)(2,1)}), bf16[16,288,128]{2,1,0:T(8,128)(2,1)S(1)}, u32[]{:S(2)}, u32[]{:S(2)}) async-start(bf16[16,288,128]{2,1,0:T(8,128)(2,1)} %pack.3), calls=%async_computation.1 | async-start | bytes 2359296 | tf_op jit(solution)/shard_map/all_to_all | solution.py:454
  52.0 1.1 collective-permute-done.7.refs_8_
  53.8 7.8 %embed_first.1 = (bf16[4,48,768]{2,1,0:T(8,128)(2,1)}, bf16[4,48,768]{2,1,0:T(8,128)(2,1)}, bf16[16,4,48,768]{3,2,1,0:T(8,128)(2,1)}) custom-call(s32[2]{0:T(128)} %pad_add_fusion.1.place_ref, bf16[16,288,128]{2,1,0:T(8,128)(2,1)} %copy-done.11, bf16[3,3072]{1,0:T(4,128)(2,1)} %fusion.pick_ref, f32[3,768]{1,0:T(4,128)} %bias_ref.3, f32[3,768]{1,0:T(4,128)} %gain_ref.3, ...), custom_call_target="tpu_custom_call" | custom-call | flops 2717908992 | bytes 5898240 | tf_op jit(solution)/shard_map/embed_first/pallas_call | solution.py:191
  61.6 9.6 %collective-permute-start.12 = (bf16[4,48,768]{2,1,0:T(8,128)(2,1)}, bf16[4,48,768]{2,1,0:T(8,128)(2,1)S(1)}, u32[]{:S(2)}, u32[]{:S(2)}) collective-permute-start(bf16[4,48,768]{2,1,0:T(8,128)(2,1)} %get-tuple-element.55.own0_ref), channel_id=1, source_target_pairs={{1,0},{2,1},{3,2},{4,3},{5,4},{6,5},{7,6},{8,7},{9,8},{10,9},{11,1... | collective-permute-start | bytes 884744 | tf_op jit(solution)/shard_map/ppermute | solution.py:462
  71.3 2.1 %collective-permute-start.11 = (bf16[4,48,768]{2,1,0:T(8,128)(2,1)}, bf16[4,48,768]{2,1,0:T(8,128)(2,1)S(1)}, u32[]{:S(2)}, u32[]{:S(2)}) collective-permute-start(bf16[4,48,768]{2,1,0:T(8,128)(2,1)} %get-tuple-element.55.own0_ref), channel_id=1, source_target_pairs={{0,1},{1,2},{2,3},{3,4},{4,5},{5,6},{6,7},{7,8},{8,9},{9,10},{10,1... | collective-permute-start | bytes 884744 | tf_op jit(solution)/shard_map/ppermute | solution.py:461
  73.4 0.8 fusion.4
  74.3 7.0 %embed_next.1 = (bf16[4,48,768]{2,1,0:T(8,128)(2,1)S(1)}, bf16[4,48,768]{2,1,0:T(8,128)(2,1)S(1)}) custom-call(bf16[16,288,128]{2,1,0:T(8,128)(2,1)S(1)} %all-to-all-done.1.x_ref, bf16[3,3072]{1,0:T(4,128)(2,1)S(1)} %copy-done.1, f32[3,768]{1,0:T(4,128)S(1)} %copy-done.7, f32[3,768]{1,0:T(4,128)S(1)} %copy-done.8, f32[1,768]{1,0:T(1,128)S(1)} %copy-done.2, ...), custom_call_target="tpu_custom_call" | custom-call | flops 2717908992 | bytes 5898240 | tf_op jit(solution)/shard_map/embed_next/pallas_call | solution.py:201
  81.3 6.9 %collective-permute-start.10 = (bf16[4,48,768]{2,1,0:T(8,128)(2,1)S(1)}, bf16[4,48,768]{2,1,0:T(8,128)(2,1)S(1)}, u32[]{:S(2)}, u32[]{:S(2)}) collective-permute-start(bf16[4,48,768]{2,1,0:T(8,128)(2,1)S(1)} %get-tuple-element.56.own1_ref), channel_id=1, source_target_pairs={{1,0},{2,1},{3,2},{4,3},{5,4},{6,5},{7,6},{8,7},{9,8},{10,9},{11,1... | collective-permute-start | bytes 884744 | tf_op jit(solution)/shard_map/ppermute | solution.py:462
  88.2 1.9 %collective-permute-start.9 = (bf16[4,48,768]{2,1,0:T(8,128)(2,1)S(1)}, bf16[4,48,768]{2,1,0:T(8,128)(2,1)S(1)}, u32[]{:S(2)}, u32[]{:S(2)}) collective-permute-start(bf16[4,48,768]{2,1,0:T(8,128)(2,1)S(1)} %get-tuple-element.56.own1_ref), channel_id=1, source_target_pairs={{0,1},{1,2},{2,3},{3,4},{4,5},{5,6},{6,7},{7,8},{8,9},{9,10},{10,1... | collective-permute-start | bytes 884744 | tf_op jit(solution)/shard_map/ppermute | solution.py:461
  90.2 1.4 %collective-permute-done.11.low_ref = bf16[4,48,768]{2,1,0:T(8,128)(2,1)S(1)} collective-permute-done((bf16[4,48,768]{2,1,0:T(8,128)(2,1)}, bf16[4,48,768]{2,1,0:T(8,128)(2,1)S(1)}, u32[]{:S(2)}, u32[]{:S(2)}) %collective-permute-start.11) | collective-permute-done | bytes 294944 | tf_op jit(solution)/shard_map/ppermute | solution.py:461
  91.8 3.9 %collective-permute-start.14 = (bf16[16,8,768]{2,1,0:T(8,128)(2,1)S(1)}, bf16[16,8,768]{2,1,0:T(8,128)(2,1)S(1)}, u32[]{:S(2)}, u32[]{:S(2)}) collective-permute-start(bf16[16,8,768]{2,1,0:T(8,128)(2,1)S(1)} %pad_maximum_fusion.1), channel_id=1, source_target_pairs={{16,0},{32,16},{48,32},{64,48},{80,64},{96,80},{112,96},{128,112},... | collective-permute-start | bytes 589832 | tf_op jit(solution)/shard_map/ppermute | solution.py:466
  95.7 2.5 %project.1 = (bf16[3,128,768]{2,1,0:T(8,128)(2,1)S(1)}, bf16[24,64,1536]{2,1,0:T(8,128)(2,1)S(1)}) custom-call(bf16[4,48,768]{2,1,0:T(8,128)(2,1)S(1)} %copy-done, bf16[4,48,768]{2,1,0:T(8,128)(2,1)S(1)} %get-tuple-element.56.own1_ref, bf16[4,48,768]{2,1,0:T(8,128)(2,1)S(1)} %collective-permute-done.11.low_ref, ...), custom_call_target="tpu_custom_call" | custom-call | flops 2264924160 | bytes 7077888 | tf_op jit(solution)/shard_map/project/pallas_call | solution.py:248
  98.2 2.4 %collective-permute-done.10.high_ref = bf16[4,48,768]{2,1,0:T(8,128)(2,1)S(1)} collective-permute-done((bf16[4,48,768]{2,1,0:T(8,128)(2,1)S(1)}, bf16[4,48,768]{2,1,0:T(8,128)(2,1)S(1)}, u32[]{:S(2)}, u32[]{:S(2)}) %collective-permute-start.10) | collective-permute-done | bytes 294944 | tf_op jit(solution)/shard_map/ppermute | solution.py:462
  100.6 7.6 %collective-permute-done.9.low_ref = bf16[4,48,768]{2,1,0:T(8,128)(2,1)S(1)} collective-permute-done((bf16[4,48,768]{2,1,0:T(8,128)(2,1)S(1)}, bf16[4,48,768]{2,1,0:T(8,128)(2,1)S(1)}, u32[]{:S(2)}, u32[]{:S(2)}) %collective-permute-start.9) | collective-permute-done | bytes 294944 | tf_op jit(solution)/shard_map/ppermute | solution.py:461
  108.4 4.1 %collective-permute-start.16 = (bf16[8,8,768]{2,1,0:T(8,128)(2,1)S(1)}, bf16[8,8,768]{2,1,0:T(8,128)(2,1)S(1)}, u32[]{:S(2)}, u32[]{:S(2)}) collective-permute-start(bf16[8,8,768]{2,1,0:T(8,128)(2,1)S(1)} %pad_maximum_fusion.3), channel_id=1, source_target_pairs={{16,0},{32,16},{48,32},{64,48},{80,64},{96,80},{112,96},{128,112},... | collective-permute-start | bytes 294920 | tf_op jit(solution)/shard_map/ppermute | solution.py:466
  112.6 4.3 %middle.1 = (bf16[24,64,1536]{2,1,0:T(8,128)(2,1)S(1)}, bf16[8,16,768]{2,1,0:T(8,128)(2,1)S(1)}) custom-call(s32[128]{0:T(128)S(1)} %copy-done.9, s32[1]{0:T(128)} %bitcast.first_ref, bf16[3,128,768]{2,1,0:T(8,128)(2,1)S(1)} %get-tuple-element.60.q_ref, bf16[24,64,1536]{2,1,0:T(8,128)(2,1)S(1)} %get-tuple-element.61._, ...), custom_call_target="tpu_custom_call", output_to_operand_aliasing={{0}: (3, {})} | custom-call | flops 8000000000 | bytes 10000000 | tf_op jit(solution)/shard_map/middle/pallas_call | solution.py:333
  116.9 6.5 %sides.1 = (bf16[8,48,768]{2,1,0:T(8,128)(2,1)}, bf16[24,64,1536]{2,1,0:T(8,128)(2,1)S(1)}) custom-call(s32[128]{0:T(128)S(1)} %copy-done.9, s32[1]{0:T(128)} %bitcast.first_ref, bf16[3,128,768]{2,1,0:T(8,128)(2,1)S(1)} %get-tuple-element.60.q_ref, bf16[24,64,1536]{2,1,0:T(8,128)(2,1)S(1)} %get-tuple-element.66._, ...), custom_call_target="tpu_custom_call", output_to_operand_aliasing={{1}: (3, {})} | custom-call | flops 8999999488 | bytes 10000000 | tf_op jit(solution)/shard_map/sides/pallas_call | solution.py:369
  (81 shorter events, 5.3 us)
Async XLA Ops:
  1.7 17.5 %all-to-all-start = ((bf16[16,48,384]{2,1,0:T(8,128)(2,1)}), bf16[16,48,384]{2,1,0:T(8,128)(2,1)S(1)}, u32[]{:S(2)}, u32[]{:S(2)}) async-start(bf16[16,48,384]{2,1,0:T(8,128)(2,1)} %bitcast.4), calls=%async_computation | async-start | bytes 1179648 | tf_op jit(solution)/shard_map/all_to_all | solution.py:395
  19.2 15.9 %copy-start.12 = (bf16[16,48,384]{2,1,0:T(8,128)(2,1)}, bf16[16,48,384]{2,1,0:T(8,128)(2,1)S(1)}, u32[]{:S(2)}) copy-start(bf16[16,48,384]{2,1,0:T(8,128)(2,1)S(1)} %all-to-all-done.refs_0_) | copy-start | bytes 1769476
  19.2 14.6 %collective-permute-start.1 = (bf16[16,48,384]{2,1,0:T(8,128)(2,1)S(1)}, bf16[16,48,384]{2,1,0:T(8,128)(2,1)S(1)}, u32[]{:S(2)}, u32[]{:S(2)}) collective-permute-start(bf16[16,48,384]{2,1,0:T(8,128)(2,1)S(1)} %all-to-all-done.refs_0_), channel_id=1, source_target_pairs={{0,12},{4,0},{8,4},{12,8},{1,13},{5,1},{9,5},{13,9},{2,14},{6,2},{... | collective-permute-start | bytes 1769480 | tf_op jit(solution)/shard_map/ppermute | solution.py:421
  19.8 15.3 %collective-permute-start = (bf16[16,48,384]{2,1,0:T(8,128)(2,1)S(1)}, bf16[16,48,384]{2,1,0:T(8,128)(2,1)S(1)}, u32[]{:S(2)}, u32[]{:S(2)}) collective-permute-start(bf16[16,48,384]{2,1,0:T(8,128)(2,1)S(1)} %all-to-all-done.refs_0_), channel_id=1, source_target_pairs={{0,4},{4,8},{8,12},{12,0},{1,5},{5,9},{9,13},{13,1},{2,6},{6,10},{... | collective-permute-start | bytes 1769480 | tf_op jit(solution)/shard_map/ppermute | solution.py:421
  21.2 26.3 %all-to-all-start.2 = ((bf16[16,288,128]{2,1,0:T(8,128)(2,1)}), bf16[16,288,128]{2,1,0:T(8,128)(2,1)S(1)}, u32[]{:S(2)}, u32[]{:S(2)}) async-start(bf16[16,288,128]{2,1,0:T(8,128)(2,1)} %pack.2), calls=%async_computation.2 | async-start | bytes 2359296 | tf_op jit(solution)/shard_map/all_to_all | solution.py:454
  25.0 14.0 %collective-permute-start.4 = (bf16[16,48,384]{2,1,0:T(8,128)(2,1)S(1)}, bf16[16,48,384]{2,1,0:T(8,128)(2,1)S(1)}, u32[]{:S(2)}, u32[]{:S(2)}) collective-permute-start(bf16[16,48,384]{2,1,0:T(8,128)(2,1)S(1)} %all-to-all-done.refs_0_), channel_id=1, source_target_pairs={{0,16},{16,0},{32,48},{48,32},{64,80},{80,64},{96,112},{112,96},{1... | collective-permute-start | bytes 1769480 | tf_op jit(solution)/shard_map/ppermute | solution.py:426
  33.8 12.2 %collective-permute-start.6 = (bf16[16,48,384]{2,1,0:T(8,128)(2,1)S(1)}, bf16[16,48,384]{2,1,0:T(8,128)(2,1)S(1)}, u32[]{:S(2)}, u32[]{:S(2)}) collective-permute-start(bf16[16,48,384]{2,1,0:T(8,128)(2,1)S(1)} %collective-permute-done.1.down_ref.refs_2_), channel_id=1, source_target_pairs={{0,16},{16,0},{32,48},{48,32},{64,80},{80,64},{96,112},{112,96},{1... | collective-permute-start | bytes 1769480 | tf_op jit(solution)/shard_map/ppermute | solution.py:426
  35.1 12.5 %collective-permute-start.5 = (bf16[16,48,384]{2,1,0:T(8,128)(2,1)S(1)}, bf16[16,48,384]{2,1,0:T(8,128)(2,1)}, u32[]{:S(2)}, u32[]{:S(2)}) collective-permute-start(bf16[16,48,384]{2,1,0:T(8,128)(2,1)S(1)} %collective-permute-done.up_ref.refs_1_), channel_id=1, source_target_pairs={{0,16},{16,0},{32,48},{48,32},{64,80},{80,64},{96,112},{112,96},{1... | collective-permute-start | bytes 1769480 | tf_op jit(solution)/shard_map/ppermute | solution.py:426
  35.9 9.9 %collective-permute-start.2 = (bf16[8,48,384]{2,1,0:T(8,128)(2,1)S(1)}, bf16[8,48,384]{2,1,0:T(8,128)(2,1)S(1)}, u32[]{:S(2)}, u32[]{:S(2)}) collective-permute-start(bf16[8,48,384]{2,1,0:T(8,128)(2,1)S(1)} %get-tuple-element.39), channel_id=1, source_target_pairs={{0,4},{4,8},{8,12},{12,0},{1,5},{5,9},{9,13},{13,1},{2,6},{6,10},{... | collective-permute-start | bytes 884744 | tf_op jit(solution)/shard_map/ppermute | solution.py:423
  36.4 9.6 %collective-permute-start.3 = (bf16[8,48,384]{2,1,0:T(8,128)(2,1)S(1)}, bf16[8,48,384]{2,1,0:T(8,128)(2,1)S(1)}, u32[]{:S(2)}, u32[]{:S(2)}) collective-permute-start(bf16[8,48,384]{2,1,0:T(8,128)(2,1)S(1)} %get-tuple-element.40), channel_id=1, source_target_pairs={{0,12},{4,0},{8,4},{12,8},{1,13},{5,1},{9,5},{13,9},{2,14},{6,2},{... | collective-permute-start | bytes 884744 | tf_op jit(solution)/shard_map/ppermute | solution.py:423
  38.9 7.1 %copy-start.15 = (bf16[16,48,384]{2,1,0:T(8,128)(2,1)}, bf16[16,48,384]{2,1,0:T(8,128)(2,1)S(1)}, u32[]{:S(2)}) copy-start(bf16[16,48,384]{2,1,0:T(8,128)(2,1)S(1)} %collective-permute-done.4.refs_5_) | copy-start | bytes 1769476
  45.9 7.8 %copy-start.17 = (bf16[8,48,384]{2,1,0:T(8,128)(2,1)}, bf16[8,48,384]{2,1,0:T(8,128)(2,1)S(1)}, u32[]{:S(2)}) copy-start(bf16[8,48,384]{2,1,0:T(8,128)(2,1)S(1)} %collective-permute-done.2.refs_3_) | copy-start | bytes 884740
  47.6 26.7 %all-to-all-start.1 = ((bf16[16,288,128]{2,1,0:T(8,128)(2,1)}), bf16[16,288,128]{2,1,0:T(8,128)(2,1)S(1)}, u32[]{:S(2)}, u32[]{:S(2)}) async-start(bf16[16,288,128]{2,1,0:T(8,128)(2,1)} %pack.3), calls=%async_computation.1 | async-start | bytes 2359296 | tf_op jit(solution)/shard_map/all_to_all | solution.py:454
  51.4 1.7 %collective-permute-start.7 = (bf16[8,48,384]{2,1,0:T(8,128)(2,1)S(1)}, bf16[8,48,384]{2,1,0:T(8,128)(2,1)S(1)}, u32[]{:S(2)}, u32[]{:S(2)}) collective-permute-start(bf16[8,48,384]{2,1,0:T(8,128)(2,1)S(1)} %collective-permute-done.2.refs_3_), channel_id=1, source_target_pairs={{0,16},{16,0},{32,48},{48,32},{64,80},{80,64},{96,112},{112,96},{1... | collective-permute-start | bytes 884744 | tf_op jit(solution)/shard_map/ppermute | solution.py:426
  51.7 1.9 %collective-permute-start.8 = (bf16[8,48,384]{2,1,0:T(8,128)(2,1)S(1)}, bf16[8,48,384]{2,1,0:T(8,128)(2,1)}, u32[]{:S(2)}, u32[]{:S(2)}) collective-permute-start(bf16[8,48,384]{2,1,0:T(8,128)(2,1)S(1)} %copy-done.19), channel_id=1, source_target_pairs={{0,16},{16,0},{32,48},{48,32},{64,80},{80,64},{96,112},{112,96},{1... | collective-permute-start | bytes 884744 | tf_op jit(solution)/shard_map/ppermute | solution.py:426
  52.0 22.2 %copy-start.1 = (bf16[3,3072]{1,0:T(4,128)(2,1)S(1)}, bf16[3,3072]{1,0:T(4,128)(2,1)}, u32[]{:S(2)}) copy-start(bf16[3,3072]{1,0:T(4,128)(2,1)} %fusion.pick_ref) | copy-start | bytes 55300
  52.0 22.2 %copy-start.2 = (f32[1,768]{1,0:T(1,128)S(1)}, f32[1,768]{1,0:T(1,128)}, u32[]{:S(2)}) copy-start(f32[1,768]{1,0:T(1,128)} %broadcast_in_dim.21.norm_ref) | copy-start | bytes 9220
  52.0 22.2 %copy-start.7 = (f32[3,768]{1,0:T(4,128)S(1)}, f32[3,768]{1,0:T(4,128)}, u32[]{:S(2)}) copy-start(f32[3,768]{1,0:T(4,128)} %bias_ref.3) | copy-start | bytes 27652
  52.0 22.2 %copy-start.8 = (f32[3,768]{1,0:T(4,128)S(1)}, f32[3,768]{1,0:T(4,128)}, u32[]{:S(2)}) copy-start(f32[3,768]{1,0:T(4,128)} %gain_ref.3) | copy-start | bytes 27652
  61.6 28.5 %collective-permute-start.12 = (bf16[4,48,768]{2,1,0:T(8,128)(2,1)}, bf16[4,48,768]{2,1,0:T(8,128)(2,1)S(1)}, u32[]{:S(2)}, u32[]{:S(2)}) collective-permute-start(bf16[4,48,768]{2,1,0:T(8,128)(2,1)} %get-tuple-element.55.own0_ref), channel_id=1, source_target_pairs={{1,0},{2,1},{3,2},{4,3},{5,4},{6,5},{7,6},{8,7},{9,8},{10,9},{11,1... | collective-permute-start | bytes 884744 | tf_op jit(solution)/shard_map/ppermute | solution.py:462
  71.3 20.3 %collective-permute-start.11 = (bf16[4,48,768]{2,1,0:T(8,128)(2,1)}, bf16[4,48,768]{2,1,0:T(8,128)(2,1)S(1)}, u32[]{:S(2)}, u32[]{:S(2)}) collective-permute-start(bf16[4,48,768]{2,1,0:T(8,128)(2,1)} %get-tuple-element.55.own0_ref), channel_id=1, source_target_pairs={{0,1},{1,2},{2,3},{3,4},{4,5},{5,6},{6,7},{7,8},{8,9},{9,10},{10,1... | collective-permute-start | bytes 884744 | tf_op jit(solution)/shard_map/ppermute | solution.py:461
  74.3 21.4 %copy-start = (bf16[4,48,768]{2,1,0:T(8,128)(2,1)S(1)}, bf16[4,48,768]{2,1,0:T(8,128)(2,1)}, u32[]{:S(2)}) copy-start(bf16[4,48,768]{2,1,0:T(8,128)(2,1)} %get-tuple-element.55.own0_ref) | copy-start | bytes 884740
  74.3 21.4 %copy-start.3 = (bf16[768,2304]{1,0:T(8,128)(2,1)S(1)}, bf16[768,2304]{1,0:T(8,128)(2,1)}, u32[]{:S(2)}) copy-start(bf16[768,2304]{1,0:T(8,128)(2,1)} %w_ref.5) | copy-start | bytes 10616836
  81.3 19.3 %collective-permute-start.10 = (bf16[4,48,768]{2,1,0:T(8,128)(2,1)S(1)}, bf16[4,48,768]{2,1,0:T(8,128)(2,1)S(1)}, u32[]{:S(2)}, u32[]{:S(2)}) collective-permute-start(bf16[4,48,768]{2,1,0:T(8,128)(2,1)S(1)} %get-tuple-element.56.own1_ref), channel_id=1, source_target_pairs={{1,0},{2,1},{3,2},{4,3},{5,4},{6,5},{7,6},{8,7},{9,8},{10,9},{11,1... | collective-permute-start | bytes 884744 | tf_op jit(solution)/shard_map/ppermute | solution.py:462
  88.2 20.0 %collective-permute-start.9 = (bf16[4,48,768]{2,1,0:T(8,128)(2,1)S(1)}, bf16[4,48,768]{2,1,0:T(8,128)(2,1)S(1)}, u32[]{:S(2)}, u32[]{:S(2)}) collective-permute-start(bf16[4,48,768]{2,1,0:T(8,128)(2,1)S(1)} %get-tuple-element.56.own1_ref), channel_id=1, source_target_pairs={{0,1},{1,2},{2,3},{3,4},{4,5},{5,6},{6,7},{7,8},{8,9},{9,10},{10,1... | collective-permute-start | bytes 884744 | tf_op jit(solution)/shard_map/ppermute | solution.py:461
  91.6 20.9 %collective-permute-start.13 = (bf16[16,8,768]{2,1,0:T(8,128)(2,1)S(1)}, bf16[16,8,768]{2,1,0:T(8,128)(2,1)S(1)}, u32[]{:S(2)}, u32[]{:S(2)}) collective-permute-start(bf16[16,8,768]{2,1,0:T(8,128)(2,1)S(1)} %pad_maximum_fusion), channel_id=1, source_target_pairs={{0,16},{16,32},{32,48},{48,64},{64,80},{80,96},{96,112},{112,128},... | collective-permute-start | bytes 589832 | tf_op jit(solution)/shard_map/ppermute | solution.py:465
  91.8 20.8 %copy-start.4 = (bf16[768,768]{1,0:T(8,128)(2,1)S(1)}, bf16[768,768]{1,0:T(8,128)(2,1)}, u32[]{:S(2)}) copy-start(bf16[768,768]{1,0:T(8,128)(2,1)} %wout_ref.3) | copy-start | bytes 3538948
  91.8 20.8 %copy-start.9 = (s32[128]{0:T(128)S(1)}, s32[128]{0:T(128)}, u32[]{:S(2)}) copy-start(s32[128]{0:T(128)} %start_ref.3) | copy-start | bytes 1540
  91.8 20.8 %copy-start.10 = (bf16[4,48,768]{2,1,0:T(8,128)(2,1)S(1)}, bf16[4,48,768]{2,1,0:T(8,128)(2,1)}, u32[]{:S(2)}) copy-start(bf16[4,48,768]{2,1,0:T(8,128)(2,1)} %get-tuple-element.64.emb0_ref) | copy-start | bytes 884740
  91.8 20.7 %collective-permute-start.14 = (bf16[16,8,768]{2,1,0:T(8,128)(2,1)S(1)}, bf16[16,8,768]{2,1,0:T(8,128)(2,1)S(1)}, u32[]{:S(2)}, u32[]{:S(2)}) collective-permute-start(bf16[16,8,768]{2,1,0:T(8,128)(2,1)S(1)} %pad_maximum_fusion.1), channel_id=1, source_target_pairs={{16,0},{32,16},{48,32},{64,48},{80,64},{96,80},{112,96},{128,112},... | collective-permute-start | bytes 589832 | tf_op jit(solution)/shard_map/ppermute | solution.py:466
  108.3 8.6 %collective-permute-start.15 = (bf16[8,8,768]{2,1,0:T(8,128)(2,1)S(1)}, bf16[8,8,768]{2,1,0:T(8,128)(2,1)S(1)}, u32[]{:S(2)}, u32[]{:S(2)}) collective-permute-start(bf16[8,8,768]{2,1,0:T(8,128)(2,1)S(1)} %pad_maximum_fusion.2), channel_id=1, source_target_pairs={{0,16},{16,32},{32,48},{48,64},{64,80},{80,96},{96,112},{112,128},... | collective-permute-start | bytes 294920 | tf_op jit(solution)/shard_map/ppermute | solution.py:465
  108.4 8.5 %collective-permute-start.16 = (bf16[8,8,768]{2,1,0:T(8,128)(2,1)S(1)}, bf16[8,8,768]{2,1,0:T(8,128)(2,1)S(1)}, u32[]{:S(2)}, u32[]{:S(2)}) collective-permute-start(bf16[8,8,768]{2,1,0:T(8,128)(2,1)S(1)} %pad_maximum_fusion.3), channel_id=1, source_target_pairs={{16,0},{32,16},{48,32},{64,48},{80,64},{96,80},{112,96},{128,112},... | collective-permute-start | bytes 294920 | tf_op jit(solution)/shard_map/ppermute | solution.py:466
  (9 other events, 20.8 us)

commit v5 on v4

--- a/solution.py
+++ b/solution.py
@@ -453,13 +453,17 @@
             packed[c] = held
         moved = lax.all_to_all(packed[c], "lev", split_axis=0, concat_axis=0, tiled=True)
         if c == 0:
-            held, *w_all[1:8] = lax.optimization_barrier((packed[1], *w_all[1:8]))
+            held, *w_all = lax.optimization_barrier((packed[1], *w_all))
         e, n, kept = embed(moved, place, w_all, pick, group_bias, group_gain, norm_gain)
         w_all = [kept]
         emb.append(e)
         normed.append(n)
-        low.append(lax.ppermute(n, "lat", up))
-        high.append(lax.ppermute(n, "lat", down))
+        if c % 2 == 0:
+            low.append(lax.ppermute(n, "lat", up))
+            high.append(lax.ppermute(n, "lat", down))
+        else:
+            high.append(lax.ppermute(n, "lat", down))
+            low.append(lax.ppermute(n, "lat", up))
 
     def strips(tall):
         left = lax.ppermute(jnp.concatenate([t[:, -STRIP:] for t in tall], axis=0), "lev", right_way)
@@ -469,7 +473,7 @@
     low[0], high[0], normed[1] = lax.optimization_barrier((low[0], high[0], normed[1]))
     left, right = strips([low[0], normed[0], normed[1], high[0]])
     q, kv = project(normed[0], normed[1], low[0], high[0], w_qkv)
-    low[1], high[1], q = lax.optimization_barrier((low[1], high[1], q))
+    high[1], low[1], q = lax.optimization_barrier((high[1], low[1], q))
     last_left, last_right = strips([low[1], high[1]])
     kv, centre = middle(
         lat_start, first_row, q, kv, low[1], high[1], left, right, w_qkv, w_out, emb[0], emb[1]

time: 124 us -> 122 us (0.984)
  the two profiles are of different devices: /device:TPU:2 before, /device:TPU:6 now
where the time goes in v5:
time: 122 us; the launch traced here: 121 us
  starting transfers between devices  45.8 us (38%)
  waiting for transfers between devices  34.8 us (29%)
  Pallas kernels  33.6 us (28%)
  local copies, waits for them, and re-layouts  5.12 us (4%)
  other arithmetic  1.32 us (1%)
    ppermute x2, starting transfers between devices, per_device(): high.append(lax.ppermute(n, 'lat', down))  9.49 us
    ppermute x2, waiting for transfers between devices, weight_pieces(): near = [lax.ppermute(own, 'lat', up), lax.ppermute(own, 'lat', down)]  8.84 us
    all_to_all x2, waiting for transfers between devices, per_device(): lax.all_to_all(packed[c], 'lev', split_axis=0, concat_axis=0, tiled=True)  8.18 us
    all_to_all x2, starting transfers between devices, per_device(): lax.all_to_all(packed[c], 'lev', split_axis=0, concat_axis=0, tiled=True)  8.07 us
    ppermute x2, starting transfers between devices, strips(): lax.ppermute(jnp.concatenate([t[:, :STRIP] for t in tall], axis=0), 'lev'...  8.05 us
    pallas_call x1, Pallas kernels, embed(): pl.pallas_call(embed_first_kernel, in_specs=[smem()] + [vmem()] * 5 + [fa...  7.83 us
    ppermute x2, waiting for transfers between devices, weight_pieces(): far = [lax.ppermute(first, 'lat', up), lax.ppermute(second, 'lat', down)]  7.46 us
    ppermute x2, starting transfers between devices, per_device(): low.append(lax.ppermute(n, 'lat', up))  7.28 us
  transfers between devices with their start and end apart: 20, of which 9 were waited for; matrix products, arithmetic and copies ran while one was open for 3% of the time, Pallas kernels for 22%

profile of v5, /device:TPU:6, one launch (start us, length us, event | category | flops | bytes accessed | tf_op | source)
XLA Modules:
  0.0 121.0 jit_solution(9945979887089131759)
XLA Ops:
  0.0 0.8 dynamic-slice_bitcast_fusion.1
  0.8 0.9 broadcast_in_dim.17
  1.7 5.9 %all-to-all-start = ((bf16[16,48,384]{2,1,0:T(8,128)(2,1)}), bf16[16,48,384]{2,1,0:T(8,128)(2,1)S(1)}, u32[]{:S(2)}, u32[]{:S(2)}) async-start(bf16[16,48,384]{2,1,0:T(8,128)(2,1)} %bitcast.4), calls=%async_computation | async-start | bytes 1179648 | tf_op jit(solution)/shard_map/all_to_all | solution.py:395
  7.6 2.7 %pack.3 = bf16[16,288,128]{2,1,0:T(8,128)(2,1)} custom-call(bf16[8,192,768]{2,1,0:T(8,128)(2,1)} %bitcast.16), custom_call_target="tpu_custom_call" | custom-call | bytes 2359296 | tf_op jit(solution)/shard_map/pack/pallas_call | solution.py:64
  10.3 2.7 %pack.2 = bf16[16,288,128]{2,1,0:T(8,128)(2,1)} custom-call(bf16[8,192,768]{2,1,0:T(8,128)(2,1)} %bitcast.17), custom_call_target="tpu_custom_call" | custom-call | bytes 2359296 | tf_op jit(solution)/shard_map/pack/pallas_call | solution.py:64
  15.3 4.0 %all-to-all-done.refs_0_ = bf16[16,48,384]{2,1,0:T(8,128)(2,1)S(1)} async-done(((bf16[16,48,384]{2,1,0:T(8,128)(2,1)}), bf16[16,48,384]{2,1,0:T(8,128)(2,1)S(1)}, u32[]{:S(2)}, u32[]{:S(2)}) %all-to-all-start) | async-done | bytes 589856 | tf_op jit(solution)/shard_map/all_to_all | solution.py:395
  19.2 0.8 collective-permute-start.1
  20.1 2.4 %collective-permute-start = (bf16[16,48,384]{2,1,0:T(8,128)(2,1)S(1)}, bf16[16,48,384]{2,1,0:T(8,128)(2,1)S(1)}, u32[]{:S(2)}, u32[]{:S(2)}) collective-permute-start(bf16[16,48,384]{2,1,0:T(8,128)(2,1)S(1)} %all-to-all-done.refs_0_), channel_id=1, source_target_pairs={{0,4},{4,8},{8,12},{12,0},{1,5},{5,9},{9,13},{13,1},{2,6},{6,10},{... | collective-permute-start | bytes 1769480 | tf_op jit(solution)/shard_map/ppermute | solution.py:421
  22.5 3.7 %all-to-all-start.2 = ((bf16[16,288,128]{2,1,0:T(8,128)(2,1)}), bf16[16,288,128]{2,1,0:T(8,128)(2,1)S(1)}, u32[]{:S(2)}, u32[]{:S(2)}) async-start(bf16[16,288,128]{2,1,0:T(8,128)(2,1)} %pack.2), calls=%async_computation.2 | async-start | bytes 2359296 | tf_op jit(solution)/shard_map/all_to_all | solution.py:454
  26.2 8.8 %collective-permute-done.1.down_ref.refs_2_ = bf16[16,48,384]{2,1,0:T(8,128)(2,1)S(1)} collective-permute-done((bf16[16,48,384]{2,1,0:T(8,128)(2,1)S(1)}, bf16[16,48,384]{2,1,0:T(8,128)(2,1)S(1)}, u32[]{:S(2)}, u32[]{:S(2)}) %collective-permute-start.1) | collective-permute-done | bytes 589856 | tf_op jit(solution)/shard_map/ppermute | solution.py:421
  35.1 3.0 %collective-permute-start.2 = (bf16[8,48,384]{2,1,0:T(8,128)(2,1)S(1)}, bf16[8,48,384]{2,1,0:T(8,128)(2,1)S(1)}, u32[]{:S(2)}, u32[]{:S(2)}) collective-permute-start(bf16[8,48,384]{2,1,0:T(8,128)(2,1)S(1)} %get-tuple-element.42), channel_id=1, source_target_pairs={{0,4},{4,8},{8,12},{12,0},{1,5},{5,9},{9,13},{13,1},{2,6},{6,10},{... | collective-permute-start | bytes 884744 | tf_op jit(solution)/shard_map/ppermute | solution.py:423
  38.6 4.1 %collective-permute-done.2.refs_3_ = bf16[8,48,384]{2,1,0:T(8,128)(2,1)S(1)} collective-permute-done((bf16[8,48,384]{2,1,0:T(8,128)(2,1)S(1)}, bf16[8,48,384]{2,1,0:T(8,128)(2,1)S(1)}, u32[]{:S(2)}, u32[]{:S(2)}) %collective-permute-start.2) | collective-permute-done | bytes 294944 | tf_op jit(solution)/shard_map/ppermute | solution.py:423
  42.7 3.4 %collective-permute-done.3.refs_4_ = bf16[8,48,384]{2,1,0:T(8,128)(2,1)S(1)} collective-permute-done((bf16[8,48,384]{2,1,0:T(8,128)(2,1)S(1)}, bf16[8,48,384]{2,1,0:T(8,128)(2,1)S(1)}, u32[]{:S(2)}, u32[]{:S(2)}) %collective-permute-start.3) | collective-permute-done | bytes 294944 | tf_op jit(solution)/shard_map/ppermute | solution.py:423
  46.1 1.6 %collective-permute-done.8.refs_9_ = bf16[8,48,384]{2,1,0:T(8,128)(2,1)S(1)} collective-permute-done((bf16[8,48,384]{2,1,0:T(8,128)(2,1)S(1)}, bf16[8,48,384]{2,1,0:T(8,128)(2,1)S(1)}, u32[]{:S(2)}, u32[]{:S(2)}) %collective-permute-start.8) | collective-permute-done | bytes 294944 | tf_op jit(solution)/shard_map/ppermute | solution.py:426
  47.7 0.7 copy-done.19
  48.4 0.8 copy-done.15
  49.2 4.4 %all-to-all-start.1 = ((bf16[16,288,128]{2,1,0:T(8,128)(2,1)}), bf16[16,288,128]{2,1,0:T(8,128)(2,1)S(1)}, u32[]{:S(2)}, u32[]{:S(2)}) async-start(bf16[16,288,128]{2,1,0:T(8,128)(2,1)} %pack.3), calls=%async_computation.1 | async-start | bytes 2359296 | tf_op jit(solution)/shard_map/all_to_all | solution.py:454
  53.7 7.8 %embed_first.1 = (bf16[4,48,768]{2,1,0:T(8,128)(2,1)}, bf16[4,48,768]{2,1,0:T(8,128)(2,1)}, bf16[16,4,48,768]{3,2,1,0:T(8,128)(2,1)}) custom-call(s32[2]{0:T(128)} %pad_add_fusion.1.place_ref, bf16[16,288,128]{2,1,0:T(8,128)(2,1)} %copy-done.11, bf16[3,3072]{1,0:T(4,128)(2,1)} %fusion.pick_ref, f32[3,768]{1,0:T(4,128)} %bias_ref.3, f32[3,768]{1,0:T(4,128)} %gain_ref.3, ...), custom_call_target="tpu_custom_call" | custom-call | flops 2717908992 | bytes 5898240 | tf_op jit(solution)/shard_map/embed_first/pallas_call | solution.py:191
  61.5 5.8 %collective-permute-start.12 = (bf16[4,48,768]{2,1,0:T(8,128)(2,1)}, bf16[4,48,768]{2,1,0:T(8,128)(2,1)S(1)}, u32[]{:S(2)}, u32[]{:S(2)}) collective-permute-start(bf16[4,48,768]{2,1,0:T(8,128)(2,1)} %get-tuple-element.61.own0_ref), channel_id=1, source_target_pairs={{1,0},{2,1},{3,2},{4,3},{5,4},{6,5},{7,6},{8,7},{9,8},{10,9},{11,1... | collective-permute-start | bytes 884744 | tf_op jit(solution)/shard_map/ppermute | solution.py:463
  67.4 2.1 %collective-permute-start.11 = (bf16[4,48,768]{2,1,0:T(8,128)(2,1)}, bf16[4,48,768]{2,1,0:T(8,128)(2,1)S(1)}, u32[]{:S(2)}, u32[]{:S(2)}) collective-permute-start(bf16[4,48,768]{2,1,0:T(8,128)(2,1)} %get-tuple-element.61.own0_ref), channel_id=1, source_target_pairs={{0,1},{1,2},{2,3},{3,4},{4,5},{5,6},{6,7},{7,8},{8,9},{9,10},{10,1... | collective-permute-start | bytes 884744 | tf_op jit(solution)/shard_map/ppermute | solution.py:462
  69.5 0.8 fusion.4
  70.3 8.2 %all-to-all-done.1.x_ref = bf16[16,288,128]{2,1,0:T(8,128)(2,1)S(1)} async-done(((bf16[16,288,128]{2,1,0:T(8,128)(2,1)}), bf16[16,288,128]{2,1,0:T(8,128)(2,1)S(1)}, u32[]{:S(2)}, u32[]{:S(2)}) %all-to-all-start.1) | async-done | bytes 1179680 | tf_op jit(solution)/shard_map/all_to_all | solution.py:454
  78.5 7.0 %embed_next.1 = (bf16[4,48,768]{2,1,0:T(8,128)(2,1)S(1)}, bf16[4,48,768]{2,1,0:T(8,128)(2,1)S(1)}) custom-call(bf16[16,288,128]{2,1,0:T(8,128)(2,1)S(1)} %all-to-all-done.1.x_ref, bf16[3,3072]{1,0:T(4,128)(2,1)S(1)} %copy-done.1, f32[3,768]{1,0:T(4,128)S(1)} %copy-done.7, f32[3,768]{1,0:T(4,128)S(1)} %copy-done.8, f32[1,768]{1,0:T(1,128)S(1)} %copy-done.2, ...), custom_call_target="tpu_custom_call" | custom-call | flops 2717908992 | bytes 5898240 | tf_op jit(solution)/shard_map/embed_next/pallas_call | solution.py:201
  85.5 5.2 %collective-permute-start.10 = (bf16[4,48,768]{2,1,0:T(8,128)(2,1)S(1)}, bf16[4,48,768]{2,1,0:T(8,128)(2,1)S(1)}, u32[]{:S(2)}, u32[]{:S(2)}) collective-permute-start(bf16[4,48,768]{2,1,0:T(8,128)(2,1)S(1)} %get-tuple-element.62.own1_ref), channel_id=1, source_target_pairs={{0,1},{1,2},{2,3},{3,4},{4,5},{5,6},{6,7},{7,8},{8,9},{9,10},{10,1... | collective-permute-start | bytes 884744 | tf_op jit(solution)/shard_map/ppermute | solution.py:466
  90.7 3.7 %collective-permute-start.9 = (bf16[4,48,768]{2,1,0:T(8,128)(2,1)S(1)}, bf16[4,48,768]{2,1,0:T(8,128)(2,1)S(1)}, u32[]{:S(2)}, u32[]{:S(2)}) collective-permute-start(bf16[4,48,768]{2,1,0:T(8,128)(2,1)S(1)} %get-tuple-element.62.own1_ref), channel_id=1, source_target_pairs={{1,0},{2,1},{3,2},{4,3},{5,4},{6,5},{7,6},{8,7},{9,8},{10,9},{11,1... | collective-permute-start | bytes 884744 | tf_op jit(solution)/shard_map/ppermute | solution.py:465
  94.6 3.9 %collective-permute-start.14 = (bf16[16,8,768]{2,1,0:T(8,128)(2,1)S(1)}, bf16[16,8,768]{2,1,0:T(8,128)(2,1)S(1)}, u32[]{:S(2)}, u32[]{:S(2)}) collective-permute-start(bf16[16,8,768]{2,1,0:T(8,128)(2,1)S(1)} %pad_maximum_fusion.1), channel_id=1, source_target_pairs={{16,0},{32,16},{48,32},{64,48},{80,64},{96,80},{112,96},{128,112},... | collective-permute-start | bytes 589832 | tf_op jit(solution)/shard_map/ppermute | solution.py:470
  98.6 2.5 %project.1 = (bf16[3,128,768]{2,1,0:T(8,128)(2,1)S(1)}, bf16[24,64,1536]{2,1,0:T(8,128)(2,1)S(1)}) custom-call(bf16[4,48,768]{2,1,0:T(8,128)(2,1)S(1)} %copy-done, bf16[4,48,768]{2,1,0:T(8,128)(2,1)S(1)} %get-tuple-element.62.own1_ref, bf16[4,48,768]{2,1,0:T(8,128)(2,1)S(1)} %collective-permute-done.11.low_ref, ...), custom_call_target="tpu_custom_call" | custom-call | flops 2264924160 | bytes 7077888 | tf_op jit(solution)/shard_map/project/pallas_call | solution.py:248
  101.1 0.9 collective-permute-done.10.low_ref
  102.0 3.8 %collective-permute-done.9.high_ref = bf16[4,48,768]{2,1,0:T(8,128)(2,1)S(1)} collective-permute-done((bf16[4,48,768]{2,1,0:T(8,128)(2,1)S(1)}, bf16[4,48,768]{2,1,0:T(8,128)(2,1)S(1)}, u32[]{:S(2)}, u32[]{:S(2)}) %collective-permute-start.9) | collective-permute-done | bytes 294944 | tf_op jit(solution)/shard_map/ppermute | solution.py:465
  105.9 4.1 %collective-permute-start.16 = (bf16[8,8,768]{2,1,0:T(8,128)(2,1)S(1)}, bf16[8,8,768]{2,1,0:T(8,128)(2,1)S(1)}, u32[]{:S(2)}, u32[]{:S(2)}) collective-permute-start(bf16[8,8,768]{2,1,0:T(8,128)(2,1)S(1)} %pad_maximum_fusion.3), channel_id=1, source_target_pairs={{16,0},{32,16},{48,32},{64,48},{80,64},{96,80},{112,96},{128,112},... | collective-permute-start | bytes 294920 | tf_op jit(solution)/shard_map/ppermute | solution.py:470
  110.2 4.3 %middle.1 = (bf16[24,64,1536]{2,1,0:T(8,128)(2,1)S(1)}, bf16[8,16,768]{2,1,0:T(8,128)(2,1)S(1)}) custom-call(s32[128]{0:T(128)S(1)} %copy-done.9, s32[1]{0:T(128)} %bitcast.first_ref, bf16[3,128,768]{2,1,0:T(8,128)(2,1)S(1)} %get-tuple-element.66.q_ref, bf16[24,64,1536]{2,1,0:T(8,128)(2,1)S(1)} %get-tuple-element.67._, ...), custom_call_target="tpu_custom_call", output_to_operand_aliasing={{0}: (3, {})} | custom-call | flops 8000000000 | bytes 10000000 | tf_op jit(solution)/shard_map/middle/pallas_call | solution.py:333
  114.5 6.5 %sides.1 = (bf16[8,48,768]{2,1,0:T(8,128)(2,1)}, bf16[24,64,1536]{2,1,0:T(8,128)(2,1)S(1)}) custom-call(s32[128]{0:T(128)S(1)} %copy-done.9, s32[1]{0:T(128)} %bitcast.first_ref, bf16[3,128,768]{2,1,0:T(8,128)(2,1)S(1)} %get-tuple-element.66.q_ref, bf16[24,64,1536]{2,1,0:T(8,128)(2,1)S(1)} %get-tuple-element.72._, ...), custom_call_target="tpu_custom_call", output_to_operand_aliasing={{1}: (3, {})} | custom-call | flops 8999999488 | bytes 10000000 | tf_op jit(solution)/shard_map/sides/pallas_call | solution.py:369
  (79 shorter events, 3.3 us)
Async XLA Ops:
  1.7 17.5 %all-to-all-start = ((bf16[16,48,384]{2,1,0:T(8,128)(2,1)}), bf16[16,48,384]{2,1,0:T(8,128)(2,1)S(1)}, u32[]{:S(2)}, u32[]{:S(2)}) async-start(bf16[16,48,384]{2,1,0:T(8,128)(2,1)} %bitcast.4), calls=%async_computation | async-start | bytes 1179648 | tf_op jit(solution)/shard_map/all_to_all | solution.py:395
  19.2 15.9 %copy-start.12 = (bf16[16,48,384]{2,1,0:T(8,128)(2,1)}, bf16[16,48,384]{2,1,0:T(8,128)(2,1)S(1)}, u32[]{:S(2)}) copy-start(bf16[16,48,384]{2,1,0:T(8,128)(2,1)S(1)} %all-to-all-done.refs_0_) | copy-start | bytes 1769476
  19.2 15.8 %collective-permute-start.1 = (bf16[16,48,384]{2,1,0:T(8,128)(2,1)S(1)}, bf16[16,48,384]{2,1,0:T(8,128)(2,1)S(1)}, u32[]{:S(2)}, u32[]{:S(2)}) collective-permute-start(bf16[16,48,384]{2,1,0:T(8,128)(2,1)S(1)} %all-to-all-done.refs_0_), channel_id=1, source_target_pairs={{0,12},{4,0},{8,4},{12,8},{1,13},{5,1},{9,5},{13,9},{2,14},{6,2},{... | collective-permute-start | bytes 1769480 | tf_op jit(solution)/shard_map/ppermute | solution.py:421
  20.1 15.0 %collective-permute-start = (bf16[16,48,384]{2,1,0:T(8,128)(2,1)S(1)}, bf16[16,48,384]{2,1,0:T(8,128)(2,1)S(1)}, u32[]{:S(2)}, u32[]{:S(2)}) collective-permute-start(bf16[16,48,384]{2,1,0:T(8,128)(2,1)S(1)} %all-to-all-done.refs_0_), channel_id=1, source_target_pairs={{0,4},{4,8},{8,12},{12,0},{1,5},{5,9},{9,13},{13,1},{2,6},{6,10},{... | collective-permute-start | bytes 1769480 | tf_op jit(solution)/shard_map/ppermute | solution.py:421
  22.5 23.6 %collective-permute-start.4 = (bf16[16,48,384]{2,1,0:T(8,128)(2,1)S(1)}, bf16[16,48,384]{2,1,0:T(8,128)(2,1)}, u32[]{:S(2)}, u32[]{:S(2)}) collective-permute-start(bf16[16,48,384]{2,1,0:T(8,128)(2,1)S(1)} %all-to-all-done.refs_0_), channel_id=1, source_target_pairs={{0,16},{16,0},{32,48},{48,32},{64,80},{80,64},{96,112},{112,96},{1... | collective-permute-start | bytes 1769480 | tf_op jit(solution)/shard_map/ppermute | solution.py:426
  22.5 26.8 %all-to-all-start.2 = ((bf16[16,288,128]{2,1,0:T(8,128)(2,1)}), bf16[16,288,128]{2,1,0:T(8,128)(2,1)S(1)}, u32[]{:S(2)}, u32[]{:S(2)}) async-start(bf16[16,288,128]{2,1,0:T(8,128)(2,1)} %pack.2), calls=%async_computation.2 | async-start | bytes 2359296 | tf_op jit(solution)/shard_map/all_to_all | solution.py:454
  35.1 7.6 %collective-permute-start.2 = (bf16[8,48,384]{2,1,0:T(8,128)(2,1)S(1)}, bf16[8,48,384]{2,1,0:T(8,128)(2,1)S(1)}, u32[]{:S(2)}, u32[]{:S(2)}) collective-permute-start(bf16[8,48,384]{2,1,0:T(8,128)(2,1)S(1)} %get-tuple-element.42), channel_id=1, source_target_pairs={{0,4},{4,8},{8,12},{12,0},{1,5},{5,9},{9,13},{13,1},{2,6},{6,10},{... | collective-permute-start | bytes 884744 | tf_op jit(solution)/shard_map/ppermute | solution.py:423
  38.1 8.0 %collective-permute-start.3 = (bf16[8,48,384]{2,1,0:T(8,128)(2,1)S(1)}, bf16[8,48,384]{2,1,0:T(8,128)(2,1)S(1)}, u32[]{:S(2)}, u32[]{:S(2)}) collective-permute-start(bf16[8,48,384]{2,1,0:T(8,128)(2,1)S(1)} %get-tuple-element.43), channel_id=1, source_target_pairs={{0,12},{4,0},{8,4},{12,8},{1,13},{5,1},{9,5},{13,9},{2,14},{6,2},{... | collective-permute-start | bytes 884744 | tf_op jit(solution)/shard_map/ppermute | solution.py:423
  38.1 9.6 %collective-permute-start.6 = (bf16[16,48,384]{2,1,0:T(8,128)(2,1)S(1)}, bf16[16,48,384]{2,1,0:T(8,128)(2,1)S(1)}, u32[]{:S(2)}, u32[]{:S(2)}) collective-permute-start(bf16[16,48,384]{2,1,0:T(8,128)(2,1)S(1)} %collective-permute-done.1.down_ref.refs_2_), channel_id=1, source_target_pairs={{0,16},{16,0},{32,48},{48,32},{64,80},{80,64},{96,112},{112,96},{1... | collective-permute-start | bytes 1769480 | tf_op jit(solution)/shard_map/ppermute | solution.py:426
  38.1 11.1 %collective-permute-start.5 = (bf16[16,48,384]{2,1,0:T(8,128)(2,1)S(1)}, bf16[16,48,384]{2,1,0:T(8,128)(2,1)}, u32[]{:S(2)}, u32[]{:S(2)}) collective-permute-start(bf16[16,48,384]{2,1,0:T(8,128)(2,1)S(1)} %collective-permute-done.up_ref.refs_1_), channel_id=1, source_target_pairs={{0,16},{16,0},{32,48},{48,32},{64,80},{80,64},{96,112},{112,96},{1... | collective-permute-start | bytes 1769480 | tf_op jit(solution)/shard_map/ppermute | solution.py:426
  42.7 10.9 %copy-start.16 = (bf16[8,48,384]{2,1,0:T(8,128)(2,1)}, bf16[8,48,384]{2,1,0:T(8,128)(2,1)S(1)}, u32[]{:S(2)}) copy-start(bf16[8,48,384]{2,1,0:T(8,128)(2,1)S(1)} %collective-permute-done.2.refs_3_) | copy-start | bytes 884740
  42.7 3.4 %collective-permute-start.7 = (bf16[8,48,384]{2,1,0:T(8,128)(2,1)S(1)}, bf16[8,48,384]{2,1,0:T(8,128)(2,1)S(1)}, u32[]{:S(2)}, u32[]{:S(2)}) collective-permute-start(bf16[8,48,384]{2,1,0:T(8,128)(2,1)S(1)} %collective-permute-done.2.refs_3_), channel_id=1, source_target_pairs={{0,16},{16,0},{32,48},{48,32},{64,80},{80,64},{96,112},{112,96},{1... | collective-permute-start | bytes 884744 | tf_op jit(solution)/shard_map/ppermute | solution.py:426
  46.1 1.6 %collective-permute-start.8 = (bf16[8,48,384]{2,1,0:T(8,128)(2,1)S(1)}, bf16[8,48,384]{2,1,0:T(8,128)(2,1)S(1)}, u32[]{:S(2)}, u32[]{:S(2)}) collective-permute-start(bf16[8,48,384]{2,1,0:T(8,128)(2,1)S(1)} %collective-permute-done.3.refs_4_), channel_id=1, source_target_pairs={{0,16},{16,0},{32,48},{48,32},{64,80},{80,64},{96,112},{112,96},{1... | collective-permute-start | bytes 884744 | tf_op jit(solution)/shard_map/ppermute | solution.py:426
  49.2 4.4 %copy-start.11 = (bf16[16,288,128]{2,1,0:T(8,128)(2,1)}, bf16[16,288,128]{2,1,0:T(8,128)(2,1)S(1)}, u32[]{:S(2)}) copy-start(bf16[16,288,128]{2,1,0:T(8,128)(2,1)S(1)} %all-to-all-done.2.x_ref) | copy-start | bytes 3538948
  49.2 29.2 %all-to-all-start.1 = ((bf16[16,288,128]{2,1,0:T(8,128)(2,1)}), bf16[16,288,128]{2,1,0:T(8,128)(2,1)S(1)}, u32[]{:S(2)}, u32[]{:S(2)}) async-start(bf16[16,288,128]{2,1,0:T(8,128)(2,1)} %pack.3), calls=%async_computation.1 | async-start | bytes 2359296 | tf_op jit(solution)/shard_map/all_to_all | solution.py:454
  53.6 24.8 %copy-start.1 = (bf16[3,3072]{1,0:T(4,128)(2,1)S(1)}, bf16[3,3072]{1,0:T(4,128)(2,1)}, u32[]{:S(2)}) copy-start(bf16[3,3072]{1,0:T(4,128)(2,1)} %fusion.pick_ref) | copy-start | bytes 55300
  53.7 24.8 %copy-start.2 = (f32[1,768]{1,0:T(1,128)S(1)}, f32[1,768]{1,0:T(1,128)}, u32[]{:S(2)}) copy-start(f32[1,768]{1,0:T(1,128)} %broadcast_in_dim.21.norm_ref) | copy-start | bytes 9220
  53.7 24.8 %copy-start.7 = (f32[3,768]{1,0:T(4,128)S(1)}, f32[3,768]{1,0:T(4,128)}, u32[]{:S(2)}) copy-start(f32[3,768]{1,0:T(4,128)} %bias_ref.3) | copy-start | bytes 27652
  53.7 24.8 %copy-start.8 = (f32[3,768]{1,0:T(4,128)S(1)}, f32[3,768]{1,0:T(4,128)}, u32[]{:S(2)}) copy-start(f32[3,768]{1,0:T(4,128)} %gain_ref.3) | copy-start | bytes 27652
  61.5 32.9 %collective-permute-start.12 = (bf16[4,48,768]{2,1,0:T(8,128)(2,1)}, bf16[4,48,768]{2,1,0:T(8,128)(2,1)S(1)}, u32[]{:S(2)}, u32[]{:S(2)}) collective-permute-start(bf16[4,48,768]{2,1,0:T(8,128)(2,1)} %get-tuple-element.61.own0_ref), channel_id=1, source_target_pairs={{1,0},{2,1},{3,2},{4,3},{5,4},{6,5},{7,6},{8,7},{9,8},{10,9},{11,1... | collective-permute-start | bytes 884744 | tf_op jit(solution)/shard_map/ppermute | solution.py:463
  67.4 27.0 %collective-permute-start.11 = (bf16[4,48,768]{2,1,0:T(8,128)(2,1)}, bf16[4,48,768]{2,1,0:T(8,128)(2,1)S(1)}, u32[]{:S(2)}, u32[]{:S(2)}) collective-permute-start(bf16[4,48,768]{2,1,0:T(8,128)(2,1)} %get-tuple-element.61.own0_ref), channel_id=1, source_target_pairs={{0,1},{1,2},{2,3},{3,4},{4,5},{5,6},{6,7},{7,8},{8,9},{9,10},{10,1... | collective-permute-start | bytes 884744 | tf_op jit(solution)/shard_map/ppermute | solution.py:462
  78.5 20.1 %copy-start = (bf16[4,48,768]{2,1,0:T(8,128)(2,1)S(1)}, bf16[4,48,768]{2,1,0:T(8,128)(2,1)}, u32[]{:S(2)}) copy-start(bf16[4,48,768]{2,1,0:T(8,128)(2,1)} %get-tuple-element.61.own0_ref) | copy-start | bytes 884740
  78.5 20.1 %copy-start.3 = (bf16[768,2304]{1,0:T(8,128)(2,1)S(1)}, bf16[768,2304]{1,0:T(8,128)(2,1)}, u32[]{:S(2)}) copy-start(bf16[768,2304]{1,0:T(8,128)(2,1)} %w_ref.5) | copy-start | bytes 10616836
  85.5 16.5 %collective-permute-start.10 = (bf16[4,48,768]{2,1,0:T(8,128)(2,1)S(1)}, bf16[4,48,768]{2,1,0:T(8,128)(2,1)S(1)}, u32[]{:S(2)}, u32[]{:S(2)}) collective-permute-start(bf16[4,48,768]{2,1,0:T(8,128)(2,1)S(1)} %get-tuple-element.62.own1_ref), channel_id=1, source_target_pairs={{0,1},{1,2},{2,3},{3,4},{4,5},{5,6},{6,7},{7,8},{8,9},{9,10},{10,1... | collective-permute-start | bytes 884744 | tf_op jit(solution)/shard_map/ppermute | solution.py:466
  90.7 15.0 %collective-permute-start.9 = (bf16[4,48,768]{2,1,0:T(8,128)(2,1)S(1)}, bf16[4,48,768]{2,1,0:T(8,128)(2,1)S(1)}, u32[]{:S(2)}, u32[]{:S(2)}) collective-permute-start(bf16[4,48,768]{2,1,0:T(8,128)(2,1)S(1)} %get-tuple-element.62.own1_ref), channel_id=1, source_target_pairs={{1,0},{2,1},{3,2},{4,3},{5,4},{6,5},{7,6},{8,7},{9,8},{10,9},{11,1... | collective-permute-start | bytes 884744 | tf_op jit(solution)/shard_map/ppermute | solution.py:465
  94.5 15.7 %collective-permute-start.13 = (bf16[16,8,768]{2,1,0:T(8,128)(2,1)S(1)}, bf16[16,8,768]{2,1,0:T(8,128)(2,1)S(1)}, u32[]{:S(2)}, u32[]{:S(2)}) collective-permute-start(bf16[16,8,768]{2,1,0:T(8,128)(2,1)S(1)} %pad_maximum_fusion), channel_id=1, source_target_pairs={{0,16},{16,32},{32,48},{48,64},{64,80},{80,96},{96,112},{112,128},... | collective-permute-start | bytes 589832 | tf_op jit(solution)/shard_map/ppermute | solution.py:469
  94.6 15.6 %copy-start.4 = (bf16[768,768]{1,0:T(8,128)(2,1)S(1)}, bf16[768,768]{1,0:T(8,128)(2,1)}, u32[]{:S(2)}) copy-start(bf16[768,768]{1,0:T(8,128)(2,1)} %wout_ref.3) | copy-start | bytes 3538948
  94.6 15.5 %copy-start.9 = (s32[128]{0:T(128)S(1)}, s32[128]{0:T(128)}, u32[]{:S(2)}) copy-start(s32[128]{0:T(128)} %start_ref.3) | copy-start | bytes 1540
  94.6 15.5 %copy-start.10 = (bf16[4,48,768]{2,1,0:T(8,128)(2,1)S(1)}, bf16[4,48,768]{2,1,0:T(8,128)(2,1)}, u32[]{:S(2)}) copy-start(bf16[4,48,768]{2,1,0:T(8,128)(2,1)} %get-tuple-element.70.emb0_ref) | copy-start | bytes 884740
  94.6 15.5 %collective-permute-start.14 = (bf16[16,8,768]{2,1,0:T(8,128)(2,1)S(1)}, bf16[16,8,768]{2,1,0:T(8,128)(2,1)S(1)}, u32[]{:S(2)}, u32[]{:S(2)}) collective-permute-start(bf16[16,8,768]{2,1,0:T(8,128)(2,1)S(1)} %pad_maximum_fusion.1), channel_id=1, source_target_pairs={{16,0},{32,16},{48,32},{64,48},{80,64},{96,80},{112,96},{128,112},... | collective-permute-start | bytes 589832 | tf_op jit(solution)/shard_map/ppermute | solution.py:470
  105.8 8.7 %collective-permute-start.15 = (bf16[8,8,768]{2,1,0:T(8,128)(2,1)S(1)}, bf16[8,8,768]{2,1,0:T(8,128)(2,1)S(1)}, u32[]{:S(2)}, u32[]{:S(2)}) collective-permute-start(bf16[8,8,768]{2,1,0:T(8,128)(2,1)S(1)} %pad_maximum_fusion.2), channel_id=1, source_target_pairs={{0,16},{16,32},{32,48},{48,64},{64,80},{80,96},{96,112},{112,128},... | collective-permute-start | bytes 294920 | tf_op jit(solution)/shard_map/ppermute | solution.py:469
  105.9 8.6 %collective-permute-start.16 = (bf16[8,8,768]{2,1,0:T(8,128)(2,1)S(1)}, bf16[8,8,768]{2,1,0:T(8,128)(2,1)S(1)}, u32[]{:S(2)}, u32[]{:S(2)}) collective-permute-start(bf16[8,8,768]{2,1,0:T(8,128)(2,1)S(1)} %pad_maximum_fusion.3), channel_id=1, source_target_pairs={{16,0},{32,16},{48,32},{64,48},{80,64},{96,80},{112,96},{128,112},... | collective-permute-start | bytes 294920 | tf_op jit(solution)/shard_map/ppermute | solution.py:470
  (8 other events, 17.0 us)

commit v6 on v5

--- a/solution.py
+++ b/solution.py
@@ -20,6 +20,7 @@
 MASKED = -1e30
 PART = 256
 SPLIT_FLOPS = 18e9
+FIRST_FLOPS = 16e9
 FIRST_LIMIT = 56
 NEXT_LIMIT = 50
 LIMIT = 36
@@ -184,7 +185,7 @@
     far = pl.BlockSpec(memory_space=pl.ANY)
     common = dict(
         compiler_params=params(FIRST_LIMIT if len(w_all) > 1 else NEXT_LIMIT),
-        cost_estimate=cost(2 * tokens * depth * width * groups, depth * width * 2 + tokens * depth * 2),
+        cost_estimate=cost(FIRST_FLOPS if len(w_all) > 1 else 2 * tokens * depth * width * groups, depth * width * 2 + tokens * depth * 2),
     )
     shared = (moved, pick, bias, gain, norm_gain)
     if len(w_all) > 1:
@@ -453,7 +454,7 @@
             packed[c] = held
         moved = lax.all_to_all(packed[c], "lev", split_axis=0, concat_axis=0, tiled=True)
         if c == 0:
-            held, *w_all = lax.optimization_barrier((packed[1], *w_all))
+            held, *w_all[5:8] = lax.optimization_barrier((packed[1], *w_all[5:8]))
         e, n, kept = embed(moved, place, w_all, pick, group_bias, group_gain, norm_gain)
         w_all = [kept]
         emb.append(e)

time: 122 us -> 117 us (0.959)
  the two profiles are of different devices: /device:TPU:6 before, /device:TPU:2 now
where the time goes in v6:
time: 117 us; the launch traced here: 116 us
  starting transfers between devices  47.2 us (40%)
  Pallas kernels  33.5 us (29%)
  waiting for transfers between devices  26.8 us (23%)
  local copies, waits for them, and re-layouts  7.03 us (6%)
  other arithmetic  1.29 us (1%)
    ppermute x2, starting transfers between devices, per_device(): high.append(lax.ppermute(n, 'lat', down))  15.4 us
    ppermute x2, waiting for transfers between devices, weight_pieces(): near = [lax.ppermute(own, 'lat', up), lax.ppermute(own, 'lat', down)]  9.82 us
    ppermute x2, waiting for transfers between devices, per_device(): low.append(lax.ppermute(n, 'lat', up))  8.85 us
    ppermute x2, starting transfers between devices, strips(): lax.ppermute(jnp.concatenate([t[:, :STRIP] for t in tall], axis=0), 'lev'...  8.05 us
    pallas_call x1, Pallas kernels, embed(): pl.pallas_call(embed_first_kernel, in_specs=[smem()] + [vmem()] * 5 + [fa...  7.81 us
    all_to_all x2, starting transfers between devices, per_device(): lax.all_to_all(packed[c], 'lev', split_axis=0, concat_axis=0, tiled=True)  7.4 us
    pallas_call x1, Pallas kernels, embed(): pl.pallas_call(embed_next_kernel, in_specs=[vmem()] * 5 + [far], out_spec...  7 us
    pallas_call x1, Pallas kernels, sides(): pl.pallas_call(sides_kernel, in_specs=[smem(), smem()] + [vmem()] * 9, ou...  6.47 us
  transfers between devices with their start and end apart: 20, of which 7 were waited for; matrix products, arithmetic and copies ran while one was open for 3% of the time, Pallas kernels for 23%

profile of v6, /device:TPU:2, one launch (start us, length us, event | category | flops | bytes accessed | tf_op | source)
XLA Modules:
  0.0 116.3 jit_solution(9220352864821087840)
XLA Ops:
  0.0 0.8 dynamic-slice_bitcast_fusion.1
  0.8 0.9 broadcast_in_dim.17
  1.7 5.9 %all-to-all-start = ((bf16[16,48,384]{2,1,0:T(8,128)(2,1)}), bf16[16,48,384]{2,1,0:T(8,128)(2,1)S(1)}, u32[]{:S(2)}, u32[]{:S(2)}) async-start(bf16[16,48,384]{2,1,0:T(8,128)(2,1)} %bitcast.4), calls=%async_computation | async-start | bytes 1179648 | tf_op jit(solution)/shard_map/all_to_all | solution.py:396
  7.6 2.7 %pack.3 = bf16[16,288,128]{2,1,0:T(8,128)(2,1)} custom-call(bf16[8,192,768]{2,1,0:T(8,128)(2,1)} %bitcast.16), custom_call_target="tpu_custom_call" | custom-call | bytes 2359296 | tf_op jit(solution)/shard_map/pack/pallas_call | solution.py:65
  10.3 2.7 %pack.2 = bf16[16,288,128]{2,1,0:T(8,128)(2,1)} custom-call(bf16[8,192,768]{2,1,0:T(8,128)(2,1)} %bitcast.17), custom_call_target="tpu_custom_call" | custom-call | bytes 2359296 | tf_op jit(solution)/shard_map/pack/pallas_call | solution.py:65
  14.6 0.6 fusion.pick_ref
  15.2 4.0 %all-to-all-done.refs_0_ = bf16[16,48,384]{2,1,0:T(8,128)(2,1)S(1)} async-done(((bf16[16,48,384]{2,1,0:T(8,128)(2,1)}), bf16[16,48,384]{2,1,0:T(8,128)(2,1)S(1)}, u32[]{:S(2)}, u32[]{:S(2)}) %all-to-all-start) | async-done | bytes 589856 | tf_op jit(solution)/shard_map/all_to_all | solution.py:396
  19.8 1.5 %collective-permute-start.1 = (bf16[16,48,384]{2,1,0:T(8,128)(2,1)S(1)}, bf16[16,48,384]{2,1,0:T(8,128)(2,1)S(1)}, u32[]{:S(2)}, u32[]{:S(2)}) collective-permute-start(bf16[16,48,384]{2,1,0:T(8,128)(2,1)S(1)} %all-to-all-done.refs_0_), channel_id=1, source_target_pairs={{0,4},{4,8},{8,12},{12,0},{1,5},{5,9},{9,13},{13,1},{2,6},{6,10},{... | collective-permute-start | bytes 1769480 | tf_op jit(solution)/shard_map/ppermute | solution.py:422
  21.2 3.7 %all-to-all-start.2 = ((bf16[16,288,128]{2,1,0:T(8,128)(2,1)}), bf16[16,288,128]{2,1,0:T(8,128)(2,1)S(1)}, u32[]{:S(2)}, u32[]{:S(2)}) async-start(bf16[16,288,128]{2,1,0:T(8,128)(2,1)} %pack.2), calls=%async_computation.2 | async-start | bytes 2359296 | tf_op jit(solution)/shard_map/all_to_all | solution.py:455
  25.2 8.6 %collective-permute-done.3.down_ref.refs_2_ = bf16[16,48,384]{2,1,0:T(8,128)(2,1)S(1)} collective-permute-done((bf16[16,48,384]{2,1,0:T(8,128)(2,1)S(1)}, bf16[16,48,384]{2,1,0:T(8,128)(2,1)S(1)}, u32[]{:S(2)}, u32[]{:S(2)}) %collective-permute-start.3) | collective-permute-done | bytes 589856 | tf_op jit(solution)/shard_map/ppermute | solution.py:422
  33.8 1.3 %collective-permute-done.1.up_ref.refs_1_ = bf16[16,48,384]{2,1,0:T(8,128)(2,1)S(1)} collective-permute-done((bf16[16,48,384]{2,1,0:T(8,128)(2,1)S(1)}, bf16[16,48,384]{2,1,0:T(8,128)(2,1)S(1)}, u32[]{:S(2)}, u32[]{:S(2)}) %collective-permute-start.1) | collective-permute-done | bytes 589856 | tf_op jit(solution)/shard_map/ppermute | solution.py:422
  35.1 0.8 copy-done.6
  36.4 2.5 %collective-permute-start.6 = (bf16[8,48,384]{2,1,0:T(8,128)(2,1)S(1)}, bf16[8,48,384]{2,1,0:T(8,128)(2,1)}, u32[]{:S(2)}, u32[]{:S(2)}) collective-permute-start(bf16[8,48,384]{2,1,0:T(8,128)(2,1)S(1)} %get-tuple-element.41), channel_id=1, source_target_pairs={{0,12},{4,0},{8,4},{12,8},{1,13},{5,1},{9,5},{13,9},{2,14},{6,2},{... | collective-permute-start | bytes 884744 | tf_op jit(solution)/shard_map/ppermute | solution.py:424
  38.9 0.8 copy-done.15
  39.7 0.8 copy-done.16
  40.6 2.4 %all-to-all-done.2.x_ref = bf16[16,288,128]{2,1,0:T(8,128)(2,1)S(1)} async-done(((bf16[16,288,128]{2,1,0:T(8,128)(2,1)}), bf16[16,288,128]{2,1,0:T(8,128)(2,1)S(1)}, u32[]{:S(2)}, u32[]{:S(2)}) %all-to-all-start.2) | async-done | bytes 1179680 | tf_op jit(solution)/shard_map/all_to_all | solution.py:455
  43.0 3.7 %all-to-all-start.1 = ((bf16[16,288,128]{2,1,0:T(8,128)(2,1)}), bf16[16,288,128]{2,1,0:T(8,128)(2,1)S(1)}, u32[]{:S(2)}, u32[]{:S(2)}) async-start(bf16[16,288,128]{2,1,0:T(8,128)(2,1)} %pack.3), calls=%async_computation.1 | async-start | bytes 2359296 | tf_op jit(solution)/shard_map/all_to_all | solution.py:455
  47.3 1.3 %collective-permute-done.7.refs_8_ = bf16[8,48,384]{2,1,0:T(8,128)(2,1)S(1)} collective-permute-done((bf16[8,48,384]{2,1,0:T(8,128)(2,1)}, bf16[8,48,384]{2,1,0:T(8,128)(2,1)S(1)}, u32[]{:S(2)}, u32[]{:S(2)}) %collective-permute-start.7) | collective-permute-done | bytes 294944 | tf_op jit(solution)/shard_map/ppermute | solution.py:427
  49.3 0.7 copy-done.18
  50.0 7.8 %embed_first.1 = (bf16[4,48,768]{2,1,0:T(8,128)(2,1)}, bf16[4,48,768]{2,1,0:T(8,128)(2,1)}, bf16[16,4,48,768]{3,2,1,0:T(8,128)(2,1)}) custom-call(s32[2]{0:T(128)} %pad_add_fusion.1.place_ref, bf16[16,288,128]{2,1,0:T(8,128)(2,1)} %copy-done.11, bf16[3,3072]{1,0:T(4,128)(2,1)} %fusion.pick_ref, f32[3,768]{1,0:T(4,128)} %bias_ref.3, f32[3,768]{1,0:T(4,128)} %gain_ref.3, ...), custom_call_target="tpu_custom_call" | custom-call | flops 16000000000 | bytes 5898240 | tf_op jit(solution)/shard_map/embed_first/pallas_call | solution.py:192
  57.8 8.9 %collective-permute-start.12 = (bf16[4,48,768]{2,1,0:T(8,128)(2,1)}, bf16[4,48,768]{2,1,0:T(8,128)(2,1)S(1)}, u32[]{:S(2)}, u32[]{:S(2)}) collective-permute-start(bf16[4,48,768]{2,1,0:T(8,128)(2,1)} %get-tuple-element.47.own0_ref), channel_id=1, source_target_pairs={{1,0},{2,1},{3,2},{4,3},{5,4},{6,5},{7,6},{8,7},{9,8},{10,9},{11,1... | collective-permute-start | bytes 884744 | tf_op jit(solution)/shard_map/ppermute | solution.py:464
  66.7 2.1 %collective-permute-start.11 = (bf16[4,48,768]{2,1,0:T(8,128)(2,1)}, bf16[4,48,768]{2,1,0:T(8,128)(2,1)S(1)}, u32[]{:S(2)}, u32[]{:S(2)}) collective-permute-start(bf16[4,48,768]{2,1,0:T(8,128)(2,1)} %get-tuple-element.47.own0_ref), channel_id=1, source_target_pairs={{0,1},{1,2},{2,3},{3,4},{4,5},{5,6},{6,7},{7,8},{8,9},{9,10},{10,1... | collective-permute-start | bytes 884744 | tf_op jit(solution)/shard_map/ppermute | solution.py:463
  68.8 0.8 fusion.4
  69.7 7.0 %embed_next.1 = (bf16[4,48,768]{2,1,0:T(8,128)(2,1)S(1)}, bf16[4,48,768]{2,1,0:T(8,128)(2,1)S(1)}) custom-call(bf16[16,288,128]{2,1,0:T(8,128)(2,1)S(1)} %all-to-all-done.1.x_ref, bf16[3,3072]{1,0:T(4,128)(2,1)S(1)} %copy-done.1, f32[3,768]{1,0:T(4,128)S(1)} %copy-done.7, f32[3,768]{1,0:T(4,128)S(1)} %copy-done.8, f32[1,768]{1,0:T(1,128)S(1)} %copy-done.2, ...), custom_call_target="tpu_custom_call" | custom-call | flops 2717908992 | bytes 5898240 | tf_op jit(solution)/shard_map/embed_next/pallas_call | solution.py:202
  76.7 2.3 %collective-permute-start.10 = (bf16[4,48,768]{2,1,0:T(8,128)(2,1)S(1)}, bf16[4,48,768]{2,1,0:T(8,128)(2,1)S(1)}, u32[]{:S(2)}, u32[]{:S(2)}) collective-permute-start(bf16[4,48,768]{2,1,0:T(8,128)(2,1)S(1)} %get-tuple-element.48.own1_ref), channel_id=1, source_target_pairs={{0,1},{1,2},{2,3},{3,4},{4,5},{5,6},{6,7},{7,8},{8,9},{9,10},{10,1... | collective-permute-start | bytes 884744 | tf_op jit(solution)/shard_map/ppermute | solution.py:467
  79.1 6.5 %collective-permute-start.9 = (bf16[4,48,768]{2,1,0:T(8,128)(2,1)S(1)}, bf16[4,48,768]{2,1,0:T(8,128)(2,1)S(1)}, u32[]{:S(2)}, u32[]{:S(2)}) collective-permute-start(bf16[4,48,768]{2,1,0:T(8,128)(2,1)S(1)} %get-tuple-element.48.own1_ref), channel_id=1, source_target_pairs={{1,0},{2,1},{3,2},{4,3},{5,4},{6,5},{7,6},{8,7},{9,8},{10,9},{11,1... | collective-permute-start | bytes 884744 | tf_op jit(solution)/shard_map/ppermute | solution.py:466
  85.6 8.8 %collective-permute-done.11.low_ref = bf16[4,48,768]{2,1,0:T(8,128)(2,1)S(1)} collective-permute-done((bf16[4,48,768]{2,1,0:T(8,128)(2,1)}, bf16[4,48,768]{2,1,0:T(8,128)(2,1)S(1)}, u32[]{:S(2)}, u32[]{:S(2)}) %collective-permute-start.11) | collective-permute-done | bytes 294944 | tf_op jit(solution)/shard_map/ppermute | solution.py:463
  94.7 3.9 %collective-permute-start.14 = (bf16[16,8,768]{2,1,0:T(8,128)(2,1)S(1)}, bf16[16,8,768]{2,1,0:T(8,128)(2,1)S(1)}, u32[]{:S(2)}, u32[]{:S(2)}) collective-permute-start(bf16[16,8,768]{2,1,0:T(8,128)(2,1)S(1)} %pad_maximum_fusion.1), channel_id=1, source_target_pairs={{16,0},{32,16},{48,32},{64,48},{80,64},{96,80},{112,96},{128,112},... | collective-permute-start | bytes 589832 | tf_op jit(solution)/shard_map/ppermute | solution.py:471
  98.6 2.5 %project.1 = (bf16[3,128,768]{2,1,0:T(8,128)(2,1)S(1)}, bf16[24,64,1536]{2,1,0:T(8,128)(2,1)S(1)}) custom-call(bf16[4,48,768]{2,1,0:T(8,128)(2,1)S(1)} %copy-done, bf16[4,48,768]{2,1,0:T(8,128)(2,1)S(1)} %get-tuple-element.48.own1_ref, bf16[4,48,768]{2,1,0:T(8,128)(2,1)S(1)} %collective-permute-done.11.low_ref, ...), custom_call_target="tpu_custom_call" | custom-call | flops 2264924160 | bytes 7077888 | tf_op jit(solution)/shard_map/project/pallas_call | solution.py:249
  101.3 4.1 %collective-permute-start.16 = (bf16[8,8,768]{2,1,0:T(8,128)(2,1)S(1)}, bf16[8,8,768]{2,1,0:T(8,128)(2,1)S(1)}, u32[]{:S(2)}, u32[]{:S(2)}) collective-permute-start(bf16[8,8,768]{2,1,0:T(8,128)(2,1)S(1)} %pad_maximum_fusion.3), channel_id=1, source_target_pairs={{16,0},{32,16},{48,32},{64,48},{80,64},{96,80},{112,96},{128,112},... | collective-permute-start | bytes 294920 | tf_op jit(solution)/shard_map/ppermute | solution.py:471
  105.5 4.3 %middle.1 = (bf16[24,64,1536]{2,1,0:T(8,128)(2,1)S(1)}, bf16[8,16,768]{2,1,0:T(8,128)(2,1)S(1)}) custom-call(s32[128]{0:T(128)S(1)} %copy-done.9, s32[1]{0:T(128)} %bitcast.first_ref, bf16[3,128,768]{2,1,0:T(8,128)(2,1)S(1)} %get-tuple-element.52.q_ref, bf16[24,64,1536]{2,1,0:T(8,128)(2,1)S(1)} %get-tuple-element.53._, ...), custom_call_target="tpu_custom_call", output_to_operand_aliasing={{0}: (3, {})} | custom-call | flops 8000000000 | bytes 10000000 | tf_op jit(solution)/shard_map/middle/pallas_call | solution.py:334
  109.8 6.5 %sides.1 = (bf16[8,48,768]{2,1,0:T(8,128)(2,1)}, bf16[24,64,1536]{2,1,0:T(8,128)(2,1)S(1)}) custom-call(s32[128]{0:T(128)S(1)} %copy-done.9, s32[1]{0:T(128)} %bitcast.first_ref, bf16[3,128,768]{2,1,0:T(8,128)(2,1)S(1)} %get-tuple-element.52.q_ref, bf16[24,64,1536]{2,1,0:T(8,128)(2,1)S(1)} %get-tuple-element.58._, ...), custom_call_target="tpu_custom_call", output_to_operand_aliasing={{1}: (3, {})} | custom-call | flops 8999999488 | bytes 10000000 | tf_op jit(solution)/shard_map/sides/pallas_call | solution.py:370
  (77 shorter events, 4.6 us)
Async XLA Ops:
  1.7 17.5 %all-to-all-start = ((bf16[16,48,384]{2,1,0:T(8,128)(2,1)}), bf16[16,48,384]{2,1,0:T(8,128)(2,1)S(1)}, u32[]{:S(2)}, u32[]{:S(2)}) async-start(bf16[16,48,384]{2,1,0:T(8,128)(2,1)} %bitcast.4), calls=%async_computation | async-start | bytes 1179648 | tf_op jit(solution)/shard_map/all_to_all | solution.py:396
  10.3 3.3 %copy-start.14 = (s32[128]{0:T(128)S(1)}, s32[128]{0:T(128)}, u32[]{:S(2)}) copy-start(s32[128]{0:T(128)} %param.10) | copy-start | bytes 1540
  19.2 15.9 %copy-start.12 = (bf16[16,48,384]{2,1,0:T(8,128)(2,1)}, bf16[16,48,384]{2,1,0:T(8,128)(2,1)S(1)}, u32[]{:S(2)}) copy-start(bf16[16,48,384]{2,1,0:T(8,128)(2,1)S(1)} %all-to-all-done.refs_0_) | copy-start | bytes 1769476
  19.2 14.6 %collective-permute-start.3 = (bf16[16,48,384]{2,1,0:T(8,128)(2,1)S(1)}, bf16[16,48,384]{2,1,0:T(8,128)(2,1)S(1)}, u32[]{:S(2)}, u32[]{:S(2)}) collective-permute-start(bf16[16,48,384]{2,1,0:T(8,128)(2,1)S(1)} %all-to-all-done.refs_0_), channel_id=1, source_target_pairs={{0,12},{4,0},{8,4},{12,8},{1,13},{5,1},{9,5},{13,9},{2,14},{6,2},{... | collective-permute-start | bytes 1769480 | tf_op jit(solution)/shard_map/ppermute | solution.py:422
  19.8 15.3 %collective-permute-start.1 = (bf16[16,48,384]{2,1,0:T(8,128)(2,1)S(1)}, bf16[16,48,384]{2,1,0:T(8,128)(2,1)S(1)}, u32[]{:S(2)}, u32[]{:S(2)}) collective-permute-start(bf16[16,48,384]{2,1,0:T(8,128)(2,1)S(1)} %all-to-all-done.refs_0_), channel_id=1, source_target_pairs={{0,4},{4,8},{8,12},{12,0},{1,5},{5,9},{9,13},{13,1},{2,6},{6,10},{... | collective-permute-start | bytes 1769480 | tf_op jit(solution)/shard_map/ppermute | solution.py:422
  21.2 21.7 %all-to-all-start.2 = ((bf16[16,288,128]{2,1,0:T(8,128)(2,1)}), bf16[16,288,128]{2,1,0:T(8,128)(2,1)S(1)}, u32[]{:S(2)}, u32[]{:S(2)}) async-start(bf16[16,288,128]{2,1,0:T(8,128)(2,1)} %pack.2), calls=%async_computation.2 | async-start | bytes 2359296 | tf_op jit(solution)/shard_map/all_to_all | solution.py:455
  25.0 13.9 %collective-permute-start = (bf16[16,48,384]{2,1,0:T(8,128)(2,1)S(1)}, bf16[16,48,384]{2,1,0:T(8,128)(2,1)S(1)}, u32[]{:S(2)}, u32[]{:S(2)}) collective-permute-start(bf16[16,48,384]{2,1,0:T(8,128)(2,1)S(1)} %all-to-all-done.refs_0_), channel_id=1, source_target_pairs={{0,16},{16,0},{32,48},{48,32},{64,80},{80,64},{96,112},{112,96},{1... | collective-permute-start | bytes 1769480 | tf_op jit(solution)/shard_map/ppermute | solution.py:427
  33.8 5.1 %collective-permute-start.4 = (bf16[16,48,384]{2,1,0:T(8,128)(2,1)S(1)}, bf16[16,48,384]{2,1,0:T(8,128)(2,1)S(1)}, u32[]{:S(2)}, u32[]{:S(2)}) collective-permute-start(bf16[16,48,384]{2,1,0:T(8,128)(2,1)S(1)} %collective-permute-done.3.down_ref.refs_2_), channel_id=1, source_target_pairs={{0,16},{16,0},{32,48},{48,32},{64,80},{80,64},{96,112},{112,96},{1... | collective-permute-start | bytes 1769480 | tf_op jit(solution)/shard_map/ppermute | solution.py:427
  35.1 5.5 %collective-permute-start.2 = (bf16[16,48,384]{2,1,0:T(8,128)(2,1)S(1)}, bf16[16,48,384]{2,1,0:T(8,128)(2,1)}, u32[]{:S(2)}, u32[]{:S(2)}) collective-permute-start(bf16[16,48,384]{2,1,0:T(8,128)(2,1)S(1)} %collective-permute-done.1.up_ref.refs_1_), channel_id=1, source_target_pairs={{0,16},{16,0},{32,48},{48,32},{64,80},{80,64},{96,112},{112,96},{1... | collective-permute-start | bytes 1769480 | tf_op jit(solution)/shard_map/ppermute | solution.py:427
  35.9 10.8 %collective-permute-start.5 = (bf16[8,48,384]{2,1,0:T(8,128)(2,1)S(1)}, bf16[8,48,384]{2,1,0:T(8,128)(2,1)}, u32[]{:S(2)}, u32[]{:S(2)}) collective-permute-start(bf16[8,48,384]{2,1,0:T(8,128)(2,1)S(1)} %get-tuple-element.40), channel_id=1, source_target_pairs={{0,4},{4,8},{8,12},{12,0},{1,5},{5,9},{9,13},{13,1},{2,6},{6,10},{... | collective-permute-start | bytes 884744 | tf_op jit(solution)/shard_map/ppermute | solution.py:424
  36.4 10.7 %collective-permute-start.6 = (bf16[8,48,384]{2,1,0:T(8,128)(2,1)S(1)}, bf16[8,48,384]{2,1,0:T(8,128)(2,1)}, u32[]{:S(2)}, u32[]{:S(2)}) collective-permute-start(bf16[8,48,384]{2,1,0:T(8,128)(2,1)S(1)} %get-tuple-element.41), channel_id=1, source_target_pairs={{0,12},{4,0},{8,4},{12,8},{1,13},{5,1},{9,5},{13,9},{2,14},{6,2},{... | collective-permute-start | bytes 884744 | tf_op jit(solution)/shard_map/ppermute | solution.py:424
  43.0 6.0 %copy-start.11 = (bf16[16,288,128]{2,1,0:T(8,128)(2,1)}, bf16[16,288,128]{2,1,0:T(8,128)(2,1)S(1)}, u32[]{:S(2)}) copy-start(bf16[16,288,128]{2,1,0:T(8,128)(2,1)S(1)} %all-to-all-done.2.x_ref) | copy-start | bytes 3538948
  43.0 26.7 %all-to-all-start.1 = ((bf16[16,288,128]{2,1,0:T(8,128)(2,1)}), bf16[16,288,128]{2,1,0:T(8,128)(2,1)S(1)}, u32[]{:S(2)}, u32[]{:S(2)}) async-start(bf16[16,288,128]{2,1,0:T(8,128)(2,1)} %pack.3), calls=%async_computation.1 | async-start | bytes 2359296 | tf_op jit(solution)/shard_map/all_to_all | solution.py:455
  46.7 1.9 %collective-permute-start.7 = (bf16[8,48,384]{2,1,0:T(8,128)(2,1)}, bf16[8,48,384]{2,1,0:T(8,128)(2,1)S(1)}, u32[]{:S(2)}, u32[]{:S(2)}) collective-permute-start(bf16[8,48,384]{2,1,0:T(8,128)(2,1)} %collective-permute-done.5.refs_3_), channel_id=1, source_target_pairs={{0,16},{16,0},{32,48},{48,32},{64,80},{80,64},{96,112},{112,96},{1... | collective-permute-start | bytes 884744 | tf_op jit(solution)/shard_map/ppermute | solution.py:427
  47.1 1.9 %collective-permute-start.8 = (bf16[8,48,384]{2,1,0:T(8,128)(2,1)}, bf16[8,48,384]{2,1,0:T(8,128)(2,1)S(1)}, u32[]{:S(2)}, u32[]{:S(2)}) collective-permute-start(bf16[8,48,384]{2,1,0:T(8,128)(2,1)} %collective-permute-done.6.refs_4_), channel_id=1, source_target_pairs={{0,16},{16,0},{32,48},{48,32},{64,80},{80,64},{96,112},{112,96},{1... | collective-permute-start | bytes 884744 | tf_op jit(solution)/shard_map/ppermute | solution.py:427
  47.3 22.4 %copy-start.1 = (bf16[3,3072]{1,0:T(4,128)(2,1)S(1)}, bf16[3,3072]{1,0:T(4,128)(2,1)}, u32[]{:S(2)}) copy-start(bf16[3,3072]{1,0:T(4,128)(2,1)} %fusion.pick_ref) | copy-start | bytes 55300
  47.3 22.4 %copy-start.2 = (f32[1,768]{1,0:T(1,128)S(1)}, f32[1,768]{1,0:T(1,128)}, u32[]{:S(2)}) copy-start(f32[1,768]{1,0:T(1,128)} %broadcast_in_dim.21.norm_ref) | copy-start | bytes 9220
  47.3 22.4 %copy-start.7 = (f32[3,768]{1,0:T(4,128)S(1)}, f32[3,768]{1,0:T(4,128)}, u32[]{:S(2)}) copy-start(f32[3,768]{1,0:T(4,128)} %bias_ref.3) | copy-start | bytes 27652
  47.3 22.4 %copy-start.8 = (f32[3,768]{1,0:T(4,128)S(1)}, f32[3,768]{1,0:T(4,128)}, u32[]{:S(2)}) copy-start(f32[3,768]{1,0:T(4,128)} %gain_ref.3) | copy-start | bytes 27652
  57.8 27.8 %collective-permute-start.12 = (bf16[4,48,768]{2,1,0:T(8,128)(2,1)}, bf16[4,48,768]{2,1,0:T(8,128)(2,1)S(1)}, u32[]{:S(2)}, u32[]{:S(2)}) collective-permute-start(bf16[4,48,768]{2,1,0:T(8,128)(2,1)} %get-tuple-element.47.own0_ref), channel_id=1, source_target_pairs={{1,0},{2,1},{3,2},{4,3},{5,4},{6,5},{7,6},{8,7},{9,8},{10,9},{11,1... | collective-permute-start | bytes 884744 | tf_op jit(solution)/shard_map/ppermute | solution.py:464
  66.7 27.7 %collective-permute-start.11 = (bf16[4,48,768]{2,1,0:T(8,128)(2,1)}, bf16[4,48,768]{2,1,0:T(8,128)(2,1)S(1)}, u32[]{:S(2)}, u32[]{:S(2)}) collective-permute-start(bf16[4,48,768]{2,1,0:T(8,128)(2,1)} %get-tuple-element.47.own0_ref), channel_id=1, source_target_pairs={{0,1},{1,2},{2,3},{3,4},{4,5},{5,6},{6,7},{7,8},{8,9},{9,10},{10,1... | collective-permute-start | bytes 884744 | tf_op jit(solution)/shard_map/ppermute | solution.py:463
  69.7 28.9 %copy-start = (bf16[4,48,768]{2,1,0:T(8,128)(2,1)S(1)}, bf16[4,48,768]{2,1,0:T(8,128)(2,1)}, u32[]{:S(2)}) copy-start(bf16[4,48,768]{2,1,0:T(8,128)(2,1)} %get-tuple-element.47.own0_ref) | copy-start | bytes 884740
  69.7 28.9 %copy-start.3 = (bf16[768,2304]{1,0:T(8,128)(2,1)S(1)}, bf16[768,2304]{1,0:T(8,128)(2,1)}, u32[]{:S(2)}) copy-start(bf16[768,2304]{1,0:T(8,128)(2,1)} %w_ref.5) | copy-start | bytes 10616836
  76.7 24.4 %collective-permute-start.10 = (bf16[4,48,768]{2,1,0:T(8,128)(2,1)S(1)}, bf16[4,48,768]{2,1,0:T(8,128)(2,1)S(1)}, u32[]{:S(2)}, u32[]{:S(2)}) collective-permute-start(bf16[4,48,768]{2,1,0:T(8,128)(2,1)S(1)} %get-tuple-element.48.own1_ref), channel_id=1, source_target_pairs={{0,1},{1,2},{2,3},{3,4},{4,5},{5,6},{6,7},{7,8},{8,9},{9,10},{10,1... | collective-permute-start | bytes 884744 | tf_op jit(solution)/shard_map/ppermute | solution.py:467
  79.1 22.1 %collective-permute-start.9 = (bf16[4,48,768]{2,1,0:T(8,128)(2,1)S(1)}, bf16[4,48,768]{2,1,0:T(8,128)(2,1)S(1)}, u32[]{:S(2)}, u32[]{:S(2)}) collective-permute-start(bf16[4,48,768]{2,1,0:T(8,128)(2,1)S(1)} %get-tuple-element.48.own1_ref), channel_id=1, source_target_pairs={{1,0},{2,1},{3,2},{4,3},{5,4},{6,5},{7,6},{8,7},{9,8},{10,9},{11,1... | collective-permute-start | bytes 884744 | tf_op jit(solution)/shard_map/ppermute | solution.py:466
  94.5 10.9 %collective-permute-start.13 = (bf16[16,8,768]{2,1,0:T(8,128)(2,1)S(1)}, bf16[16,8,768]{2,1,0:T(8,128)(2,1)S(1)}, u32[]{:S(2)}, u32[]{:S(2)}) collective-permute-start(bf16[16,8,768]{2,1,0:T(8,128)(2,1)S(1)} %pad_maximum_fusion), channel_id=1, source_target_pairs={{0,16},{16,32},{32,48},{48,64},{64,80},{80,96},{96,112},{112,128},... | collective-permute-start | bytes 589832 | tf_op jit(solution)/shard_map/ppermute | solution.py:470
  94.6 10.8 %copy-start.4 = (bf16[768,768]{1,0:T(8,128)(2,1)S(1)}, bf16[768,768]{1,0:T(8,128)(2,1)}, u32[]{:S(2)}) copy-start(bf16[768,768]{1,0:T(8,128)(2,1)} %wout_ref.3) | copy-start | bytes 3538948
  94.7 10.8 %copy-start.9 = (s32[128]{0:T(128)S(1)}, s32[128]{0:T(128)}, u32[]{:S(2)}) copy-start(s32[128]{0:T(128)} %start_ref.3) | copy-start | bytes 1540
  94.7 10.8 %copy-start.10 = (bf16[4,48,768]{2,1,0:T(8,128)(2,1)S(1)}, bf16[4,48,768]{2,1,0:T(8,128)(2,1)}, u32[]{:S(2)}) copy-start(bf16[4,48,768]{2,1,0:T(8,128)(2,1)} %get-tuple-element.56.emb0_ref) | copy-start | bytes 884740
  94.7 10.7 %collective-permute-start.14 = (bf16[16,8,768]{2,1,0:T(8,128)(2,1)S(1)}, bf16[16,8,768]{2,1,0:T(8,128)(2,1)S(1)}, u32[]{:S(2)}, u32[]{:S(2)}) collective-permute-start(bf16[16,8,768]{2,1,0:T(8,128)(2,1)S(1)} %pad_maximum_fusion.1), channel_id=1, source_target_pairs={{16,0},{32,16},{48,32},{64,48},{80,64},{96,80},{112,96},{128,112},... | collective-permute-start | bytes 589832 | tf_op jit(solution)/shard_map/ppermute | solution.py:471
  101.2 8.6 %collective-permute-start.15 = (bf16[8,8,768]{2,1,0:T(8,128)(2,1)S(1)}, bf16[8,8,768]{2,1,0:T(8,128)(2,1)S(1)}, u32[]{:S(2)}, u32[]{:S(2)}) collective-permute-start(bf16[8,8,768]{2,1,0:T(8,128)(2,1)S(1)} %pad_maximum_fusion.2), channel_id=1, source_target_pairs={{0,16},{16,32},{32,48},{48,64},{64,80},{80,96},{96,112},{112,128},... | collective-permute-start | bytes 294920 | tf_op jit(solution)/shard_map/ppermute | solution.py:470
  101.3 8.5 %collective-permute-start.16 = (bf16[8,8,768]{2,1,0:T(8,128)(2,1)S(1)}, bf16[8,8,768]{2,1,0:T(8,128)(2,1)S(1)}, u32[]{:S(2)}, u32[]{:S(2)}) collective-permute-start(bf16[8,8,768]{2,1,0:T(8,128)(2,1)S(1)} %pad_maximum_fusion.3), channel_id=1, source_target_pairs={{16,0},{32,16},{48,32},{64,48},{80,64},{96,80},{112,96},{128,112},... | collective-permute-start | bytes 294920 | tf_op jit(solution)/shard_map/ppermute | solution.py:471
  (7 other events, 8.0 us)

commit v7 on v6

--- a/solution.py
+++ b/solution.py
@@ -130,27 +130,30 @@
     lev, quarters, _, width = w_ref.shape
     half = width // 2
     plane, core = place_ref[0], place_ref[1]
-    loads = []
-    for sibling in (0, 1):
-        column = pl.multiple_of(lax.rem(core + sibling, 2) * half, 128)
-        spots = ((0, 0, lev), (quarters - 1, 0, lev), (1, 0, lev), (2, 0, lev // 2), (2, lev // 2, lev))
+    spots = ((0, 0, lev), (quarters - 1, 0, lev), (1, 0, lev), (2, 0, lev // 2), (2, lev // 2, lev))
+
+    def loads(side, sibling):
+        out = []
         for n, (ahead, first, last) in enumerate(spots):
-            quarter = lax.rem(plane + ahead, quarters)
-            loads.append(
-                pltpu.make_async_copy(
-                    pieces[sibling * 5 + n],
-                    w_ref.at[first:last, quarter, :, pl.ds(column, half)],
-                    sem.at[sibling * 5 + n],
-                )
-            )
-    for load in loads:
-        load.start()
+            spot = w_ref.at[first:last, lax.rem(plane + ahead, quarters), :, side * half:(side + 1) * half]
+            out.append(pltpu.make_async_copy(pieces[sibling * 5 + n], spot, sem.at[side * 5 + n]))
+        return out
+
+    for own_side in (0, 1):
+
+        @pl.when(core == own_side)
+        def _():
+            for side in (0, 1):
+                for load in loads(side, 0 if side == own_side else 1):
+                    load.start()
+
     keep = pltpu.make_async_copy(w_ref, kept_ref, sem.at[10])
 
     def before(j):
-        if j == 0:
-            for load in loads:
+        if j < 2:
+            for load in loads(j, j):
                 load.wait()
+        if j == 1:
             keep.start()
 
     embed_body(x_ref, w_ref, pick_ref, bias_ref, gain_ref, norm_ref, emb_ref, normed_ref, xs_ref, sum_ref, before)
@@ -388,11 +391,28 @@
     ]
 
 
-def quarter_of_weights(w_embed, plane, lev):
-    size, half = w_embed.shape[0] // PLANES, w_embed.shape[1] // 2
-    mine = lax.dynamic_slice_in_dim(w_embed, plane * size, size, 0)
-    both = jnp.stack([mine[:, :half], mine[:, half:]], axis=0)
-    sent = jnp.broadcast_to(both[None], (lev // 2, 2, size, half)).reshape(lev, size, half)
+def spread_kernel(plane_ref, w_ref, o_ref):
+    half = o_ref.shape[2]
+    for core in (0, 1):
+        mine = w_ref[:, core * half:(core + 1) * half]
+        for chip in range(o_ref.shape[0] // 2):
+            o_ref[2 * chip + core] = mine
+
+
+def quarter_of_weights(w_embed, place, lev):
+    size, width = w_embed.shape[0] // PLANES, w_embed.shape[1]
+    sent = pl.pallas_call(
+        spread_kernel,
+        grid_spec=pltpu.PrefetchScalarGridSpec(
+            num_scalar_prefetch=1,
+            grid=(1,),
+            in_specs=[pl.BlockSpec((size, width), lambda i, plane: (plane[0], 0))],
+            out_specs=pl.BlockSpec((lev, size, width // 2), lambda i, plane: (0, 0, 0)),
+        ),
+        out_shape=jax.ShapeDtypeStruct((lev, size, width // 2), w_embed.dtype),
+        compiler_params=params(60),
+        name="spread",
+    )(place, w_embed)
     return lax.all_to_all(sent, "lev", split_axis=0, concat_axis=0, tiled=True)
 
 
@@ -435,7 +455,7 @@
     lat = lax.axis_size("lat")
     plane = lax.axis_index("lat") // (lat // PLANES)
     place = jnp.stack([plane, lax.axis_index("lev") % 2]).astype(jnp.int32)
-    own = quarter_of_weights(w_embed, plane, lev)
+    own = quarter_of_weights(w_embed, plane.astype(jnp.int32).reshape(1), lev)
     turned = jnp.transpose(fields, (0, 2, 1))
     pick = picks(level_group, lev, group_bias.shape[0])
     first_row = (lax.axis_index("lat") * rows).astype(jnp.int32).reshape(1)

time: 117 us -> 116 us (level)
  local copies, waits for them, and re-layouts: 7.03 us -> 5.37 us
  Pallas kernels: 33.5 us -> 34.8 us
    pallas_call x0 -> x1, Pallas kernels: none -> 1.75 us  [quarter_of_weights(): pl.pallas_call(spread_kernel, grid_spec=pltpu.PrefetchScalarGridSpec(num_...]
where the time goes in v7:
time: 116 us
  starting transfers between devices  47.2 us (41%)
  Pallas kernels  34.8 us (30%)
  waiting for transfers between devices  26.7 us (23%)
  local copies, waits for them, and re-layouts  5.37 us (5%)
  other arithmetic  1.31 us (1%)
    ppermute x2, starting transfers between devices, per_device(): high.append(lax.ppermute(n, 'lat', down))  15.4 us
    ppermute x2, waiting for transfers between devices, weight_pieces(): near = [lax.ppermute(own, 'lat', up), lax.ppermute(own, 'lat', down)]  9.82 us
    ppermute x2, waiting for transfers between devices, per_device(): low.append(lax.ppermute(n, 'lat', up))  8.84 us
    ppermute x2, starting transfers between devices, strips(): lax.ppermute(jnp.concatenate([t[:, :STRIP] for t in tall], axis=0), 'lev'...  8.05 us
    all_to_all x2, starting transfers between devices, per_device(): lax.all_to_all(packed[c], 'lev', split_axis=0, concat_axis=0, tiled=True)  7.4 us
    pallas_call x1, Pallas kernels, embed(): pl.pallas_call(embed_first_kernel, in_specs=[smem()] + [vmem()] * 5 + [fa...  7.33 us
    pallas_call x1, Pallas kernels, embed(): pl.pallas_call(embed_next_kernel, in_specs=[vmem()] * 5 + [far], out_spec...  7 us
    pallas_call x1, Pallas kernels, sides(): pl.pallas_call(sides_kernel, in_specs=[smem(), smem()] + [vmem()] * 9, ou...  6.47 us
  transfers between devices with their start and end apart: 20, of which 7 were waited for; matrix products, arithmetic and copies ran while one was open for 3% of the time, Pallas kernels for 23%

profile of v7, /device:TPU:2, one launch (start us, length us, event | category | flops | bytes accessed | tf_op | source)
XLA Modules:
  0.0 115.8 jit_solution(13740158106286546347)
XLA Ops:
  0.0 1.7 %spread.1 = bf16[16,48,384]{2,1,0:T(8,128)(2,1)} custom-call(s32[1]{0:T(128)} %bitcast.2.plane_ref, bf16[192,768]{1,0:T(8,128)(2,1)} %w_ref.4), custom_call_target="tpu_custom_call" | custom-call | tf_op jit(solution)/shard_map/spread/pallas_call | solution.py:404
  1.7 5.9 %all-to-all-start = ((bf16[16,48,384]{2,1,0:T(8,128)(2,1)}), bf16[16,48,384]{2,1,0:T(8,128)(2,1)S(1)}, u32[]{:S(2)}, u32[]{:S(2)}) async-start(bf16[16,48,384]{2,1,0:T(8,128)(2,1)} %spread.1), calls=%async_computation | async-start | bytes 1179648 | tf_op jit(solution)/shard_map/all_to_all | solution.py:416
  7.7 2.7 %pack.3 = bf16[16,288,128]{2,1,0:T(8,128)(2,1)} custom-call(bf16[8,192,768]{2,1,0:T(8,128)(2,1)} %bitcast.11), custom_call_target="tpu_custom_call" | custom-call | bytes 2359296 | tf_op jit(solution)/shard_map/pack/pallas_call | solution.py:65
  10.4 2.7 %pack.2 = bf16[16,288,128]{2,1,0:T(8,128)(2,1)} custom-call(bf16[8,192,768]{2,1,0:T(8,128)(2,1)} %bitcast.12), custom_call_target="tpu_custom_call" | custom-call | bytes 2359296 | tf_op jit(solution)/shard_map/pack/pallas_call | solution.py:65
  14.1 0.6 pad_add_fusion.1.place_ref
  14.7 0.6 fusion.pick_ref
  15.3 4.0 %all-to-all-done.refs_0_ = bf16[16,48,384]{2,1,0:T(8,128)(2,1)S(1)} async-done(((bf16[16,48,384]{2,1,0:T(8,128)(2,1)}), bf16[16,48,384]{2,1,0:T(8,128)(2,1)S(1)}, u32[]{:S(2)}, u32[]{:S(2)}) %all-to-all-start) | async-done | bytes 589856 | tf_op jit(solution)/shard_map/all_to_all | solution.py:416
  19.8 1.5 %collective-permute-start.1 = (bf16[16,48,384]{2,1,0:T(8,128)(2,1)S(1)}, bf16[16,48,384]{2,1,0:T(8,128)(2,1)S(1)}, u32[]{:S(2)}, u32[]{:S(2)}) collective-permute-start(bf16[16,48,384]{2,1,0:T(8,128)(2,1)S(1)} %all-to-all-done.refs_0_), channel_id=1, source_target_pairs={{0,4},{4,8},{8,12},{12,0},{1,5},{5,9},{9,13},{13,1},{2,6},{6,10},{... | collective-permute-start | bytes 1769480 | tf_op jit(solution)/shard_map/ppermute | solution.py:442
  21.3 3.7 %all-to-all-start.2 = ((bf16[16,288,128]{2,1,0:T(8,128)(2,1)}), bf16[16,288,128]{2,1,0:T(8,128)(2,1)S(1)}, u32[]{:S(2)}, u32[]{:S(2)}) async-start(bf16[16,288,128]{2,1,0:T(8,128)(2,1)} %pack.2), calls=%async_computation.2 | async-start | bytes 2359296 | tf_op jit(solution)/shard_map/all_to_all | solution.py:475
  25.3 8.6 %collective-permute-done.3.down_ref.refs_2_ = bf16[16,48,384]{2,1,0:T(8,128)(2,1)S(1)} collective-permute-done((bf16[16,48,384]{2,1,0:T(8,128)(2,1)S(1)}, bf16[16,48,384]{2,1,0:T(8,128)(2,1)S(1)}, u32[]{:S(2)}, u32[]{:S(2)}) %collective-permute-start.3) | collective-permute-done | bytes 589856 | tf_op jit(solution)/shard_map/ppermute | solution.py:442
  33.9 1.3 %collective-permute-done.1.up_ref.refs_1_ = bf16[16,48,384]{2,1,0:T(8,128)(2,1)S(1)} collective-permute-done((bf16[16,48,384]{2,1,0:T(8,128)(2,1)S(1)}, bf16[16,48,384]{2,1,0:T(8,128)(2,1)S(1)}, u32[]{:S(2)}, u32[]{:S(2)}) %collective-permute-start.1) | collective-permute-done | bytes 589856 | tf_op jit(solution)/shard_map/ppermute | solution.py:442
  35.2 0.8 copy-done.6
  36.5 2.5 %collective-permute-start.6 = (bf16[8,48,384]{2,1,0:T(8,128)(2,1)S(1)}, bf16[8,48,384]{2,1,0:T(8,128)(2,1)}, u32[]{:S(2)}, u32[]{:S(2)}) collective-permute-start(bf16[8,48,384]{2,1,0:T(8,128)(2,1)S(1)} %get-tuple-element.41), channel_id=1, source_target_pairs={{0,12},{4,0},{8,4},{12,8},{1,13},{5,1},{9,5},{13,9},{2,14},{6,2},{... | collective-permute-start | bytes 884744 | tf_op jit(solution)/shard_map/ppermute | solution.py:444
  39.0 0.8 copy-done.15
  39.8 0.8 copy-done.16
  40.7 2.4 %all-to-all-done.2.x_ref = bf16[16,288,128]{2,1,0:T(8,128)(2,1)S(1)} async-done(((bf16[16,288,128]{2,1,0:T(8,128)(2,1)}), bf16[16,288,128]{2,1,0:T(8,128)(2,1)S(1)}, u32[]{:S(2)}, u32[]{:S(2)}) %all-to-all-start.2) | async-done | bytes 1179680 | tf_op jit(solution)/shard_map/all_to_all | solution.py:475
  43.1 3.7 %all-to-all-start.1 = ((bf16[16,288,128]{2,1,0:T(8,128)(2,1)}), bf16[16,288,128]{2,1,0:T(8,128)(2,1)S(1)}, u32[]{:S(2)}, u32[]{:S(2)}) async-start(bf16[16,288,128]{2,1,0:T(8,128)(2,1)} %pack.3), calls=%async_computation.1 | async-start | bytes 2359296 | tf_op jit(solution)/shard_map/all_to_all | solution.py:475
  47.4 1.3 %collective-permute-done.7.refs_8_ = bf16[8,48,384]{2,1,0:T(8,128)(2,1)S(1)} collective-permute-done((bf16[8,48,384]{2,1,0:T(8,128)(2,1)}, bf16[8,48,384]{2,1,0:T(8,128)(2,1)S(1)}, u32[]{:S(2)}, u32[]{:S(2)}) %collective-permute-start.7) | collective-permute-done | bytes 294944 | tf_op jit(solution)/shard_map/ppermute | solution.py:447
  49.4 0.7 copy-done.18
  50.1 7.3 %embed_first.1 = (bf16[4,48,768]{2,1,0:T(8,128)(2,1)}, bf16[4,48,768]{2,1,0:T(8,128)(2,1)}, bf16[16,4,48,768]{3,2,1,0:T(8,128)(2,1)}) custom-call(s32[2]{0:T(128)} %pad_add_fusion.1.place_ref, bf16[16,288,128]{2,1,0:T(8,128)(2,1)} %copy-done.11, bf16[3,3072]{1,0:T(4,128)(2,1)} %fusion.pick_ref, f32[3,768]{1,0:T(4,128)} %bias_ref.3, f32[3,768]{1,0:T(4,128)} %gain_ref.3, ...), custom_call_target="tpu_custom_call" | custom-call | flops 16000000000 | bytes 5898240 | tf_op jit(solution)/shard_map/embed_first/pallas_call | solution.py:195
  57.4 8.9 %collective-permute-start.12 = (bf16[4,48,768]{2,1,0:T(8,128)(2,1)}, bf16[4,48,768]{2,1,0:T(8,128)(2,1)S(1)}, u32[]{:S(2)}, u32[]{:S(2)}) collective-permute-start(bf16[4,48,768]{2,1,0:T(8,128)(2,1)} %get-tuple-element.47.own0_ref), channel_id=1, source_target_pairs={{1,0},{2,1},{3,2},{4,3},{5,4},{6,5},{7,6},{8,7},{9,8},{10,9},{11,1... | collective-permute-start | bytes 884744 | tf_op jit(solution)/shard_map/ppermute | solution.py:484
  66.3 2.1 %collective-permute-start.11 = (bf16[4,48,768]{2,1,0:T(8,128)(2,1)}, bf16[4,48,768]{2,1,0:T(8,128)(2,1)S(1)}, u32[]{:S(2)}, u32[]{:S(2)}) collective-permute-start(bf16[4,48,768]{2,1,0:T(8,128)(2,1)} %get-tuple-element.47.own0_ref), channel_id=1, source_target_pairs={{0,1},{1,2},{2,3},{3,4},{4,5},{5,6},{6,7},{7,8},{8,9},{9,10},{10,1... | collective-permute-start | bytes 884744 | tf_op jit(solution)/shard_map/ppermute | solution.py:483
  68.4 0.8 fusion.4
  69.3 7.0 %embed_next.1 = (bf16[4,48,768]{2,1,0:T(8,128)(2,1)S(1)}, bf16[4,48,768]{2,1,0:T(8,128)(2,1)S(1)}) custom-call(bf16[16,288,128]{2,1,0:T(8,128)(2,1)S(1)} %all-to-all-done.1.x_ref, bf16[3,3072]{1,0:T(4,128)(2,1)S(1)} %copy-done.1, f32[3,768]{1,0:T(4,128)S(1)} %copy-done.7, f32[3,768]{1,0:T(4,128)S(1)} %copy-done.8, f32[1,768]{1,0:T(1,128)S(1)} %copy-done.2, ...), custom_call_target="tpu_custom_call" | custom-call | flops 2717908992 | bytes 5898240 | tf_op jit(solution)/shard_map/embed_next/pallas_call | solution.py:205
  76.3 2.3 %collective-permute-start.10 = (bf16[4,48,768]{2,1,0:T(8,128)(2,1)S(1)}, bf16[4,48,768]{2,1,0:T(8,128)(2,1)S(1)}, u32[]{:S(2)}, u32[]{:S(2)}) collective-permute-start(bf16[4,48,768]{2,1,0:T(8,128)(2,1)S(1)} %get-tuple-element.48.own1_ref), channel_id=1, source_target_pairs={{0,1},{1,2},{2,3},{3,4},{4,5},{5,6},{6,7},{7,8},{8,9},{9,10},{10,1... | collective-permute-start | bytes 884744 | tf_op jit(solution)/shard_map/ppermute | solution.py:487
  78.6 6.5 %collective-permute-start.9 = (bf16[4,48,768]{2,1,0:T(8,128)(2,1)S(1)}, bf16[4,48,768]{2,1,0:T(8,128)(2,1)S(1)}, u32[]{:S(2)}, u32[]{:S(2)}) collective-permute-start(bf16[4,48,768]{2,1,0:T(8,128)(2,1)S(1)} %get-tuple-element.48.own1_ref), channel_id=1, source_target_pairs={{1,0},{2,1},{3,2},{4,3},{5,4},{6,5},{7,6},{8,7},{9,8},{10,9},{11,1... | collective-permute-start | bytes 884744 | tf_op jit(solution)/shard_map/ppermute | solution.py:486
  85.2 8.8 %collective-permute-done.11.low_ref = bf16[4,48,768]{2,1,0:T(8,128)(2,1)S(1)} collective-permute-done((bf16[4,48,768]{2,1,0:T(8,128)(2,1)}, bf16[4,48,768]{2,1,0:T(8,128)(2,1)S(1)}, u32[]{:S(2)}, u32[]{:S(2)}) %collective-permute-start.11) | collective-permute-done | bytes 294944 | tf_op jit(solution)/shard_map/ppermute | solution.py:483
  94.3 3.9 %collective-permute-start.14 = (bf16[16,8,768]{2,1,0:T(8,128)(2,1)S(1)}, bf16[16,8,768]{2,1,0:T(8,128)(2,1)S(1)}, u32[]{:S(2)}, u32[]{:S(2)}) collective-permute-start(bf16[16,8,768]{2,1,0:T(8,128)(2,1)S(1)} %pad_maximum_fusion.1), channel_id=1, source_target_pairs={{16,0},{32,16},{48,32},{64,48},{80,64},{96,80},{112,96},{128,112},... | collective-permute-start | bytes 589832 | tf_op jit(solution)/shard_map/ppermute | solution.py:491
  98.2 2.5 %project.1 = (bf16[3,128,768]{2,1,0:T(8,128)(2,1)S(1)}, bf16[24,64,1536]{2,1,0:T(8,128)(2,1)S(1)}) custom-call(bf16[4,48,768]{2,1,0:T(8,128)(2,1)S(1)} %copy-done, bf16[4,48,768]{2,1,0:T(8,128)(2,1)S(1)} %get-tuple-element.48.own1_ref, bf16[4,48,768]{2,1,0:T(8,128)(2,1)S(1)} %collective-permute-done.11.low_ref, ...), custom_call_target="tpu_custom_call" | custom-call | flops 2264924160 | bytes 7077888 | tf_op jit(solution)/shard_map/project/pallas_call | solution.py:252
  100.9 4.1 %collective-permute-start.16 = (bf16[8,8,768]{2,1,0:T(8,128)(2,1)S(1)}, bf16[8,8,768]{2,1,0:T(8,128)(2,1)S(1)}, u32[]{:S(2)}, u32[]{:S(2)}) collective-permute-start(bf16[8,8,768]{2,1,0:T(8,128)(2,1)S(1)} %pad_maximum_fusion.3), channel_id=1, source_target_pairs={{16,0},{32,16},{48,32},{64,48},{80,64},{96,80},{112,96},{128,112},... | collective-permute-start | bytes 294920 | tf_op jit(solution)/shard_map/ppermute | solution.py:491
  105.0 4.3 %middle.1 = (bf16[24,64,1536]{2,1,0:T(8,128)(2,1)S(1)}, bf16[8,16,768]{2,1,0:T(8,128)(2,1)S(1)}) custom-call(s32[128]{0:T(128)S(1)} %copy-done.9, s32[1]{0:T(128)} %bitcast.first_ref, bf16[3,128,768]{2,1,0:T(8,128)(2,1)S(1)} %get-tuple-element.52.q_ref, bf16[24,64,1536]{2,1,0:T(8,128)(2,1)S(1)} %get-tuple-element.53._, ...), custom_call_target="tpu_custom_call", output_to_operand_aliasing={{0}: (3, {})} | custom-call | flops 8000000000 | bytes 10000000 | tf_op jit(solution)/shard_map/middle/pallas_call | solution.py:337
  109.4 6.5 %sides.1 = (bf16[8,48,768]{2,1,0:T(8,128)(2,1)}, bf16[24,64,1536]{2,1,0:T(8,128)(2,1)S(1)}) custom-call(s32[128]{0:T(128)S(1)} %copy-done.9, s32[1]{0:T(128)} %bitcast.first_ref, bf16[3,128,768]{2,1,0:T(8,128)(2,1)S(1)} %get-tuple-element.52.q_ref, bf16[24,64,1536]{2,1,0:T(8,128)(2,1)S(1)} %get-tuple-element.58._, ...), custom_call_target="tpu_custom_call", output_to_operand_aliasing={{1}: (3, {})} | custom-call | flops 8999999488 | bytes 10000000 | tf_op jit(solution)/shard_map/sides/pallas_call | solution.py:373
  (75 shorter events, 4.0 us)
Async XLA Ops:
  1.7 17.5 %all-to-all-start = ((bf16[16,48,384]{2,1,0:T(8,128)(2,1)}), bf16[16,48,384]{2,1,0:T(8,128)(2,1)S(1)}, u32[]{:S(2)}, u32[]{:S(2)}) async-start(bf16[16,48,384]{2,1,0:T(8,128)(2,1)} %spread.1), calls=%async_computation | async-start | bytes 1179648 | tf_op jit(solution)/shard_map/all_to_all | solution.py:416
  10.4 3.3 %copy-start.14 = (s32[128]{0:T(128)S(1)}, s32[128]{0:T(128)}, u32[]{:S(2)}) copy-start(s32[128]{0:T(128)} %param.10) | copy-start | bytes 1540
  19.3 15.9 %copy-start.12 = (bf16[16,48,384]{2,1,0:T(8,128)(2,1)}, bf16[16,48,384]{2,1,0:T(8,128)(2,1)S(1)}, u32[]{:S(2)}) copy-start(bf16[16,48,384]{2,1,0:T(8,128)(2,1)S(1)} %all-to-all-done.refs_0_) | copy-start | bytes 1769476
  19.3 14.6 %collective-permute-start.3 = (bf16[16,48,384]{2,1,0:T(8,128)(2,1)S(1)}, bf16[16,48,384]{2,1,0:T(8,128)(2,1)S(1)}, u32[]{:S(2)}, u32[]{:S(2)}) collective-permute-start(bf16[16,48,384]{2,1,0:T(8,128)(2,1)S(1)} %all-to-all-done.refs_0_), channel_id=1, source_target_pairs={{0,12},{4,0},{8,4},{12,8},{1,13},{5,1},{9,5},{13,9},{2,14},{6,2},{... | collective-permute-start | bytes 1769480 | tf_op jit(solution)/shard_map/ppermute | solution.py:442
  19.8 15.3 %collective-permute-start.1 = (bf16[16,48,384]{2,1,0:T(8,128)(2,1)S(1)}, bf16[16,48,384]{2,1,0:T(8,128)(2,1)S(1)}, u32[]{:S(2)}, u32[]{:S(2)}) collective-permute-start(bf16[16,48,384]{2,1,0:T(8,128)(2,1)S(1)} %all-to-all-done.refs_0_), channel_id=1, source_target_pairs={{0,4},{4,8},{8,12},{12,0},{1,5},{5,9},{9,13},{13,1},{2,6},{6,10},{... | collective-permute-start | bytes 1769480 | tf_op jit(solution)/shard_map/ppermute | solution.py:442
  21.3 21.7 %all-to-all-start.2 = ((bf16[16,288,128]{2,1,0:T(8,128)(2,1)}), bf16[16,288,128]{2,1,0:T(8,128)(2,1)S(1)}, u32[]{:S(2)}, u32[]{:S(2)}) async-start(bf16[16,288,128]{2,1,0:T(8,128)(2,1)} %pack.2), calls=%async_computation.2 | async-start | bytes 2359296 | tf_op jit(solution)/shard_map/all_to_all | solution.py:475
  25.0 13.9 %collective-permute-start = (bf16[16,48,384]{2,1,0:T(8,128)(2,1)S(1)}, bf16[16,48,384]{2,1,0:T(8,128)(2,1)S(1)}, u32[]{:S(2)}, u32[]{:S(2)}) collective-permute-start(bf16[16,48,384]{2,1,0:T(8,128)(2,1)S(1)} %all-to-all-done.refs_0_), channel_id=1, source_target_pairs={{0,16},{16,0},{32,48},{48,32},{64,80},{80,64},{96,112},{112,96},{1... | collective-permute-start | bytes 1769480 | tf_op jit(solution)/shard_map/ppermute | solution.py:447
  33.9 5.1 %collective-permute-start.4 = (bf16[16,48,384]{2,1,0:T(8,128)(2,1)S(1)}, bf16[16,48,384]{2,1,0:T(8,128)(2,1)S(1)}, u32[]{:S(2)}, u32[]{:S(2)}) collective-permute-start(bf16[16,48,384]{2,1,0:T(8,128)(2,1)S(1)} %collective-permute-done.3.down_ref.refs_2_), channel_id=1, source_target_pairs={{0,16},{16,0},{32,48},{48,32},{64,80},{80,64},{96,112},{112,96},{1... | collective-permute-start | bytes 1769480 | tf_op jit(solution)/shard_map/ppermute | solution.py:447
  35.1 5.5 %collective-permute-start.2 = (bf16[16,48,384]{2,1,0:T(8,128)(2,1)S(1)}, bf16[16,48,384]{2,1,0:T(8,128)(2,1)}, u32[]{:S(2)}, u32[]{:S(2)}) collective-permute-start(bf16[16,48,384]{2,1,0:T(8,128)(2,1)S(1)} %collective-permute-done.1.up_ref.refs_1_), channel_id=1, source_target_pairs={{0,16},{16,0},{32,48},{48,32},{64,80},{80,64},{96,112},{112,96},{1... | collective-permute-start | bytes 1769480 | tf_op jit(solution)/shard_map/ppermute | solution.py:447
  36.0 10.8 %collective-permute-start.5 = (bf16[8,48,384]{2,1,0:T(8,128)(2,1)S(1)}, bf16[8,48,384]{2,1,0:T(8,128)(2,1)}, u32[]{:S(2)}, u32[]{:S(2)}) collective-permute-start(bf16[8,48,384]{2,1,0:T(8,128)(2,1)S(1)} %get-tuple-element.40), channel_id=1, source_target_pairs={{0,4},{4,8},{8,12},{12,0},{1,5},{5,9},{9,13},{13,1},{2,6},{6,10},{... | collective-permute-start | bytes 884744 | tf_op jit(solution)/shard_map/ppermute | solution.py:444
  36.5 10.7 %collective-permute-start.6 = (bf16[8,48,384]{2,1,0:T(8,128)(2,1)S(1)}, bf16[8,48,384]{2,1,0:T(8,128)(2,1)}, u32[]{:S(2)}, u32[]{:S(2)}) collective-permute-start(bf16[8,48,384]{2,1,0:T(8,128)(2,1)S(1)} %get-tuple-element.41), channel_id=1, source_target_pairs={{0,12},{4,0},{8,4},{12,8},{1,13},{5,1},{9,5},{13,9},{2,14},{6,2},{... | collective-permute-start | bytes 884744 | tf_op jit(solution)/shard_map/ppermute | solution.py:444
  43.1 6.0 %copy-start.11 = (bf16[16,288,128]{2,1,0:T(8,128)(2,1)}, bf16[16,288,128]{2,1,0:T(8,128)(2,1)S(1)}, u32[]{:S(2)}) copy-start(bf16[16,288,128]{2,1,0:T(8,128)(2,1)S(1)} %all-to-all-done.2.x_ref) | copy-start | bytes 3538948
  43.1 26.2 %all-to-all-start.1 = ((bf16[16,288,128]{2,1,0:T(8,128)(2,1)}), bf16[16,288,128]{2,1,0:T(8,128)(2,1)S(1)}, u32[]{:S(2)}, u32[]{:S(2)}) async-start(bf16[16,288,128]{2,1,0:T(8,128)(2,1)} %pack.3), calls=%async_computation.1 | async-start | bytes 2359296 | tf_op jit(solution)/shard_map/all_to_all | solution.py:475
  46.8 1.9 %collective-permute-start.7 = (bf16[8,48,384]{2,1,0:T(8,128)(2,1)}, bf16[8,48,384]{2,1,0:T(8,128)(2,1)S(1)}, u32[]{:S(2)}, u32[]{:S(2)}) collective-permute-start(bf16[8,48,384]{2,1,0:T(8,128)(2,1)} %collective-permute-done.5.refs_3_), channel_id=1, source_target_pairs={{0,16},{16,0},{32,48},{48,32},{64,80},{80,64},{96,112},{112,96},{1... | collective-permute-start | bytes 884744 | tf_op jit(solution)/shard_map/ppermute | solution.py:447
  47.2 1.9 %collective-permute-start.8 = (bf16[8,48,384]{2,1,0:T(8,128)(2,1)}, bf16[8,48,384]{2,1,0:T(8,128)(2,1)S(1)}, u32[]{:S(2)}, u32[]{:S(2)}) collective-permute-start(bf16[8,48,384]{2,1,0:T(8,128)(2,1)} %collective-permute-done.6.refs_4_), channel_id=1, source_target_pairs={{0,16},{16,0},{32,48},{48,32},{64,80},{80,64},{96,112},{112,96},{1... | collective-permute-start | bytes 884744 | tf_op jit(solution)/shard_map/ppermute | solution.py:447
  47.4 21.9 %copy-start.1 = (bf16[3,3072]{1,0:T(4,128)(2,1)S(1)}, bf16[3,3072]{1,0:T(4,128)(2,1)}, u32[]{:S(2)}) copy-start(bf16[3,3072]{1,0:T(4,128)(2,1)} %fusion.pick_ref) | copy-start | bytes 55300
  47.4 21.9 %copy-start.2 = (f32[1,768]{1,0:T(1,128)S(1)}, f32[1,768]{1,0:T(1,128)}, u32[]{:S(2)}) copy-start(f32[1,768]{1,0:T(1,128)} %broadcast_in_dim.14.norm_ref) | copy-start | bytes 9220
  47.4 21.9 %copy-start.7 = (f32[3,768]{1,0:T(4,128)S(1)}, f32[3,768]{1,0:T(4,128)}, u32[]{:S(2)}) copy-start(f32[3,768]{1,0:T(4,128)} %bias_ref.3) | copy-start | bytes 27652
  47.4 21.9 %copy-start.8 = (f32[3,768]{1,0:T(4,128)S(1)}, f32[3,768]{1,0:T(4,128)}, u32[]{:S(2)}) copy-start(f32[3,768]{1,0:T(4,128)} %gain_ref.3) | copy-start | bytes 27652
  57.4 27.8 %collective-permute-start.12 = (bf16[4,48,768]{2,1,0:T(8,128)(2,1)}, bf16[4,48,768]{2,1,0:T(8,128)(2,1)S(1)}, u32[]{:S(2)}, u32[]{:S(2)}) collective-permute-start(bf16[4,48,768]{2,1,0:T(8,128)(2,1)} %get-tuple-element.47.own0_ref), channel_id=1, source_target_pairs={{1,0},{2,1},{3,2},{4,3},{5,4},{6,5},{7,6},{8,7},{9,8},{10,9},{11,1... | collective-permute-start | bytes 884744 | tf_op jit(solution)/shard_map/ppermute | solution.py:484
  66.3 27.7 %collective-permute-start.11 = (bf16[4,48,768]{2,1,0:T(8,128)(2,1)}, bf16[4,48,768]{2,1,0:T(8,128)(2,1)S(1)}, u32[]{:S(2)}, u32[]{:S(2)}) collective-permute-start(bf16[4,48,768]{2,1,0:T(8,128)(2,1)} %get-tuple-element.47.own0_ref), channel_id=1, source_target_pairs={{0,1},{1,2},{2,3},{3,4},{4,5},{5,6},{6,7},{7,8},{8,9},{9,10},{10,1... | collective-permute-start | bytes 884744 | tf_op jit(solution)/shard_map/ppermute | solution.py:483
  69.3 28.9 %copy-start = (bf16[4,48,768]{2,1,0:T(8,128)(2,1)S(1)}, bf16[4,48,768]{2,1,0:T(8,128)(2,1)}, u32[]{:S(2)}) copy-start(bf16[4,48,768]{2,1,0:T(8,128)(2,1)} %get-tuple-element.47.own0_ref) | copy-start | bytes 884740
  69.3 28.9 %copy-start.3 = (bf16[768,2304]{1,0:T(8,128)(2,1)S(1)}, bf16[768,2304]{1,0:T(8,128)(2,1)}, u32[]{:S(2)}) copy-start(bf16[768,2304]{1,0:T(8,128)(2,1)} %w_ref.7) | copy-start | bytes 10616836
  76.3 24.4 %collective-permute-start.10 = (bf16[4,48,768]{2,1,0:T(8,128)(2,1)S(1)}, bf16[4,48,768]{2,1,0:T(8,128)(2,1)S(1)}, u32[]{:S(2)}, u32[]{:S(2)}) collective-permute-start(bf16[4,48,768]{2,1,0:T(8,128)(2,1)S(1)} %get-tuple-element.48.own1_ref), channel_id=1, source_target_pairs={{0,1},{1,2},{2,3},{3,4},{4,5},{5,6},{6,7},{7,8},{8,9},{9,10},{10,1... | collective-permute-start | bytes 884744 | tf_op jit(solution)/shard_map/ppermute | solution.py:487
  78.6 22.1 %collective-permute-start.9 = (bf16[4,48,768]{2,1,0:T(8,128)(2,1)S(1)}, bf16[4,48,768]{2,1,0:T(8,128)(2,1)S(1)}, u32[]{:S(2)}, u32[]{:S(2)}) collective-permute-start(bf16[4,48,768]{2,1,0:T(8,128)(2,1)S(1)} %get-tuple-element.48.own1_ref), channel_id=1, source_target_pairs={{1,0},{2,1},{3,2},{4,3},{5,4},{6,5},{7,6},{8,7},{9,8},{10,9},{11,1... | collective-permute-start | bytes 884744 | tf_op jit(solution)/shard_map/ppermute | solution.py:486
  94.1 10.9 %collective-permute-start.13 = (bf16[16,8,768]{2,1,0:T(8,128)(2,1)S(1)}, bf16[16,8,768]{2,1,0:T(8,128)(2,1)S(1)}, u32[]{:S(2)}, u32[]{:S(2)}) collective-permute-start(bf16[16,8,768]{2,1,0:T(8,128)(2,1)S(1)} %pad_maximum_fusion), channel_id=1, source_target_pairs={{0,16},{16,32},{32,48},{48,64},{64,80},{80,96},{96,112},{112,128},... | collective-permute-start | bytes 589832 | tf_op jit(solution)/shard_map/ppermute | solution.py:490
  94.2 10.8 %copy-start.4 = (bf16[768,768]{1,0:T(8,128)(2,1)S(1)}, bf16[768,768]{1,0:T(8,128)(2,1)}, u32[]{:S(2)}) copy-start(bf16[768,768]{1,0:T(8,128)(2,1)} %wout_ref.3) | copy-start | bytes 3538948
  94.2 10.8 %copy-start.9 = (s32[128]{0:T(128)S(1)}, s32[128]{0:T(128)}, u32[]{:S(2)}) copy-start(s32[128]{0:T(128)} %start_ref.3) | copy-start | bytes 1540
  94.2 10.8 %copy-start.10 = (bf16[4,48,768]{2,1,0:T(8,128)(2,1)S(1)}, bf16[4,48,768]{2,1,0:T(8,128)(2,1)}, u32[]{:S(2)}) copy-start(bf16[4,48,768]{2,1,0:T(8,128)(2,1)} %get-tuple-element.56.emb0_ref) | copy-start | bytes 884740
  94.3 10.7 %collective-permute-start.14 = (bf16[16,8,768]{2,1,0:T(8,128)(2,1)S(1)}, bf16[16,8,768]{2,1,0:T(8,128)(2,1)S(1)}, u32[]{:S(2)}, u32[]{:S(2)}) collective-permute-start(bf16[16,8,768]{2,1,0:T(8,128)(2,1)S(1)} %pad_maximum_fusion.1), channel_id=1, source_target_pairs={{16,0},{32,16},{48,32},{64,48},{80,64},{96,80},{112,96},{128,112},... | collective-permute-start | bytes 589832 | tf_op jit(solution)/shard_map/ppermute | solution.py:491
  100.8 8.6 %collective-permute-start.15 = (bf16[8,8,768]{2,1,0:T(8,128)(2,1)S(1)}, bf16[8,8,768]{2,1,0:T(8,128)(2,1)S(1)}, u32[]{:S(2)}, u32[]{:S(2)}) collective-permute-start(bf16[8,8,768]{2,1,0:T(8,128)(2,1)S(1)} %pad_maximum_fusion.2), channel_id=1, source_target_pairs={{0,16},{16,32},{32,48},{48,64},{64,80},{80,96},{96,112},{112,128},... | collective-permute-start | bytes 294920 | tf_op jit(solution)/shard_map/ppermute | solution.py:490
  100.9 8.5 %collective-permute-start.16 = (bf16[8,8,768]{2,1,0:T(8,128)(2,1)S(1)}, bf16[8,8,768]{2,1,0:T(8,128)(2,1)S(1)}, u32[]{:S(2)}, u32[]{:S(2)}) collective-permute-start(bf16[8,8,768]{2,1,0:T(8,128)(2,1)S(1)} %pad_maximum_fusion.3), channel_id=1, source_target_pairs={{16,0},{32,16},{48,32},{64,48},{80,64},{96,80},{112,96},{128,112},... | collective-permute-start | bytes 294920 | tf_op jit(solution)/shard_map/ppermute | solution.py:491
  (7 other events, 8.0 us)

commit v8 on v7

--- a/solution.py
+++ b/solution.py
@@ -392,9 +392,10 @@
 
 
 def spread_kernel(plane_ref, w_ref, o_ref):
-    half = o_ref.shape[2]
+    size, half = o_ref.shape[1:]
+    rows = pl.ds(pl.multiple_of(plane_ref[0] * size, size), size)
     for core in (0, 1):
-        mine = w_ref[:, core * half:(core + 1) * half]
+        mine = w_ref[rows, core * half:(core + 1) * half]
         for chip in range(o_ref.shape[0] // 2):
             o_ref[2 * chip + core] = mine
 
@@ -403,12 +404,8 @@
     size, width = w_embed.shape[0] // PLANES, w_embed.shape[1]
     sent = pl.pallas_call(
         spread_kernel,
-        grid_spec=pltpu.PrefetchScalarGridSpec(
-            num_scalar_prefetch=1,
-            grid=(1,),
-            in_specs=[pl.BlockSpec((size, width), lambda i, plane: (plane[0], 0))],
-            out_specs=pl.BlockSpec((lev, size, width // 2), lambda i, plane: (0, 0, 0)),
-        ),
+        in_specs=[smem(), vmem()],
+        out_specs=vmem(),
         out_shape=jax.ShapeDtypeStruct((lev, size, width // 2), w_embed.dtype),
         compiler_params=params(60),
         name="spread",

time: 116 us -> 117 us (level)
  no operation moved by 1% of the time
where the time goes in v8:
time: 117 us; the launch traced here: 116 us
  starting transfers between devices  47.2 us (40%)
  Pallas kernels  34.9 us (30%)
  waiting for transfers between devices  26.7 us (23%)
  local copies, waits for them, and re-layouts  5.37 us (5%)
  other arithmetic  1.31 us (1%)
    ppermute x2, starting transfers between devices, per_device(): high.append(lax.ppermute(n, 'lat', down))  15.4 us
    ppermute x2, waiting for transfers between devices, weight_pieces(): near = [lax.ppermute(own, 'lat', up), lax.ppermute(own, 'lat', down)]  9.82 us
    ppermute x2, waiting for transfers between devices, per_device(): low.append(lax.ppermute(n, 'lat', up))  8.84 us
    ppermute x2, starting transfers between devices, strips(): lax.ppermute(jnp.concatenate([t[:, :STRIP] for t in tall], axis=0), 'lev'...  8.05 us
    all_to_all x2, starting transfers between devices, per_device(): lax.all_to_all(packed[c], 'lev', split_axis=0, concat_axis=0, tiled=True)  7.4 us
    pallas_call x1, Pallas kernels, embed(): pl.pallas_call(embed_first_kernel, in_specs=[smem()] + [vmem()] * 5 + [fa...  7.33 us
    pallas_call x1, Pallas kernels, embed(): pl.pallas_call(embed_next_kernel, in_specs=[vmem()] * 5 + [far], out_spec...  7 us
    pallas_call x1, Pallas kernels, sides(): pl.pallas_call(sides_kernel, in_specs=[smem(), smem()] + [vmem()] * 9, ou...  6.47 us
  transfers between devices with their start and end apart: 20, of which 7 were waited for; matrix products, arithmetic and copies ran while one was open for 3% of the time, Pallas kernels for 23%

profile of v8, /device:TPU:2, one launch (start us, length us, event | category | flops | bytes accessed | tf_op | source)
XLA Modules:
  0.0 115.9 jit_solution(11047634424782341981)
XLA Ops:
  0.0 1.8 %spread.1 = bf16[16,48,384]{2,1,0:T(8,128)(2,1)} custom-call(s32[1]{0:T(128)} %bitcast.2.plane_ref, bf16[192,768]{1,0:T(8,128)(2,1)} %w_ref.4), custom_call_target="tpu_custom_call" | custom-call | tf_op jit(solution)/shard_map/spread/pallas_call | solution.py:405
  1.8 5.9 %all-to-all-start = ((bf16[16,48,384]{2,1,0:T(8,128)(2,1)}), bf16[16,48,384]{2,1,0:T(8,128)(2,1)S(1)}, u32[]{:S(2)}, u32[]{:S(2)}) async-start(bf16[16,48,384]{2,1,0:T(8,128)(2,1)} %spread.1), calls=%async_computation | async-start | bytes 1179648 | tf_op jit(solution)/shard_map/all_to_all | solution.py:413
  7.8 2.7 %pack.3 = bf16[16,288,128]{2,1,0:T(8,128)(2,1)} custom-call(bf16[8,192,768]{2,1,0:T(8,128)(2,1)} %bitcast.11), custom_call_target="tpu_custom_call" | custom-call | bytes 2359296 | tf_op jit(solution)/shard_map/pack/pallas_call | solution.py:65
  10.5 2.7 %pack.2 = bf16[16,288,128]{2,1,0:T(8,128)(2,1)} custom-call(bf16[8,192,768]{2,1,0:T(8,128)(2,1)} %bitcast.12), custom_call_target="tpu_custom_call" | custom-call | bytes 2359296 | tf_op jit(solution)/shard_map/pack/pallas_call | solution.py:65
  14.2 0.6 pad_add_fusion.1.place_ref
  14.8 0.6 fusion.pick_ref
  15.4 4.0 %all-to-all-done.refs_0_ = bf16[16,48,384]{2,1,0:T(8,128)(2,1)S(1)} async-done(((bf16[16,48,384]{2,1,0:T(8,128)(2,1)}), bf16[16,48,384]{2,1,0:T(8,128)(2,1)S(1)}, u32[]{:S(2)}, u32[]{:S(2)}) %all-to-all-start) | async-done | bytes 589856 | tf_op jit(solution)/shard_map/all_to_all | solution.py:413
  19.9 1.5 %collective-permute-start.1 = (bf16[16,48,384]{2,1,0:T(8,128)(2,1)S(1)}, bf16[16,48,384]{2,1,0:T(8,128)(2,1)S(1)}, u32[]{:S(2)}, u32[]{:S(2)}) collective-permute-start(bf16[16,48,384]{2,1,0:T(8,128)(2,1)S(1)} %all-to-all-done.refs_0_), channel_id=1, source_target_pairs={{0,4},{4,8},{8,12},{12,0},{1,5},{5,9},{9,13},{13,1},{2,6},{6,10},{... | collective-permute-start | bytes 1769480 | tf_op jit(solution)/shard_map/ppermute | solution.py:439
  21.4 3.7 %all-to-all-start.2 = ((bf16[16,288,128]{2,1,0:T(8,128)(2,1)}), bf16[16,288,128]{2,1,0:T(8,128)(2,1)S(1)}, u32[]{:S(2)}, u32[]{:S(2)}) async-start(bf16[16,288,128]{2,1,0:T(8,128)(2,1)} %pack.2), calls=%async_computation.2 | async-start | bytes 2359296 | tf_op jit(solution)/shard_map/all_to_all | solution.py:472
  25.4 8.6 %collective-permute-done.3.down_ref.refs_2_ = bf16[16,48,384]{2,1,0:T(8,128)(2,1)S(1)} collective-permute-done((bf16[16,48,384]{2,1,0:T(8,128)(2,1)S(1)}, bf16[16,48,384]{2,1,0:T(8,128)(2,1)S(1)}, u32[]{:S(2)}, u32[]{:S(2)}) %collective-permute-start.3) | collective-permute-done | bytes 589856 | tf_op jit(solution)/shard_map/ppermute | solution.py:439
  34.0 1.3 %collective-permute-done.1.up_ref.refs_1_ = bf16[16,48,384]{2,1,0:T(8,128)(2,1)S(1)} collective-permute-done((bf16[16,48,384]{2,1,0:T(8,128)(2,1)S(1)}, bf16[16,48,384]{2,1,0:T(8,128)(2,1)S(1)}, u32[]{:S(2)}, u32[]{:S(2)}) %collective-permute-start.1) | collective-permute-done | bytes 589856 | tf_op jit(solution)/shard_map/ppermute | solution.py:439
  35.3 0.8 copy-done.6
  36.6 2.5 %collective-permute-start.6 = (bf16[8,48,384]{2,1,0:T(8,128)(2,1)S(1)}, bf16[8,48,384]{2,1,0:T(8,128)(2,1)}, u32[]{:S(2)}, u32[]{:S(2)}) collective-permute-start(bf16[8,48,384]{2,1,0:T(8,128)(2,1)S(1)} %get-tuple-element.41), channel_id=1, source_target_pairs={{0,12},{4,0},{8,4},{12,8},{1,13},{5,1},{9,5},{13,9},{2,14},{6,2},{... | collective-permute-start | bytes 884744 | tf_op jit(solution)/shard_map/ppermute | solution.py:441
  39.1 0.8 copy-done.15
  39.9 0.8 copy-done.16
  40.7 2.4 %all-to-all-done.2.x_ref = bf16[16,288,128]{2,1,0:T(8,128)(2,1)S(1)} async-done(((bf16[16,288,128]{2,1,0:T(8,128)(2,1)}), bf16[16,288,128]{2,1,0:T(8,128)(2,1)S(1)}, u32[]{:S(2)}, u32[]{:S(2)}) %all-to-all-start.2) | async-done | bytes 1179680 | tf_op jit(solution)/shard_map/all_to_all | solution.py:472
  43.1 3.7 %all-to-all-start.1 = ((bf16[16,288,128]{2,1,0:T(8,128)(2,1)}), bf16[16,288,128]{2,1,0:T(8,128)(2,1)S(1)}, u32[]{:S(2)}, u32[]{:S(2)}) async-start(bf16[16,288,128]{2,1,0:T(8,128)(2,1)} %pack.3), calls=%async_computation.1 | async-start | bytes 2359296 | tf_op jit(solution)/shard_map/all_to_all | solution.py:472
  47.5 1.3 %collective-permute-done.7.refs_8_ = bf16[8,48,384]{2,1,0:T(8,128)(2,1)S(1)} collective-permute-done((bf16[8,48,384]{2,1,0:T(8,128)(2,1)}, bf16[8,48,384]{2,1,0:T(8,128)(2,1)S(1)}, u32[]{:S(2)}, u32[]{:S(2)}) %collective-permute-start.7) | collective-permute-done | bytes 294944 | tf_op jit(solution)/shard_map/ppermute | solution.py:444
  49.4 0.7 copy-done.18
  50.1 7.3 %embed_first.1 = (bf16[4,48,768]{2,1,0:T(8,128)(2,1)}, bf16[4,48,768]{2,1,0:T(8,128)(2,1)}, bf16[16,4,48,768]{3,2,1,0:T(8,128)(2,1)}) custom-call(s32[2]{0:T(128)} %pad_add_fusion.1.place_ref, bf16[16,288,128]{2,1,0:T(8,128)(2,1)} %copy-done.11, bf16[3,3072]{1,0:T(4,128)(2,1)} %fusion.pick_ref, f32[3,768]{1,0:T(4,128)} %bias_ref.3, f32[3,768]{1,0:T(4,128)} %gain_ref.3, ...), custom_call_target="tpu_custom_call" | custom-call | flops 16000000000 | bytes 5898240 | tf_op jit(solution)/shard_map/embed_first/pallas_call | solution.py:195
  57.5 8.9 %collective-permute-start.12 = (bf16[4,48,768]{2,1,0:T(8,128)(2,1)}, bf16[4,48,768]{2,1,0:T(8,128)(2,1)S(1)}, u32[]{:S(2)}, u32[]{:S(2)}) collective-permute-start(bf16[4,48,768]{2,1,0:T(8,128)(2,1)} %get-tuple-element.47.own0_ref), channel_id=1, source_target_pairs={{1,0},{2,1},{3,2},{4,3},{5,4},{6,5},{7,6},{8,7},{9,8},{10,9},{11,1... | collective-permute-start | bytes 884744 | tf_op jit(solution)/shard_map/ppermute | solution.py:481
  66.4 2.1 %collective-permute-start.11 = (bf16[4,48,768]{2,1,0:T(8,128)(2,1)}, bf16[4,48,768]{2,1,0:T(8,128)(2,1)S(1)}, u32[]{:S(2)}, u32[]{:S(2)}) collective-permute-start(bf16[4,48,768]{2,1,0:T(8,128)(2,1)} %get-tuple-element.47.own0_ref), channel_id=1, source_target_pairs={{0,1},{1,2},{2,3},{3,4},{4,5},{5,6},{6,7},{7,8},{8,9},{9,10},{10,1... | collective-permute-start | bytes 884744 | tf_op jit(solution)/shard_map/ppermute | solution.py:480
  68.5 0.8 fusion.4
  69.4 7.0 %embed_next.1 = (bf16[4,48,768]{2,1,0:T(8,128)(2,1)S(1)}, bf16[4,48,768]{2,1,0:T(8,128)(2,1)S(1)}) custom-call(bf16[16,288,128]{2,1,0:T(8,128)(2,1)S(1)} %all-to-all-done.1.x_ref, bf16[3,3072]{1,0:T(4,128)(2,1)S(1)} %copy-done.1, f32[3,768]{1,0:T(4,128)S(1)} %copy-done.7, f32[3,768]{1,0:T(4,128)S(1)} %copy-done.8, f32[1,768]{1,0:T(1,128)S(1)} %copy-done.2, ...), custom_call_target="tpu_custom_call" | custom-call | flops 2717908992 | bytes 5898240 | tf_op jit(solution)/shard_map/embed_next/pallas_call | solution.py:205
  76.4 2.3 %collective-permute-start.10 = (bf16[4,48,768]{2,1,0:T(8,128)(2,1)S(1)}, bf16[4,48,768]{2,1,0:T(8,128)(2,1)S(1)}, u32[]{:S(2)}, u32[]{:S(2)}) collective-permute-start(bf16[4,48,768]{2,1,0:T(8,128)(2,1)S(1)} %get-tuple-element.48.own1_ref), channel_id=1, source_target_pairs={{0,1},{1,2},{2,3},{3,4},{4,5},{5,6},{6,7},{7,8},{8,9},{9,10},{10,1... | collective-permute-start | bytes 884744 | tf_op jit(solution)/shard_map/ppermute | solution.py:484
  78.7 6.5 %collective-permute-start.9 = (bf16[4,48,768]{2,1,0:T(8,128)(2,1)S(1)}, bf16[4,48,768]{2,1,0:T(8,128)(2,1)S(1)}, u32[]{:S(2)}, u32[]{:S(2)}) collective-permute-start(bf16[4,48,768]{2,1,0:T(8,128)(2,1)S(1)} %get-tuple-element.48.own1_ref), channel_id=1, source_target_pairs={{1,0},{2,1},{3,2},{4,3},{5,4},{6,5},{7,6},{8,7},{9,8},{10,9},{11,1... | collective-permute-start | bytes 884744 | tf_op jit(solution)/shard_map/ppermute | solution.py:483
  85.3 8.8 %collective-permute-done.11.low_ref = bf16[4,48,768]{2,1,0:T(8,128)(2,1)S(1)} collective-permute-done((bf16[4,48,768]{2,1,0:T(8,128)(2,1)}, bf16[4,48,768]{2,1,0:T(8,128)(2,1)S(1)}, u32[]{:S(2)}, u32[]{:S(2)}) %collective-permute-start.11) | collective-permute-done | bytes 294944 | tf_op jit(solution)/shard_map/ppermute | solution.py:480
  94.3 3.9 %collective-permute-start.14 = (bf16[16,8,768]{2,1,0:T(8,128)(2,1)S(1)}, bf16[16,8,768]{2,1,0:T(8,128)(2,1)S(1)}, u32[]{:S(2)}, u32[]{:S(2)}) collective-permute-start(bf16[16,8,768]{2,1,0:T(8,128)(2,1)S(1)} %pad_maximum_fusion.1), channel_id=1, source_target_pairs={{16,0},{32,16},{48,32},{64,48},{80,64},{96,80},{112,96},{128,112},... | collective-permute-start | bytes 589832 | tf_op jit(solution)/shard_map/ppermute | solution.py:488
  98.3 2.5 %project.1 = (bf16[3,128,768]{2,1,0:T(8,128)(2,1)S(1)}, bf16[24,64,1536]{2,1,0:T(8,128)(2,1)S(1)}) custom-call(bf16[4,48,768]{2,1,0:T(8,128)(2,1)S(1)} %copy-done, bf16[4,48,768]{2,1,0:T(8,128)(2,1)S(1)} %get-tuple-element.48.own1_ref, bf16[4,48,768]{2,1,0:T(8,128)(2,1)S(1)} %collective-permute-done.11.low_ref, ...), custom_call_target="tpu_custom_call" | custom-call | flops 2264924160 | bytes 7077888 | tf_op jit(solution)/shard_map/project/pallas_call | solution.py:252
  100.9 4.1 %collective-permute-start.16 = (bf16[8,8,768]{2,1,0:T(8,128)(2,1)S(1)}, bf16[8,8,768]{2,1,0:T(8,128)(2,1)S(1)}, u32[]{:S(2)}, u32[]{:S(2)}) collective-permute-start(bf16[8,8,768]{2,1,0:T(8,128)(2,1)S(1)} %pad_maximum_fusion.3), channel_id=1, source_target_pairs={{16,0},{32,16},{48,32},{64,48},{80,64},{96,80},{112,96},{128,112},... | collective-permute-start | bytes 294920 | tf_op jit(solution)/shard_map/ppermute | solution.py:488
  105.1 4.3 %middle.1 = (bf16[24,64,1536]{2,1,0:T(8,128)(2,1)S(1)}, bf16[8,16,768]{2,1,0:T(8,128)(2,1)S(1)}) custom-call(s32[128]{0:T(128)S(1)} %copy-done.9, s32[1]{0:T(128)} %bitcast.first_ref, bf16[3,128,768]{2,1,0:T(8,128)(2,1)S(1)} %get-tuple-element.52.q_ref, bf16[24,64,1536]{2,1,0:T(8,128)(2,1)S(1)} %get-tuple-element.53._, ...), custom_call_target="tpu_custom_call", output_to_operand_aliasing={{0}: (3, {})} | custom-call | flops 8000000000 | bytes 10000000 | tf_op jit(solution)/shard_map/middle/pallas_call | solution.py:337
  109.4 6.5 %sides.1 = (bf16[8,48,768]{2,1,0:T(8,128)(2,1)}, bf16[24,64,1536]{2,1,0:T(8,128)(2,1)S(1)}) custom-call(s32[128]{0:T(128)S(1)} %copy-done.9, s32[1]{0:T(128)} %bitcast.first_ref, bf16[3,128,768]{2,1,0:T(8,128)(2,1)S(1)} %get-tuple-element.52.q_ref, bf16[24,64,1536]{2,1,0:T(8,128)(2,1)S(1)} %get-tuple-element.58._, ...), custom_call_target="tpu_custom_call", output_to_operand_aliasing={{1}: (3, {})} | custom-call | flops 8999999488 | bytes 10000000 | tf_op jit(solution)/shard_map/sides/pallas_call | solution.py:373
  (75 shorter events, 4.0 us)
Async XLA Ops:
  1.8 17.5 %all-to-all-start = ((bf16[16,48,384]{2,1,0:T(8,128)(2,1)}), bf16[16,48,384]{2,1,0:T(8,128)(2,1)S(1)}, u32[]{:S(2)}, u32[]{:S(2)}) async-start(bf16[16,48,384]{2,1,0:T(8,128)(2,1)} %spread.1), calls=%async_computation | async-start | bytes 1179648 | tf_op jit(solution)/shard_map/all_to_all | solution.py:413
  10.4 3.3 %copy-start.14 = (s32[128]{0:T(128)S(1)}, s32[128]{0:T(128)}, u32[]{:S(2)}) copy-start(s32[128]{0:T(128)} %param.10) | copy-start | bytes 1540
  19.4 15.9 %copy-start.12 = (bf16[16,48,384]{2,1,0:T(8,128)(2,1)}, bf16[16,48,384]{2,1,0:T(8,128)(2,1)S(1)}, u32[]{:S(2)}) copy-start(bf16[16,48,384]{2,1,0:T(8,128)(2,1)S(1)} %all-to-all-done.refs_0_) | copy-start | bytes 1769476
  19.4 14.6 %collective-permute-start.3 = (bf16[16,48,384]{2,1,0:T(8,128)(2,1)S(1)}, bf16[16,48,384]{2,1,0:T(8,128)(2,1)S(1)}, u32[]{:S(2)}, u32[]{:S(2)}) collective-permute-start(bf16[16,48,384]{2,1,0:T(8,128)(2,1)S(1)} %all-to-all-done.refs_0_), channel_id=1, source_target_pairs={{0,12},{4,0},{8,4},{12,8},{1,13},{5,1},{9,5},{13,9},{2,14},{6,2},{... | collective-permute-start | bytes 1769480 | tf_op jit(solution)/shard_map/ppermute | solution.py:439
  19.9 15.3 %collective-permute-start.1 = (bf16[16,48,384]{2,1,0:T(8,128)(2,1)S(1)}, bf16[16,48,384]{2,1,0:T(8,128)(2,1)S(1)}, u32[]{:S(2)}, u32[]{:S(2)}) collective-permute-start(bf16[16,48,384]{2,1,0:T(8,128)(2,1)S(1)} %all-to-all-done.refs_0_), channel_id=1, source_target_pairs={{0,4},{4,8},{8,12},{12,0},{1,5},{5,9},{9,13},{13,1},{2,6},{6,10},{... | collective-permute-start | bytes 1769480 | tf_op jit(solution)/shard_map/ppermute | solution.py:439
  21.4 21.7 %all-to-all-start.2 = ((bf16[16,288,128]{2,1,0:T(8,128)(2,1)}), bf16[16,288,128]{2,1,0:T(8,128)(2,1)S(1)}, u32[]{:S(2)}, u32[]{:S(2)}) async-start(bf16[16,288,128]{2,1,0:T(8,128)(2,1)} %pack.2), calls=%async_computation.2 | async-start | bytes 2359296 | tf_op jit(solution)/shard_map/all_to_all | solution.py:472
  25.1 13.9 %collective-permute-start = (bf16[16,48,384]{2,1,0:T(8,128)(2,1)S(1)}, bf16[16,48,384]{2,1,0:T(8,128)(2,1)S(1)}, u32[]{:S(2)}, u32[]{:S(2)}) collective-permute-start(bf16[16,48,384]{2,1,0:T(8,128)(2,1)S(1)} %all-to-all-done.refs_0_), channel_id=1, source_target_pairs={{0,16},{16,0},{32,48},{48,32},{64,80},{80,64},{96,112},{112,96},{1... | collective-permute-start | bytes 1769480 | tf_op jit(solution)/shard_map/ppermute | solution.py:444
  34.0 5.1 %collective-permute-start.4 = (bf16[16,48,384]{2,1,0:T(8,128)(2,1)S(1)}, bf16[16,48,384]{2,1,0:T(8,128)(2,1)S(1)}, u32[]{:S(2)}, u32[]{:S(2)}) collective-permute-start(bf16[16,48,384]{2,1,0:T(8,128)(2,1)S(1)} %collective-permute-done.3.down_ref.refs_2_), channel_id=1, source_target_pairs={{0,16},{16,0},{32,48},{48,32},{64,80},{80,64},{96,112},{112,96},{1... | collective-permute-start | bytes 1769480 | tf_op jit(solution)/shard_map/ppermute | solution.py:444
  35.2 5.5 %collective-permute-start.2 = (bf16[16,48,384]{2,1,0:T(8,128)(2,1)S(1)}, bf16[16,48,384]{2,1,0:T(8,128)(2,1)}, u32[]{:S(2)}, u32[]{:S(2)}) collective-permute-start(bf16[16,48,384]{2,1,0:T(8,128)(2,1)S(1)} %collective-permute-done.1.up_ref.refs_1_), channel_id=1, source_target_pairs={{0,16},{16,0},{32,48},{48,32},{64,80},{80,64},{96,112},{112,96},{1... | collective-permute-start | bytes 1769480 | tf_op jit(solution)/shard_map/ppermute | solution.py:444
  36.1 10.8 %collective-permute-start.5 = (bf16[8,48,384]{2,1,0:T(8,128)(2,1)S(1)}, bf16[8,48,384]{2,1,0:T(8,128)(2,1)}, u32[]{:S(2)}, u32[]{:S(2)}) collective-permute-start(bf16[8,48,384]{2,1,0:T(8,128)(2,1)S(1)} %get-tuple-element.40), channel_id=1, source_target_pairs={{0,4},{4,8},{8,12},{12,0},{1,5},{5,9},{9,13},{13,1},{2,6},{6,10},{... | collective-permute-start | bytes 884744 | tf_op jit(solution)/shard_map/ppermute | solution.py:441
  36.6 10.7 %collective-permute-start.6 = (bf16[8,48,384]{2,1,0:T(8,128)(2,1)S(1)}, bf16[8,48,384]{2,1,0:T(8,128)(2,1)}, u32[]{:S(2)}, u32[]{:S(2)}) collective-permute-start(bf16[8,48,384]{2,1,0:T(8,128)(2,1)S(1)} %get-tuple-element.41), channel_id=1, source_target_pairs={{0,12},{4,0},{8,4},{12,8},{1,13},{5,1},{9,5},{13,9},{2,14},{6,2},{... | collective-permute-start | bytes 884744 | tf_op jit(solution)/shard_map/ppermute | solution.py:441
  43.1 6.0 %copy-start.11 = (bf16[16,288,128]{2,1,0:T(8,128)(2,1)}, bf16[16,288,128]{2,1,0:T(8,128)(2,1)S(1)}, u32[]{:S(2)}) copy-start(bf16[16,288,128]{2,1,0:T(8,128)(2,1)S(1)} %all-to-all-done.2.x_ref) | copy-start | bytes 3538948
  43.1 26.2 %all-to-all-start.1 = ((bf16[16,288,128]{2,1,0:T(8,128)(2,1)}), bf16[16,288,128]{2,1,0:T(8,128)(2,1)S(1)}, u32[]{:S(2)}, u32[]{:S(2)}) async-start(bf16[16,288,128]{2,1,0:T(8,128)(2,1)} %pack.3), calls=%async_computation.1 | async-start | bytes 2359296 | tf_op jit(solution)/shard_map/all_to_all | solution.py:472
  46.9 1.9 %collective-permute-start.7 = (bf16[8,48,384]{2,1,0:T(8,128)(2,1)}, bf16[8,48,384]{2,1,0:T(8,128)(2,1)S(1)}, u32[]{:S(2)}, u32[]{:S(2)}) collective-permute-start(bf16[8,48,384]{2,1,0:T(8,128)(2,1)} %collective-permute-done.5.refs_3_), channel_id=1, source_target_pairs={{0,16},{16,0},{32,48},{48,32},{64,80},{80,64},{96,112},{112,96},{1... | collective-permute-start | bytes 884744 | tf_op jit(solution)/shard_map/ppermute | solution.py:444
  47.2 1.9 %collective-permute-start.8 = (bf16[8,48,384]{2,1,0:T(8,128)(2,1)}, bf16[8,48,384]{2,1,0:T(8,128)(2,1)S(1)}, u32[]{:S(2)}, u32[]{:S(2)}) collective-permute-start(bf16[8,48,384]{2,1,0:T(8,128)(2,1)} %collective-permute-done.6.refs_4_), channel_id=1, source_target_pairs={{0,16},{16,0},{32,48},{48,32},{64,80},{80,64},{96,112},{112,96},{1... | collective-permute-start | bytes 884744 | tf_op jit(solution)/shard_map/ppermute | solution.py:444
  47.5 21.9 %copy-start.1 = (bf16[3,3072]{1,0:T(4,128)(2,1)S(1)}, bf16[3,3072]{1,0:T(4,128)(2,1)}, u32[]{:S(2)}) copy-start(bf16[3,3072]{1,0:T(4,128)(2,1)} %fusion.pick_ref) | copy-start | bytes 55300
  47.5 21.9 %copy-start.2 = (f32[1,768]{1,0:T(1,128)S(1)}, f32[1,768]{1,0:T(1,128)}, u32[]{:S(2)}) copy-start(f32[1,768]{1,0:T(1,128)} %broadcast_in_dim.14.norm_ref) | copy-start | bytes 9220
  47.5 21.9 %copy-start.7 = (f32[3,768]{1,0:T(4,128)S(1)}, f32[3,768]{1,0:T(4,128)}, u32[]{:S(2)}) copy-start(f32[3,768]{1,0:T(4,128)} %bias_ref.3) | copy-start | bytes 27652
  47.5 21.9 %copy-start.8 = (f32[3,768]{1,0:T(4,128)S(1)}, f32[3,768]{1,0:T(4,128)}, u32[]{:S(2)}) copy-start(f32[3,768]{1,0:T(4,128)} %gain_ref.3) | copy-start | bytes 27652
  57.5 27.8 %collective-permute-start.12 = (bf16[4,48,768]{2,1,0:T(8,128)(2,1)}, bf16[4,48,768]{2,1,0:T(8,128)(2,1)S(1)}, u32[]{:S(2)}, u32[]{:S(2)}) collective-permute-start(bf16[4,48,768]{2,1,0:T(8,128)(2,1)} %get-tuple-element.47.own0_ref), channel_id=1, source_target_pairs={{1,0},{2,1},{3,2},{4,3},{5,4},{6,5},{7,6},{8,7},{9,8},{10,9},{11,1... | collective-permute-start | bytes 884744 | tf_op jit(solution)/shard_map/ppermute | solution.py:481
  66.4 27.7 %collective-permute-start.11 = (bf16[4,48,768]{2,1,0:T(8,128)(2,1)}, bf16[4,48,768]{2,1,0:T(8,128)(2,1)S(1)}, u32[]{:S(2)}, u32[]{:S(2)}) collective-permute-start(bf16[4,48,768]{2,1,0:T(8,128)(2,1)} %get-tuple-element.47.own0_ref), channel_id=1, source_target_pairs={{0,1},{1,2},{2,3},{3,4},{4,5},{5,6},{6,7},{7,8},{8,9},{9,10},{10,1... | collective-permute-start | bytes 884744 | tf_op jit(solution)/shard_map/ppermute | solution.py:480
  69.4 28.9 %copy-start = (bf16[4,48,768]{2,1,0:T(8,128)(2,1)S(1)}, bf16[4,48,768]{2,1,0:T(8,128)(2,1)}, u32[]{:S(2)}) copy-start(bf16[4,48,768]{2,1,0:T(8,128)(2,1)} %get-tuple-element.47.own0_ref) | copy-start | bytes 884740
  69.4 28.9 %copy-start.3 = (bf16[768,2304]{1,0:T(8,128)(2,1)S(1)}, bf16[768,2304]{1,0:T(8,128)(2,1)}, u32[]{:S(2)}) copy-start(bf16[768,2304]{1,0:T(8,128)(2,1)} %w_ref.7) | copy-start | bytes 10616836
  76.4 24.4 %collective-permute-start.10 = (bf16[4,48,768]{2,1,0:T(8,128)(2,1)S(1)}, bf16[4,48,768]{2,1,0:T(8,128)(2,1)S(1)}, u32[]{:S(2)}, u32[]{:S(2)}) collective-permute-start(bf16[4,48,768]{2,1,0:T(8,128)(2,1)S(1)} %get-tuple-element.48.own1_ref), channel_id=1, source_target_pairs={{0,1},{1,2},{2,3},{3,4},{4,5},{5,6},{6,7},{7,8},{8,9},{9,10},{10,1... | collective-permute-start | bytes 884744 | tf_op jit(solution)/shard_map/ppermute | solution.py:484
  78.7 22.1 %collective-permute-start.9 = (bf16[4,48,768]{2,1,0:T(8,128)(2,1)S(1)}, bf16[4,48,768]{2,1,0:T(8,128)(2,1)S(1)}, u32[]{:S(2)}, u32[]{:S(2)}) collective-permute-start(bf16[4,48,768]{2,1,0:T(8,128)(2,1)S(1)} %get-tuple-element.48.own1_ref), channel_id=1, source_target_pairs={{1,0},{2,1},{3,2},{4,3},{5,4},{6,5},{7,6},{8,7},{9,8},{10,9},{11,1... | collective-permute-start | bytes 884744 | tf_op jit(solution)/shard_map/ppermute | solution.py:483
  94.2 10.9 %collective-permute-start.13 = (bf16[16,8,768]{2,1,0:T(8,128)(2,1)S(1)}, bf16[16,8,768]{2,1,0:T(8,128)(2,1)S(1)}, u32[]{:S(2)}, u32[]{:S(2)}) collective-permute-start(bf16[16,8,768]{2,1,0:T(8,128)(2,1)S(1)} %pad_maximum_fusion), channel_id=1, source_target_pairs={{0,16},{16,32},{32,48},{48,64},{64,80},{80,96},{96,112},{112,128},... | collective-permute-start | bytes 589832 | tf_op jit(solution)/shard_map/ppermute | solution.py:487
  94.3 10.8 %copy-start.4 = (bf16[768,768]{1,0:T(8,128)(2,1)S(1)}, bf16[768,768]{1,0:T(8,128)(2,1)}, u32[]{:S(2)}) copy-start(bf16[768,768]{1,0:T(8,128)(2,1)} %wout_ref.3) | copy-start | bytes 3538948
  94.3 10.8 %copy-start.9 = (s32[128]{0:T(128)S(1)}, s32[128]{0:T(128)}, u32[]{:S(2)}) copy-start(s32[128]{0:T(128)} %start_ref.3) | copy-start | bytes 1540
  94.3 10.8 %copy-start.10 = (bf16[4,48,768]{2,1,0:T(8,128)(2,1)S(1)}, bf16[4,48,768]{2,1,0:T(8,128)(2,1)}, u32[]{:S(2)}) copy-start(bf16[4,48,768]{2,1,0:T(8,128)(2,1)} %get-tuple-element.56.emb0_ref) | copy-start | bytes 884740
  94.3 10.7 %collective-permute-start.14 = (bf16[16,8,768]{2,1,0:T(8,128)(2,1)S(1)}, bf16[16,8,768]{2,1,0:T(8,128)(2,1)S(1)}, u32[]{:S(2)}, u32[]{:S(2)}) collective-permute-start(bf16[16,8,768]{2,1,0:T(8,128)(2,1)S(1)} %pad_maximum_fusion.1), channel_id=1, source_target_pairs={{16,0},{32,16},{48,32},{64,48},{80,64},{96,80},{112,96},{128,112},... | collective-permute-start | bytes 589832 | tf_op jit(solution)/shard_map/ppermute | solution.py:488
  100.8 8.6 %collective-permute-start.15 = (bf16[8,8,768]{2,1,0:T(8,128)(2,1)S(1)}, bf16[8,8,768]{2,1,0:T(8,128)(2,1)S(1)}, u32[]{:S(2)}, u32[]{:S(2)}) collective-permute-start(bf16[8,8,768]{2,1,0:T(8,128)(2,1)S(1)} %pad_maximum_fusion.2), channel_id=1, source_target_pairs={{0,16},{16,32},{32,48},{48,64},{64,80},{80,96},{96,112},{112,128},... | collective-permute-start | bytes 294920 | tf_op jit(solution)/shard_map/ppermute | solution.py:487
  100.9 8.5 %collective-permute-start.16 = (bf16[8,8,768]{2,1,0:T(8,128)(2,1)S(1)}, bf16[8,8,768]{2,1,0:T(8,128)(2,1)S(1)}, u32[]{:S(2)}, u32[]{:S(2)}) collective-permute-start(bf16[8,8,768]{2,1,0:T(8,128)(2,1)S(1)} %pad_maximum_fusion.3), channel_id=1, source_target_pairs={{16,0},{32,16},{48,32},{64,48},{80,64},{96,80},{112,96},{128,112},... | collective-permute-start | bytes 294920 | tf_op jit(solution)/shard_map/ppermute | solution.py:488
  (7 other events, 8.0 us)
